TPU v7x, 32 devices: a whole 2x2x4 slice. The times are simulated.
32 devices in a mesh: pour: 2 (over x), brick: 16 (over z, y, core).
Axes of the slice: x: 2, y: 2, z: 4, core: 2. Of those that a mesh axis runs over, the one named last changes fastest.
Arguments:
- initial_voxel_degrees: float32 [256, 256, 256], P(('pour', 'brick')), parts along dimension 0, may hold values from -2 to 4
- alloy_tag_per_voxel: int32 [128, 256, 256], P('brick'), may hold values from 0 to 7
- thermal_conductance_per_alloy: float32 [8], replicated, may hold values from 0.2 to 1
- specific_storage_per_alloy: float32 [8], replicated, may hold values from 1 to 4
- bore_boundary_positions: int32 [16, 32, 256], P('brick'), may hold values from 0 to 524287
- surface_transfer_coefficient: float32 [16, 32], P('brick'), may hold values from 0 to 18
- surface_over_flow_ratio: float32 [32], replicated, may hold values from 0 to 1
- flow_direction_flag: int32 [32], replicated, may hold values from 0 to 1
- entry_coolant_degrees: float32 [64], P('pour'), parts along dimension 0, may hold values from -1 to 0
Outputs:
- die_temperature: float32 [256, 256, 256], P(('pour', 'brick')), parts along dimension 0
- coolant_mid: float32 [32, 32], P(('pour', 'brick')), parts along dimension 0
There are 2 independent parts, one for each index of `pour`. A program takes and returns all parts, laid end to end along the dimension named above; an argument that names none is the same for every part. Nothing has to cross between parts.
Inputs may be any that keep to these rules, and one draw needn't show every extreme that they name: `bore_boundary_positions`: indices refer to cells of the segment's own brick.
All inputs are finite; a program needn't handle non-finite values.
Results may differ from a plain program's by a relative error of at most 0.00006.
Values sent between devices are 32-bit elements; how exact they have to be, the bound alone decides.
No kernel may reach another device: no remote copies, remote signals or barrier semaphores. Data moves between devices by JAX's collectives and lax.ppermute only.
A program may use at most 64 MiB of HBM per device.

v0:
```python
import jax
import jax.numpy as jnp
from jax import lax
from jax.sharding import PartitionSpec as P

STEPS = 3


def with_halo(cells, sides, width):
    for axis, dim in sides:
        count = lax.axis_size(axis)
        ends = count - 1
        head = lax.slice_in_dim(cells, 0, width, axis=dim)
        tail = lax.slice_in_dim(cells, cells.shape[dim] - width, cells.shape[dim], axis=dim)
        cells = jnp.concatenate(
            [
                lax.ppermute(tail, axis, [(i, (i + 1) % count) for i in range(ends)]),
                cells,
                lax.ppermute(head, axis, [((i + 1) % count, i) for i in range(ends)]),
            ],
            axis=dim,
        )
    return cells


def carried_in(value, axis, join, neutral, backward):
    count, mine = (lax.axis_size(axis), lax.axis_index(axis))
    pieces = jax.tree.map(lambda part: lax.all_gather(part, axis), value)
    if backward:
        pieces = jax.tree.map(lambda part: part[::-1], pieces)
        mine = count - 1 - mine
    so_far = jax.tree.map(
        lambda part, zero: jnp.full_like(part, 0) + jnp.asarray(zero, part.dtype), value, neutral
    )

    def turn(position, so_far):
        longer = join(so_far, jax.tree.map(lambda part: part[position], pieces))
        return jax.tree.map(lambda new, old: jnp.where(position < mine, new, old), longer, so_far)

    return lax.fori_loop(0, count - 1, turn, so_far)


def lookup(alloy_tag_per_voxel, table):
    result = jnp.zeros(alloy_tag_per_voxel.shape, table.dtype)
    for material in range(table.shape[0]):
        result = jnp.where(alloy_tag_per_voxel == material, table[material], result)
    return result


def face_mean(left, right):
    return 2.0 * left * right / (left + right + 1e-30)


def advance(updated_thermal_state, conduct, coeffs):
    center = updated_thermal_state[1:-1]
    center_cond = conduct[1:-1]
    fluxes = face_mean(center_cond, conduct[2:]) * (updated_thermal_state[2:] - center)
    fluxes = fluxes + face_mean(center_cond, conduct[:-2]) * (updated_thermal_state[:-2] - center)
    widths = ((0, 0), (1, 1), (0, 0))
    cond_pad = jnp.pad(center_cond, widths)
    heat_pad = jnp.pad(center, widths)
    fluxes = fluxes + face_mean(center_cond, cond_pad[:, 2:]) * (heat_pad[:, 2:] - center)
    fluxes = fluxes + face_mean(center_cond, cond_pad[:, :-2]) * (heat_pad[:, :-2] - center)
    widths = ((0, 0), (0, 0), (1, 1))
    cond_pad = jnp.pad(center_cond, widths)
    heat_pad = jnp.pad(center, widths)
    fluxes = fluxes + face_mean(center_cond, cond_pad[:, :, 2:]) * (heat_pad[:, :, 2:] - center)
    fluxes = fluxes + face_mean(center_cond, cond_pad[:, :, :-2]) * (heat_pad[:, :, :-2] - center)
    return center + coeffs[1:-1] * fluxes


def compose(earlier, later):
    return (later[0] * earlier[0], later[0] * earlier[1] + later[1])


def per_device(
    initial_voxel_degrees,
    alloy_tag_per_voxel,
    thermal_conductance_per_alloy,
    specific_storage_per_alloy,
    bore_boundary_positions,
    surface_transfer_coefficient,
    surface_over_flow_ratio,
    flow_direction_flag,
    entry_coolant_degrees,
):
    depth = 1
    conduct = lookup(alloy_tag_per_voxel, thermal_conductance_per_alloy)
    coeffs = 0.16 / lookup(alloy_tag_per_voxel, specific_storage_per_alloy)
    properties = with_halo(jnp.stack([conduct, coeffs]), (("brick", 1),), depth)
    conduct_wide = properties[0]
    coeff_wide = properties[1]
    updated_thermal_state = initial_voxel_degrees
    for repeat in range(STEPS):
        padded = with_halo(updated_thermal_state, (("brick", 0),), 1)
        updated_thermal_state = advance(padded, conduct_wide, coeff_wide)
    flat = updated_thermal_state.reshape(-1)
    cells = bore_boundary_positions[0]
    wall_temps = flat[cells]
    wall_mean = jnp.mean(wall_temps, axis=1)
    keep = jnp.exp(-surface_over_flow_ratio * surface_transfer_coefficient[0])
    gain = (1.0 - keep) * wall_mean
    identity = (jnp.ones_like(keep), jnp.zeros_like(gain))
    downstream = carried_in((keep, gain), "brick", compose, identity, False)
    upstream = carried_in((keep, gain), "brick", compose, identity, True)
    forward = flow_direction_flag == 0
    carry_keep = jnp.where(forward, downstream[0], upstream[0])
    carry_gain = jnp.where(forward, downstream[1], upstream[1])
    inflow = carry_keep * entry_coolant_degrees + carry_gain
    coolant = 0.5 * (inflow + keep * inflow + gain)
    change = 0.5 * (1.0 - keep)[:, None] * (coolant[:, None] - wall_temps)
    final = flat.at[cells.reshape(-1)].add(change.reshape(-1)).reshape(updated_thermal_state.shape)
    return (final, coolant[None])


def solution(mesh):
    return jax.shard_map(
        per_device,
        mesh=mesh,
        in_specs=(
            P(("pour", "brick"), None, None),
            P("brick", None, None),
            P(),
            P(),
            P("brick", None, None),
            P("brick", None),
            P(),
            P(),
            P("pour"),
        ),
        out_specs=(P(("pour", "brick"), None, None), P(("pour", "brick"), None)),
        check_vma=False,
    )
```

profile of v0, /device:TPU:0, one launch (start us, length us, event | category | flops | bytes accessed | tf_op | source)
XLA Modules:
  0.0 222.3 jit_solution(8987759714099487587)
XLA Ops:
  0.6 1.6 fusion.59
  2.3 1.6 fusion.58
  3.9 9.3 %select_select_fusion = (f32[8,256,256]{2,1,0:T(8,128)S(1)}, pred[8,256,256]{2,1,0:T(8,128)(4,1)S(1)}, pred[8,256,256]{2,1,0:T(8,128)(4,1)S(1)}, pred[8,256,256]...) fusion(f32[]{:T(128)} %bitcast.15, f32[]{:T(128)} %bitcast.14, ...), kind=kLoop, calls=%fused_computation.87 | loop fusion | flops 8388608 | bytes 8388640 | tf_op jit(solution)/shard_map/jit(_where)/select_n | solution.py:46
  13.2 6.7 %select_divide_fusion = f32[8,256,256]{2,1,0:T(8,128)S(1)} fusion(pred[8,256,256]{2,1,0:T(8,128)(4,1)S(1)} %get-tuple-element.307, pred[8,256,256]{2,1,0:T(8,128)(4,1)S(1)} %get-tuple-element.306, pred[8,256,256]{2,1,0:T(8,128)(4,1)S(1)} %get-tuple-element.305, pred[8,256,256]{2,1,0:T(8,128)(4,1)S(1)} %get-tuple-element.304, ...), kind=kLoop, calls=%fused_computation.88 | loop fusion | flops 4718592 | bytes 6291488 | tf_op jit(solution)/shard_map/div | solution.py:89
  20.0 0.0 copy-start
  20.0 0.0 copy-start.5
  20.0 0.1 pad_maximum_fusion.10
  20.1 1.3 collective-permute-start
  21.4 3.1 %collective-permute-start.2 = (f32[2,1,256,256]{3,2,1,0:T(8,128)S(1)}, f32[2,1,256,256]{3,2,1,0:T(8,128)S(1)}, u32[]{:S(2)}, u32[]{:S(2)}) collective-permute-start(f32[2,1,256,256]{3,2,1,0:T(8,128)S(1)} %get-tuple-element.312), channel_id=1, source_target_pairs={{0,1},{1,2},{2,3},{3,4},{4,5},{5,6},{6,7},{7,8},{8,9},{9,10},{10,1... | collective-permute-start | bytes 1572872 | tf_op jit(solution)/shard_map/ppermute | solution.py:17
  24.4 1.1 fusion.57
  25.5 1.3 collective-permute-start.1
  26.8 5.1 %collective-permute-start.3 = (f32[1,256,256]{2,1,0:T(8,128)S(1)}, f32[1,256,256]{2,1,0:T(8,128)S(1)}, u32[]{:S(2)}, u32[]{:S(2)}) collective-permute-start(f32[1,256,256]{2,1,0:T(8,128)S(1)} %get-tuple-element.319), channel_id=1, source_target_pairs={{0,1},{1,2},{2,3},{3,4},{4,5},{5,6},{6,7},{7,8},{8,9},{9,10},{10,1... | collective-permute-start | bytes 786440 | tf_op jit(solution)/shard_map/ppermute | solution.py:17
  31.9 0.0 copy-done.5
  32.0 0.0 collective-permute-done.1
  32.0 1.1 collective-permute-done.3
  33.1 0.0 copy-start.4
  33.1 0.0 collective-permute-done
  33.1 0.7 copy-done.4
  33.8 0.0 collective-permute-done.2
  33.8 10.7 %fusion.5 = (f32[8,256,256]{2,1,0:T(8,128)}, f32[8,256,256]{2,1,0:T(8,128)S(1)}, f32[8,256,256]{2,1,0:T(8,128)S(1)}) fusion(f32[8,256,256]{2,1,0:T(8,128)} %param.13, f32[8,256,256]{2,1,0:T(8,128)S(1)} %select_divide_fusion, f32[1,256,256]{2,1,0:T(8,128)} %copy-done.4, f32[1,256,256]{2,1,0:T(8,128)S(1)} %collective-permute-done.1, ...), kind=kLoop, calls=%fused_computation.29 | loop fusion | flops 26214400 | bytes 18350080 | tf_op jit(solution)/shard_map/add | solution.py:69
  44.5 0.0 copy-start.1
  44.5 0.0 copy-start.2
  44.5 1.4 fusion.56
  45.9 1.3 collective-permute-start.4
  47.2 12.8 %collective-permute-start.5 = (f32[1,256,256]{2,1,0:T(8,128)S(1)}, f32[1,256,256]{2,1,0:T(8,128)S(1)}, u32[]{:S(2)}, u32[]{:S(2)}) collective-permute-start(f32[1,256,256]{2,1,0:T(8,128)S(1)} %get-tuple-element.317), channel_id=1, source_target_pairs={{0,1},{1,2},{2,3},{3,4},{4,5},{5,6},{6,7},{7,8},{8,9},{9,10},{10,1... | collective-permute-start | bytes 786440 | tf_op jit(solution)/shard_map/ppermute | solution.py:17
  60.1 0.0 collective-permute-done.4
  60.1 1.1 collective-permute-done.5
  61.2 0.0 copy-done
  61.2 0.0 copy-start.9
  61.2 0.0 copy-start.10
  61.2 0.0 copy-start.11
  61.2 9.0 %fusion.13 = f32[8,256,256]{2,1,0:T(8,128)S(1)} fusion(f32[8,256,256]{2,1,0:T(8,128)} %get-tuple-element.296, f32[8,256,256]{2,1,0:T(8,128)S(1)} %select_divide_fusion, f32[8,256,256]{2,1,0:T(8,128)S(1)} %get-tuple-element.298, f32[1,256,256]{2,1,0:T(8,128)S(1)} %collective-permute-done.5, f32[8,256,256]{2,1,0:T(8,128)S(1)} %get-tuple-element.297, ...), kind=kLoop, calls=%fused_computation.37 | loop fusion | flops 19922944 | bytes 13107200 | tf_op jit(solution)/shard_map/add | solution.py:69
  70.2 0.0 copy-done.1
  70.2 0.0 copy-done.2
  70.2 0.0 copy-start.3
  70.3 1.3 copy-done.3
  71.5 1.3 collective-permute-start.6
  72.8 7.4 %collective-permute-start.7 = (f32[1,256,256]{2,1,0:T(8,128)S(1)}, f32[1,256,256]{2,1,0:T(8,128)S(1)}, u32[]{:S(2)}, u32[]{:S(2)}) collective-permute-start(f32[1,256,256]{2,1,0:T(8,128)S(1)} %get-tuple-element.315), channel_id=1, source_target_pairs={{0,1},{1,2},{2,3},{3,4},{4,5},{5,6},{6,7},{7,8},{8,9},{9,10},{10,1... | collective-permute-start | bytes 786440 | tf_op jit(solution)/shard_map/ppermute | solution.py:17
  80.2 0.0 copy-done.9
  80.2 0.0 copy-done.10
  80.3 0.0 copy-done.11
  80.3 0.6 dynamic-slice
  81.7 0.2 dynamic-update-slice
  81.9 0.0 collective-permute-done.6
  81.9 0.0 collective-permute-done.7
  81.9 10.4 %fusion.21 = f32[8,256,256]{2,1,0:T(8,128)S(1)} fusion(f32[8,256,256]{2,1,0:T(8,128)} %copy-done.3, f32[8,256,256]{2,1,0:T(8,128)} %copy-done, f32[8,256,256]{2,1,0:T(8,128)} %copy-done.2, f32[1,256,256]{2,1,0:T(8,128)S(1)} %collective-permute-done.7, f32[8,256,256]{2,1,0:T(8,128)} %copy-done.1, f32[1,256,256]{2,1,0:T(8,128)S(1)} %collective-permute-done.6, ...), kind=kLoop, calls=%fused_computation.45 | loop fusion | flops 19922944 | bytes 13107200 | tf_op jit(solution)/shard_map/add | solution.py:69
  92.3 1.1 copy.11
  93.4 0.0 copy-start.7
  93.4 0.0 copy-start.8
  93.4 45.5 %gather_fusion = f32[8192]{0:T(1024)S(1)} fusion(f32[524288]{0:T(1024)S(1)} %bitcast.76, s32[8192]{0:T(1024)S(1)} %broadcast_clamp_fusion), kind=kCustom, calls=%fused_computation | custom fusion | bytes 98304 | tf_op jit(solution)/shard_map/gather | solution.py:99
  139.0 0.1 reduce_sum.9
  139.1 0.1 fusion.53
  139.2 34.8 %all-reduce.10 = (f32[512]{0:T(512)S(1)}, f32[512]{0:T(512)S(1)}) all-reduce(f32[512]{0:T(512)S(1)} %dynamic-update-slice, f32[512]{0:T(512)S(1)} %fusion.53), channel_id=2, replica_groups=mesh['pour'=2,'brick'=16] {'brick'}, use_global_device_ids=true, to_apply=%add.8 | all-reduce | flops 1024 | bytes 8192
  174.0 0.1 reshape.99
  174.1 0.1 reshape.100
  174.2 0.6 while.33
  174.8 0.7 while.32
  175.5 0.0 copy-done.7
  175.5 0.0 copy-done.8
  175.5 0.0 copy-start.6
  175.5 0.1 multiply_bitcast_fusion
  175.6 45.0 %scatter_fusion = f32[524288]{0:T(1024)S(1)} fusion(f32[524288]{0:T(1024)S(1)} %bitcast.77, s32[8192]{0:T(1024)S(1)} %bitcast.83, f32[8192]{0:T(1024)S(1)} %bitcast.84), kind=kCustom, calls=%fused_computation.1 | custom fusion | flops 8192 | bytes 131072 | tf_op jit(solution)/shard_map/scatter-add | solution.py:112
  220.6 0.0 copy-done.6
  220.6 1.6 reshape.82
  (48 shorter events, 0.8 us)
Async XLA Ops:
  20.0 41.2 %copy-start = (f32[8,256,256]{2,1,0:T(8,128)}, f32[8,256,256]{2,1,0:T(8,128)S(1)}, u32[]{:S(2)}) copy-start(f32[8,256,256]{2,1,0:T(8,128)S(1)} %select_divide_fusion) | copy-start | bytes 6291460
  20.0 12.0 %copy-start.5 = (s32[1,32,256]{2,1,0:T(8,128)S(1)}, s32[1,32,256]{2,1,0:T(8,128)}, u32[]{:S(2)}) copy-start(s32[1,32,256]{2,1,0:T(8,128)} %param.17) | copy-start | bytes 98308
  20.1 13.0 %collective-permute-start = (f32[2,1,256,256]{3,2,1,0:T(8,128)S(1)}, f32[2,1,256,256]{3,2,1,0:T(8,128)S(1)}, u32[]{:S(2)}, u32[]{:S(2)}) collective-permute-start(f32[2,1,256,256]{3,2,1,0:T(8,128)S(1)} %get-tuple-element.313), channel_id=1, source_target_pairs={{1,0},{2,1},{3,2},{4,3},{5,4},{6,5},{7,6},{8,7},{9,8},{10,9},{11,1... | collective-permute-start | bytes 1572872 | tf_op jit(solution)/shard_map/ppermute | solution.py:19
  21.4 12.4 %collective-permute-start.2 = (f32[2,1,256,256]{3,2,1,0:T(8,128)S(1)}, f32[2,1,256,256]{3,2,1,0:T(8,128)S(1)}, u32[]{:S(2)}, u32[]{:S(2)}) collective-permute-start(f32[2,1,256,256]{3,2,1,0:T(8,128)S(1)} %get-tuple-element.312), channel_id=1, source_target_pairs={{0,1},{1,2},{2,3},{3,4},{4,5},{5,6},{6,7},{7,8},{8,9},{9,10},{10,1... | collective-permute-start | bytes 1572872 | tf_op jit(solution)/shard_map/ppermute | solution.py:17
  25.5 6.5 %collective-permute-start.1 = (f32[1,256,256]{2,1,0:T(8,128)S(1)}, f32[1,256,256]{2,1,0:T(8,128)S(1)}, u32[]{:S(2)}, u32[]{:S(2)}) collective-permute-start(f32[1,256,256]{2,1,0:T(8,128)S(1)} %get-tuple-element.318), channel_id=1, source_target_pairs={{1,0},{2,1},{3,2},{4,3},{5,4},{6,5},{7,6},{8,7},{9,8},{10,9},{11,1... | collective-permute-start | bytes 786440 | tf_op jit(solution)/shard_map/ppermute | solution.py:19
  26.8 6.2 %collective-permute-start.3 = (f32[1,256,256]{2,1,0:T(8,128)S(1)}, f32[1,256,256]{2,1,0:T(8,128)S(1)}, u32[]{:S(2)}, u32[]{:S(2)}) collective-permute-start(f32[1,256,256]{2,1,0:T(8,128)S(1)} %get-tuple-element.319), channel_id=1, source_target_pairs={{0,1},{1,2},{2,3},{3,4},{4,5},{5,6},{6,7},{7,8},{8,9},{9,10},{10,1... | collective-permute-start | bytes 786440 | tf_op jit(solution)/shard_map/ppermute | solution.py:17
  33.1 0.7 copy-start.4
  44.5 25.8 %copy-start.1 = (f32[8,256,256]{2,1,0:T(8,128)}, f32[8,256,256]{2,1,0:T(8,128)S(1)}, u32[]{:S(2)}) copy-start(f32[8,256,256]{2,1,0:T(8,128)S(1)} %get-tuple-element.297) | copy-start | bytes 6291460
  44.5 25.8 %copy-start.2 = (f32[8,256,256]{2,1,0:T(8,128)}, f32[8,256,256]{2,1,0:T(8,128)S(1)}, u32[]{:S(2)}) copy-start(f32[8,256,256]{2,1,0:T(8,128)S(1)} %get-tuple-element.298) | copy-start | bytes 6291460
  45.9 14.2 %collective-permute-start.4 = (f32[1,256,256]{2,1,0:T(8,128)S(1)}, f32[1,256,256]{2,1,0:T(8,128)S(1)}, u32[]{:S(2)}, u32[]{:S(2)}) collective-permute-start(f32[1,256,256]{2,1,0:T(8,128)S(1)} %get-tuple-element.316), channel_id=1, source_target_pairs={{1,0},{2,1},{3,2},{4,3},{5,4},{6,5},{7,6},{8,7},{9,8},{10,9},{11,1... | collective-permute-start | bytes 786440 | tf_op jit(solution)/shard_map/ppermute | solution.py:19
  47.2 14.0 %collective-permute-start.5 = (f32[1,256,256]{2,1,0:T(8,128)S(1)}, f32[1,256,256]{2,1,0:T(8,128)S(1)}, u32[]{:S(2)}, u32[]{:S(2)}) collective-permute-start(f32[1,256,256]{2,1,0:T(8,128)S(1)} %get-tuple-element.317), channel_id=1, source_target_pairs={{0,1},{1,2},{2,3},{3,4},{4,5},{5,6},{6,7},{7,8},{8,9},{9,10},{10,1... | collective-permute-start | bytes 786440 | tf_op jit(solution)/shard_map/ppermute | solution.py:17
  61.2 19.0 %copy-start.9 = (f32[1,32]{1,0:T(1,128)S(1)}, f32[1,32]{1,0:T(1,128)}, u32[]{:S(2)}) copy-start(f32[1,32]{1,0:T(1,128)} %param.18) | copy-start | bytes 388
  61.2 19.1 %copy-start.10 = (f32[32]{0:T(128)S(1)}, f32[32]{0:T(128)}, u32[]{:S(2)}) copy-start(f32[32]{0:T(128)} %param.19) | copy-start | bytes 388
  61.2 19.2 %copy-start.11 = (u32[32]{0:T(128)S(1)}, u32[32]{0:T(128)}, u32[]{:S(2)}) copy-start(u32[32]{0:T(128)} %constant.114) | copy-start | bytes 388
  70.2 1.3 copy-start.3
  71.5 10.4 %collective-permute-start.6 = (f32[1,256,256]{2,1,0:T(8,128)S(1)}, f32[1,256,256]{2,1,0:T(8,128)S(1)}, u32[]{:S(2)}, u32[]{:S(2)}) collective-permute-start(f32[1,256,256]{2,1,0:T(8,128)S(1)} %get-tuple-element.314), channel_id=1, source_target_pairs={{1,0},{2,1},{3,2},{4,3},{5,4},{6,5},{7,6},{8,7},{9,8},{10,9},{11,1... | collective-permute-start | bytes 786440 | tf_op jit(solution)/shard_map/ppermute | solution.py:19
  72.8 9.1 %collective-permute-start.7 = (f32[1,256,256]{2,1,0:T(8,128)S(1)}, f32[1,256,256]{2,1,0:T(8,128)S(1)}, u32[]{:S(2)}, u32[]{:S(2)}) collective-permute-start(f32[1,256,256]{2,1,0:T(8,128)S(1)} %get-tuple-element.315), channel_id=1, source_target_pairs={{0,1},{1,2},{2,3},{3,4},{4,5},{5,6},{6,7},{7,8},{8,9},{9,10},{10,1... | collective-permute-start | bytes 786440 | tf_op jit(solution)/shard_map/ppermute | solution.py:17
  93.4 82.1 %copy-start.7 = (f32[32]{0:T(128)S(1)}, f32[32]{0:T(128)}, u32[]{:S(2)}) copy-start(f32[32]{0:T(128)} %param.21) | copy-start | bytes 388
  93.4 82.1 %copy-start.8 = (s32[32]{0:T(128)S(1)}, s32[32]{0:T(128)}, u32[]{:S(2)}) copy-start(s32[32]{0:T(128)} %param.20) | copy-start | bytes 388
  175.5 45.1 %copy-start.6 = (f32[32]{0:T(128)}, f32[32]{0:T(128)S(1)}, u32[]{:S(2)}) copy-start(f32[32]{0:T(128)S(1)} %fusion.52) | copy-start | bytes 388
where the time goes:
time: 223 us; the launch traced here: 222 us
  other arithmetic  92.1 us (41%)
  local copies, waits for them, and re-layouts  57.2 us (26%)
  blocking collectives  34.8 us (16%)
  starting transfers between devices  33.5 us (15%)
    gather x2, local copies, waits for them, and re-layouts, per_device(): wall_temps = flat[cells]  45.5 us
    scatter-add x1, other arithmetic, per_device(): flat.at[cells.reshape(-1)].add(change.reshape(-1))  45 us
    unnamed x1, blocking collectives  34.8 us
    add x3, other arithmetic, advance(): return center + coeffs[1:-1] * fluxes  30.1 us
    ppermute x4, starting transfers between devices, with_halo(): lax.ppermute(tail, axis, [(i, (i + 1) % count) for i in range(ends)])  28.3 us
    select_n x1, other arithmetic, lookup(): result = jnp.where(alloy_tag_per_voxel == material, table[material], result)  9.32 us
    div x1, other arithmetic, per_device(): coeffs = 0.16 / lookup(alloy_tag_per_voxel, specific_storage_per_alloy)  6.73 us
    ppermute x4, starting transfers between devices, with_halo(): lax.ppermute(head, axis, [((i + 1) % count, i) for i in range(ends)])  5.16 us
  transfers between devices with their start and end apart: 8, of which 2 were waited for; matrix products, arithmetic and copies ran while one was open for 1% of the time, Pallas kernels for 0%

commit v1 on v0

v1 whole, which is shorter than its diff:
```python
import jax
import jax.numpy as jnp
from jax import lax
from jax.experimental import pallas as pl
from jax.experimental.pallas import tpu as pltpu
from jax.sharding import PartitionSpec as P

LANES = 128
PAD = 8
STRIP = 16
VMEM = pl.BlockSpec(memory_space=pltpu.VMEM)
SMEM = pl.BlockSpec(memory_space=pltpu.SMEM)
HBM = pl.BlockSpec(memory_space=pltpu.HBM)
HALVES = (0, 1)


def f32(*shape):
    return jax.ShapeDtypeStruct(shape, jnp.float32)


def i32(*shape):
    return jax.ShapeDtypeStruct(shape, jnp.int32)


def call(kernel, args, in_specs, out_shape, out_specs, scratch=(), cost=2_000_000, **kw):
    return pl.pallas_call(
        kernel,
        out_shape=out_shape,
        in_specs=in_specs,
        out_specs=out_specs,
        scratch_shapes=list(scratch),
        cost_estimate=pl.CostEstimate(flops=cost, bytes_accessed=cost, transcendentals=0),
        compiler_params=pltpu.CompilerParams(vmem_limit_bytes=12 << 20),
        **kw,
    )(*args)


def plane_of(j, planes):
    odd = lax.rem(lax.axis_index("brick"), 2)
    return jnp.where(odd == 1, j, planes - 1 - j)


def lanes_iota(rows):
    return lax.broadcasted_iota(jnp.int32, (rows, LANES), 1)


def pick(tag, table):
    level = [jnp.broadcast_to(v, tag.shape) for v in table]
    bit = 0
    while len(level) > 1:
        on = (tag & (1 << bit)) != 0
        if len(level) % 2:
            level.append(level[-1])
        level = [jnp.where(on, level[k + 1], level[k]) for k in range(0, len(level), 2)]
        bit += 1
    return level[0]


def face_mean(left, right):
    return 2.0 * left * right / (left + right + 1e-30)


def rows_loop(count, body, step=STRIP, unroll=4):
    def turn(s, carry):
        body(pl.multiple_of(s * step, step))
        return carry

    lax.fori_loop(0, count // step, turn, 0, unroll=unroll)


def advance_rows(cur, r, up, down, gx_up, gx_down, gy, ry, gz, coeff, rz):
    n = STRIP
    lane = lanes_iota(n)
    t = [cur[h, pl.ds(r, n), :] for h in HALVES]
    nxt = [pltpu.roll(t[h], LANES - 1, 1) for h in HALVES]
    ahead = [jnp.where(lane == LANES - 1, nxt[1], nxt[0]), nxt[1]]
    prv = [pltpu.roll(t[h], 1, 1) for h in HALVES]
    behind = [prv[0], jnp.where(lane == 0, prv[0], prv[1])]
    new = []
    for h in HALVES:
        c = t[h]
        flux = gx_up(h) * (up(h) - c) + gx_down(h) * (down(h) - c)
        flux = flux + gy[h, pl.ds(ry, n), :] * (cur[h, pl.ds(r + 1, n), :] - c)
        flux = flux + gy[h, pl.ds(ry - 1, n), :] * (cur[h, pl.ds(r - 1, n), :] - c)
        flux = flux + gz[h, pl.ds(rz, n), :] * (ahead[h] - c)
        flux = flux + gz[2 + h, pl.ds(rz, n), :] * (behind[h] - c)
        new.append(c + coeff[h, pl.ds(rz, n), :] * flux)
    return new


def main_planes(cur, last, halo, gxa, gxm, gy, gz, coeff, planes, ny, emit):
    def plane(j, first, final):
        def body(y):
            r = PAD + j * ny + y
            rz = j * ny + y

            def down(h):
                return halo[h, pl.ds(y, STRIP), :] if first else cur[h, pl.ds(r - ny, STRIP), :]

            def gx_down(h):
                return gxa[h, pl.ds(y, STRIP), :] if first else gxm[h, pl.ds(rz - ny, STRIP), :]

            def up(h):
                return last(h, y) if final else cur[h, pl.ds(r + ny, STRIP), :]

            def gx_up(h):
                return gxm[h, pl.ds(rz, STRIP), :]

            new = advance_rows(cur, r, up, down, gx_up, gx_down, gy, PAD + rz, gz, coeff, rz)
            emit(j, y, new, first)

        rows_loop(ny, body, unroll=8)

    plane(0, True, planes == 2)

    def inner(j, carry):
        plane(j, False, False)
        return carry

    lax.fori_loop(1, planes - 2, inner, 0)
    plane(planes - 2, False, True)


def send_kernel(t_ref, tag_ref, a_ref, b_ref, tags, sem):
    planes = t_ref.shape[0]
    copies = []
    for side, out in ((1, b_ref), (0, a_ref)):
        x = plane_of(0 if side == 0 else planes - 1, planes)
        for h in HALVES:
            part = pl.ds(h * LANES, LANES)
            copies.append(
                pltpu.make_async_copy(t_ref.at[x, :, part], out.at[0, h], sem.at[len(copies)])
            )
            copies.append(
                pltpu.make_async_copy(tag_ref.at[x, :, part], tags.at[side, h], sem.at[len(copies)])
            )
    for copy in copies:
        copy.start()
    for copy in copies:
        copy.wait()
    for side, out in ((1, b_ref), (0, a_ref)):
        for h in HALVES:
            out[1, h] = tags[side, h].astype(jnp.float32)


def prepare_kernel(
    t_ref, tag_ref, cond_ref, store_ref, halo, t0, gxa, gxm, gy, gz, coeff, t1, ta, tags, cond, sem
):
    planes, ny = t_ref.shape[0], t_ref.shape[1]
    copies = []
    for j in range(planes):
        x = plane_of(j, planes)
        for h in HALVES:
            part = pl.ds(h * LANES, LANES)
            rows = pl.ds(PAD + j * ny, ny)
            copies.append(pltpu.make_async_copy(tag_ref.at[x, :, part], tags.at[h, pl.ds(j * ny, ny)], sem.at[0, j, h]))
            copies.append(pltpu.make_async_copy(t_ref.at[x, :, part], t0.at[h, rows], sem.at[1, j, h]))
    for copy in copies:
        copy.start()
    zero = jnp.zeros((PAD, LANES), jnp.float32)
    for h in HALVES:
        for ref in (t0, t1, cond):
            ref[h, pl.ds(0, PAD), :] = zero
            ref[h, pl.ds(ref.shape[1] - PAD, PAD), :] = zero
        gy[h, pl.ds(0, PAD), :] = zero
    shape = (STRIP, LANES)
    lane = lanes_iota(STRIP)
    conds = [jnp.full((1, LANES), cond_ref[m], jnp.float32) for m in range(cond_ref.shape[0])]
    scales = [0.16 / jnp.full((1, LANES), store_ref[m], jnp.float32) for m in range(store_ref.shape[0])]
    for copy in copies:
        copy.wait()

    def materials(r):
        for h in HALVES:
            tag = tags[h, pl.ds(r, STRIP), :]
            cond[h, pl.ds(PAD + r, STRIP), :] = pick(tag, conds)
            coeff[h, pl.ds(r, STRIP), :] = pick(tag, scales)

    rows_loop(planes * ny, materials)

    def halo_face(y):
        for h in HALVES:
            other = pick(halo[1, h, pl.ds(y, STRIP), :].astype(jnp.int32), conds)
            gxa[h, pl.ds(y, STRIP), :] = face_mean(cond[h, pl.ds(PAD + y, STRIP), :], other)

    rows_loop(ny, halo_face)

    def x_faces(r):
        for h in HALVES:
            mine = cond[h, pl.ds(PAD + r, STRIP), :]
            gxm[h, pl.ds(r, STRIP), :] = face_mean(mine, cond[h, pl.ds(PAD + r + ny, STRIP), :])

    rows_loop((planes - 1) * ny, x_faces)

    def yz_faces(r):
        y = lax.rem(r, ny) + lax.broadcasted_iota(jnp.int32, shape, 0)
        mine = [cond[h, pl.ds(PAD + r, STRIP), :] for h in HALVES]
        nxt = [pltpu.roll(mine[h], LANES - 1, 1) for h in HALVES]
        ahead = [jnp.where(lane == LANES - 1, nxt[1], nxt[0]), nxt[1]]
        prv = [pltpu.roll(mine[h], 1, 1) for h in HALVES]
        behind = [prv[0], jnp.where(lane == 0, prv[0], prv[1])]
        for h in HALVES:
            below = face_mean(mine[h], cond[h, pl.ds(PAD + r + 1, STRIP), :])
            gy[h, pl.ds(PAD + r, STRIP), :] = jnp.where(y == ny - 1, 0.0, below)
            right = face_mean(mine[h], ahead[h])
            gz[h, pl.ds(r, STRIP), :] = jnp.where(lane == LANES - 1, 0.0, right) if h else right
            left = face_mean(behind[h], mine[h])
            gz[2 + h, pl.ds(r, STRIP), :] = left if h else jnp.where(lane == 0, 0.0, left)

    rows_loop(planes * ny, yz_faces)

    def emit(j, y, new, first):
        for h in HALVES:
            t1[h, pl.ds(PAD + j * ny + y, STRIP), :] = new[h]
            if first:
                ta[h, pl.ds(y, STRIP), :] = new[h]

    def last(h, y):
        return t0[h, pl.ds(PAD + (planes - 1) * ny + y, STRIP), :]

    main_planes(t0, last, halo.at[0], gxa, gxm, gy, gz, coeff, planes, ny, emit)


def last_plane(cur, below, halo, gxb, gxm, gy, gz, coeff, ny, emit):
    rows = gz.shape[1]
    base = rows - ny

    def body(y):
        new = advance_rows(
            cur,
            PAD + y,
            lambda h: halo[h, pl.ds(y, STRIP), :],
            lambda h: below(h, y),
            lambda h: gxb[h, pl.ds(y, STRIP), :],
            lambda h: gxm[h, pl.ds(base - ny + y, STRIP), :],
            gy,
            PAD + base + y,
            gz,
            coeff,
            base + y,
        )
        emit(y, new)

    rows_loop(ny, body, unroll=8)


def padded(pad, rows_of, ny):
    zero = jnp.zeros((PAD, LANES), jnp.float32)
    for h in HALVES:
        pad[h, pl.ds(0, PAD), :] = zero
        pad[h, pl.ds(PAD + ny, PAD), :] = zero

    def body(y):
        for h in HALVES:
            pad[h, pl.ds(PAD + y, STRIP), :] = rows_of(h, y)

    rows_loop(ny, body)


def first_last_kernel(brick_count, tag_ref, cond_ref, t0, halo, gxm, gy, gz, coeff, gxb, tb, pad, tags, sem):
    ny = tb.shape[1]
    planes = gz.shape[1] // ny
    base = (planes - 1) * ny
    x = plane_of(planes - 1, planes)
    copies = [
        pltpu.make_async_copy(tag_ref.at[x, :, pl.ds(h * LANES, LANES)], tags.at[h], sem.at[h])
        for h in HALVES
    ]
    for copy in copies:
        copy.start()
    me = lax.axis_index("brick")
    edge = (me == 0) | (me == brick_count - 1)
    keep = jnp.where(edge, 0.0, 1.0).astype(jnp.float32)
    conds = [jnp.full((1, LANES), cond_ref[m], jnp.float32) for m in range(cond_ref.shape[0])]
    padded(pad, lambda h, y: t0[h, pl.ds(PAD + base + y, STRIP), :], ny)
    for copy in copies:
        copy.wait()

    def faces(y):
        for h in HALVES:
            other = keep * pick(halo[1, h, pl.ds(y, STRIP), :].astype(jnp.int32), conds)
            mine = pick(tags[h, pl.ds(y, STRIP), :], conds)
            gxb[h, pl.ds(y, STRIP), :] = face_mean(mine, other)

    rows_loop(ny, faces)

    def emit(y, new):
        for h in HALVES:
            tb[h, pl.ds(y, STRIP), :] = new[h]

    def below(h, y):
        return t0[h, pl.ds(PAD + base - ny + y, STRIP), :]

    last_plane(pad, below, halo.at[0], gxb, gxm, gy, gz, coeff, ny, emit)


def next_last_kernel(tm, tb_old, halo, gxb, gxm, gy, gz, coeff, tb, pad):
    ny = tb.shape[1]
    planes = gz.shape[1] // ny
    padded(pad, lambda h, y: tb_old[h, pl.ds(y, STRIP), :], ny)

    def emit(y, new):
        for h in HALVES:
            tb[h, pl.ds(y, STRIP), :] = new[h]

    def below(h, y):
        return tm[h, pl.ds(PAD + (planes - 2) * ny + y, STRIP), :]

    last_plane(pad, below, halo, gxb, gxm, gy, gz, coeff, ny, emit)


def next_main_kernel(tm, tb_old, halo, gxa, gxm, gy, gz, coeff, out, ta):
    ny = ta.shape[1]
    planes = gz.shape[1] // ny
    zero = jnp.zeros((PAD, LANES), jnp.float32)
    for h in HALVES:
        out[h, pl.ds(0, PAD), :] = zero
        out[h, pl.ds(out.shape[1] - PAD, PAD), :] = zero

    def emit(j, y, new, first):
        for h in HALVES:
            out[h, pl.ds(PAD + j * ny + y, STRIP), :] = new[h]
            if first:
                ta[h, pl.ds(y, STRIP), :] = new[h]

    def last(h, y):
        return tb_old[h, pl.ds(y, STRIP), :]

    main_planes(tm, last, halo, gxa, gxm, gy, gz, coeff, planes, ny, emit)


def bin_rows(heat, owner, start, count, totals, lines):
    def turn(s, acc):
        r = pl.multiple_of(start + s * 8, 8)
        own = owner[pl.ds(r, 8), :]
        hot = heat[pl.ds(r, 8), :]
        return tuple(acc[k] + jnp.where(own == k, hot, 0.0) for k in range(lines))

    acc = lax.fori_loop(0, count // 8, turn, tuple(totals[k] for k in range(lines)), unroll=4)
    for k in range(lines):
        totals[k] = acc[k]


def final_main_kernel(tm, tb_old, halo, gxa, gxm, gy, gz, coeff, owner, heat, totals):
    ny = tb_old.shape[1]
    planes = gz.shape[1] // ny
    rows = planes * ny

    def emit(j, y, new, first):
        for h in HALVES:
            heat[pl.ds(h * rows + j * ny + y, STRIP), :] = new[h]

    def last(h, y):
        return tb_old[h, pl.ds(y, STRIP), :]

    main_planes(tm, last, halo, gxa, gxm, gy, gz, coeff, planes, ny, emit)
    totals[...] = jnp.zeros_like(totals)
    for h in HALVES:
        bin_rows(heat, owner, h * rows, rows - ny, totals, totals.shape[0])


def unpack(entry):
    row = lax.shift_right_logical(entry, 20)
    lane = lax.shift_right_logical(entry, 13) & (LANES - 1)
    return row, lane


def walls_kernel(
    wall, tm, tb_old, halo, gxb, gxm, gy, gz, coeff, owner, extra, extra_n, totals_in, film, ratio, heat_in, heat, send, pad, totals, sums
):
    ny = tb_old.shape[1]
    rows = gz.shape[1]
    planes = rows // ny
    lines = totals.shape[0]
    padded(pad, lambda h, y: tb_old[h, pl.ds(y, STRIP), :], ny)

    def emit(y, new):
        for h in HALVES:
            heat[pl.ds(h * rows + rows - ny + y, STRIP), :] = new[h]

    def below(h, y):
        return tm[h, pl.ds(PAD + (planes - 2) * ny + y, STRIP), :]

    last_plane(pad, below, halo, gxb, gxm, gy, gz, coeff, ny, emit)
    totals[...] = totals_in[...]
    for h in HALVES:
        bin_rows(heat, owner, h * rows + rows - ny, ny, totals, lines)
    sums[...] = jnp.sum(totals[...], axis=1)
    lane = lanes_iota(1)

    def more(n, carry):
        entry = extra[n]
        row, col = unpack(entry)
        line = lax.shift_right_logical(entry, wall.bit_length() - 1) & (lines - 1)
        hit = jnp.where(lane == col, heat[pl.ds(row, 1), :], 0.0)
        sums[pl.ds(line, 1), :] = sums[pl.ds(line, 1), :] + hit
        return carry

    lax.fori_loop(0, extra_n[0], more, 0)
    mean = lax.dot_general(
        jnp.ones((8, LANES), jnp.float32),
        sums[...],
        (((1,), (1,)), ((), ())),
        precision=lax.Precision.HIGHEST,
        preferred_element_type=jnp.float32,
    )[0:1] * (1.0 / wall)
    keep = jnp.exp(-ratio[...] * film[...])
    gain = (1.0 - keep) * mean
    count = send.shape[0]
    send[...] = jnp.zeros_like(send)
    send[:, 0:lines] = jnp.broadcast_to(keep, (count, lines))
    send[:, lines : 2 * lines] = jnp.broadcast_to(gain, (count, lines))


def owners_kernel(wall, keys, packed, ordered, owner, extra, extra_n, words, words_s, sem):
    rows, total = owner.shape[0], keys.shape[0]
    lines = total // wall
    bits = 32
    one = packed[...]
    depth = one.shape[0]
    nxt = pltpu.roll(one, LANES - 1, 1)
    wrap = pltpu.roll(nxt, depth - 1, 0)
    lane = lanes_iota(depth)
    place = lax.broadcasted_iota(jnp.int32, (depth, LANES), 0)
    after = jnp.where(lane == LANES - 1, wrap, nxt)
    same = lax.shift_right_logical(one ^ after, 13) == 0
    same = same & ((lane < LANES - 1) | (place < depth - 1))
    flag = jnp.where(same, lax.shift_left(jnp.int32(1), place & (bits - 1)), 0)
    words[...] = jnp.zeros_like(words)
    for g in range(depth // bits):
        words[pl.ds(g, 1), :] = jnp.sum(flag[g * bits : (g + 1) * bits], axis=0, keepdims=True)
    copy = pltpu.make_async_copy(words, words_s, sem)
    copy.start()

    def clear(r):
        owner[pl.ds(r, 64), :] = jnp.full((64, LANES), LANES - 1, jnp.int32)

    rows_loop(rows, clear, 64)
    ones = lanes_iota(1)
    unroll = 32

    def line(k, carry):
        value = jnp.full((1, LANES), k, jnp.int32)

        def body(s, inner):
            for u in range(unroll):
                key = keys[k * wall + s * unroll + u]
                row = lax.shift_right_logical(key, 7)
                pltpu.store(owner.at[pl.ds(row, 1), :], value, mask=ones == (key & (LANES - 1)))
            return inner

        return lax.fori_loop(0, wall // unroll, body, carry)

    lax.fori_loop(0, lines, line, 0)
    copy.wait()

    def lane_turn(c, n):
        for g in range(depth // bits):

            def go(state):
                word, n = state
                low = word & (-word)
                bit = 31 - lax.clz(low)
                extra[n] = ordered[(g * bits + bit) * LANES + c]
                return word ^ low, n + 1

            _, n = lax.while_loop(lambda state: state[0] != 0, go, (words_s[g, c], n))
        return n

    extra_n[0] = lax.fori_loop(0, LANES, lane_turn, 0)


def finish_kernel(
    wall, heat, owner, extra, extra_n, rows_all, film, ratio, direction, entry, out, mid, final, table, splat, sem
):
    planes, ny = out.shape[0], out.shape[1]
    rows = planes * ny
    count, lines = rows_all.shape[0], mid.shape[1]
    me = lax.axis_index("brick")

    def pass_on(k, water):
        row = rows_all[pl.ds(k, 1), :]
        return row[:, 0:lines] * water + row[:, lines : 2 * lines]

    start = entry[...]
    ahead = lax.fori_loop(0, me, pass_on, start)
    behind = lax.fori_loop(0, count - 1 - me, lambda k, w: pass_on(count - 1 - k, w), start)
    inflow = jnp.where(direction[...] == 0, ahead, behind)
    own = rows_all[pl.ds(me, 1), :]
    keep, gain = own[:, 0:lines], own[:, lines : 2 * lines]
    coolant = 0.5 * (inflow + keep * inflow + gain)
    mid[...] = coolant
    table[...] = jnp.zeros_like(table)
    table[0:1, 0:lines] = 0.5 * (1.0 - keep)
    table[1:2, 0:lines] = coolant
    eye = lax.broadcasted_iota(jnp.int32, (lines, LANES), 0) == lanes_iota(lines)
    for k in range(2):
        spread = jnp.broadcast_to(table[k : k + 1, :], (lines, LANES))
        column = jnp.sum(jnp.where(eye, spread, 0.0), axis=1, keepdims=True)
        splat[k] = jnp.broadcast_to(column, (lines, LANES))
    pull = jnp.broadcast_to(table[0:1, :], (8, LANES))
    cool = jnp.broadcast_to(table[1:2, :], (8, LANES))

    def dense(r):
        own = owner[pl.ds(r, 8), :]
        hot = heat[pl.ds(r, 8), :]
        a = jnp.take_along_axis(pull, own, axis=1)
        c = jnp.take_along_axis(cool, own, axis=1)
        final[pl.ds(r, 8), :] = hot + a * (c - hot)

    rows_loop(2 * rows, dense, 8, unroll=16)
    lane = lanes_iota(1)

    def more(n, carry):
        item = extra[n]
        row, col = unpack(item)
        line = lax.shift_right_logical(item, wall.bit_length() - 1) & (lines - 1)
        a = splat[0, pl.ds(line, 1), :]
        c = splat[1, pl.ds(line, 1), :]
        hot = heat[pl.ds(row, 1), :]
        final[pl.ds(row, 1), :] = final[pl.ds(row, 1), :] + jnp.where(lane == col, a * (c - hot), 0.0)
        return carry

    lax.fori_loop(0, extra_n[0], more, 0)
    copies = []
    for j in range(planes):
        x = plane_of(j, planes)
        for h in HALVES:
            copies.append(
                pltpu.make_async_copy(
                    final.at[pl.ds(h * rows + j * ny, ny), :],
                    out.at[x, :, pl.ds(h * LANES, LANES)],
                    sem.at[j, h],
                )
            )
    for copy in copies:
        copy.start()
    for copy in copies:
        copy.wait()


def per_device(
    initial_voxel_degrees,
    alloy_tag_per_voxel,
    thermal_conductance_per_alloy,
    specific_storage_per_alloy,
    bore_boundary_positions,
    surface_transfer_coefficient,
    surface_over_flow_ratio,
    flow_direction_flag,
    entry_coolant_degrees,
):
    planes, ny, nz = initial_voxel_degrees.shape
    _, lines, wall = bore_boundary_positions.shape
    rows, hits = planes * ny, lines * wall
    count = lax.axis_size("brick")
    me = lax.axis_index("brick")
    dma = pltpu.SemaphoreType.DMA
    on_chip = [(i, i ^ 1) for i in range(count)]
    across = [(i, (i + 1) % count) for i in range(1, count, 2)]
    across = across + [(b, a) for a, b in across]

    def swap(value, pairs):
        return lax.ppermute(value, "brick", pairs)

    plane = f32(2, ny, LANES)
    pair = f32(2, 2, ny, LANES)
    ta, tb = call(
        send_kernel,
        (initial_voxel_degrees, alloy_tag_per_voxel),
        [HBM, HBM],
        (pair, pair),
        (VMEM, VMEM),
        [pltpu.VMEM((2, 2, ny, LANES), jnp.int32), dma((8,))],
    )
    halo_b = swap(tb, across)
    halo_a = swap(ta, on_chip)

    cell = bore_boundary_positions.reshape(hits)
    flip = jnp.where(lax.rem(me, 2) == 1, 0, (planes - 1) * ny * nz)
    cell = cell ^ flip
    keys = ((cell & LANES) * (rows * LANES // LANES)) | ((cell >> 8) << 7) | (cell & (LANES - 1))
    packed = lax.sort(keys * 8192 + lax.iota(jnp.int32, hits), is_stable=False)
    owner, extra, extra_n = call(
        lambda *refs: owners_kernel(wall, *refs),
        (keys, packed.reshape(hits // LANES, LANES), packed),
        [SMEM, VMEM, SMEM],
        (i32(2 * rows, LANES), i32(hits), i32(1)),
        (VMEM, SMEM, SMEM),
        [pltpu.VMEM((8, LANES), jnp.int32), pltpu.SMEM((8, LANES), jnp.int32), dma],
        cost=20_000_000,
    )

    full = f32(2, rows + 2 * PAD, LANES)
    most = f32(2, rows - ny + 2 * PAD, LANES)
    t0, gxa, gxm, gy, gz, coeff, t1, ta = call(
        prepare_kernel,
        (
            initial_voxel_degrees,
            alloy_tag_per_voxel,
            thermal_conductance_per_alloy,
            specific_storage_per_alloy,
            halo_a,
        ),
        [HBM, HBM, SMEM, SMEM, VMEM],
        (full, plane, f32(2, rows - ny, LANES), full, f32(4, rows, LANES), f32(2, rows, LANES), most, plane),
        (VMEM,) * 8,
        [
            pltpu.VMEM((2, rows, LANES), jnp.int32),
            pltpu.VMEM((2, rows + 2 * PAD, LANES), jnp.float32),
            dma((2, planes, 2)),
        ],
        cost=10_000_000,
    )
    pad = pltpu.VMEM((2, ny + 2 * PAD, LANES), jnp.float32)
    gxb, tb = call(
        lambda *refs: first_last_kernel(count, *refs),
        (alloy_tag_per_voxel, thermal_conductance_per_alloy, t0, halo_b, gxm, gy, gz, coeff),
        [HBM, SMEM] + [VMEM] * 6,
        (plane, plane),
        (VMEM, VMEM),
        [pad, pltpu.VMEM((2, ny, LANES), jnp.int32), dma((2,))],
    )
    halo_b = swap(tb, across)
    halo_a = swap(ta, on_chip)

    t2, ta = call(
        next_main_kernel,
        (t1, tb, halo_a, gxa, gxm, gy, gz, coeff),
        [VMEM] * 8,
        (most, plane),
        (VMEM, VMEM),
        cost=4_000_000,
    )
    tb2 = call(
        next_last_kernel,
        (t1, tb, halo_b, gxb, gxm, gy, gz, coeff),
        [VMEM] * 8,
        plane,
        VMEM,
        [pad],
    )
    halo_b = swap(tb2, across)
    halo_a = swap(ta, on_chip)

    heat, totals = call(
        final_main_kernel,
        (t2, tb2, halo_a, gxa, gxm, gy, gz, coeff, owner),
        [VMEM] * 9,
        (f32(2 * rows, LANES), f32(lines, 8, LANES)),
        (VMEM, VMEM),
        cost=10_000_000,
    )
    ratio = surface_over_flow_ratio.reshape(1, lines)
    heat, send = call(
        lambda *refs: walls_kernel(wall, *refs),
        (t2, tb2, halo_b, gxb, gxm, gy, gz, coeff, owner, extra, extra_n, totals, surface_transfer_coefficient, ratio, heat),
        [VMEM] * 9 + [SMEM, SMEM] + [VMEM] * 4,
        (f32(2 * rows, LANES), f32(count, LANES)),
        (VMEM, VMEM),
        [pad, pltpu.VMEM((lines, 8, LANES), jnp.float32), pltpu.VMEM((lines, LANES), jnp.float32)],
        input_output_aliases={14: 0},
    )
    rows_all = lax.all_to_all(send, "brick", 0, 0, tiled=True)
    final, mid = call(
        lambda *refs: finish_kernel(wall, *refs),
        (
            heat,
            owner,
            extra,
            extra_n,
            rows_all,
            surface_transfer_coefficient,
            ratio,
            flow_direction_flag.reshape(1, lines),
            entry_coolant_degrees.reshape(1, lines),
        ),
        [VMEM, VMEM, SMEM, SMEM] + [VMEM] * 5,
        (f32(planes, ny, nz), f32(1, lines)),
        (HBM, VMEM),
        [
            pltpu.VMEM((2 * rows, LANES), jnp.float32),
            pltpu.VMEM((8, LANES), jnp.float32),
            pltpu.VMEM((2, lines, LANES), jnp.float32),
            dma((planes, 2)),
        ],
    )
    return final, mid


def solution(mesh):
    return jax.shard_map(
        per_device,
        mesh=mesh,
        in_specs=(
            P(("pour", "brick"), None, None),
            P("brick", None, None),
            P(),
            P(),
            P("brick", None, None),
            P("brick", None),
            P(),
            P(),
            P("pour"),
        ),
        out_specs=(P(("pour", "brick"), None, None), P(("pour", "brick"), None)),
        check_vma=False,
    )
```

time: 223 us -> 114 us (0.51)
  other arithmetic: 92.1 us -> 5.61 us
  Pallas kernels: 0 us -> 58.8 us
  local copies, waits for them, and re-layouts: 57.2 us -> 22.1 us
  blocking collectives: 34.8 us -> 10.1 us
  starting transfers between devices: 33.5 us -> 9.3 us
  waiting for transfers between devices: 2.14 us -> 6.98 us
    pallas_call x0 -> x9, Pallas kernels: none -> 58.8 us  [call(): pl.pallas_call(kernel, out_shape=out_shape, in_specs=in_specs, out_specs=...]
    gather x2 -> x0, local copies, waits for them, and re-layouts: 45.5 us -> none  [per_device(): wall_temps = flat[cells]]
    scatter-add x1 -> x0, other arithmetic: 45 us -> none  [per_device(): flat.at[cells.reshape(-1)].add(change.reshape(-1))]
    unnamed x1 -> x0, blocking collectives: 34.8 us -> none
    add x3 -> x1, other arithmetic: 30.1 us -> 0.01 us  [per_device(): packed = lax.sort(keys * 8192 + lax.iota(jnp.int32, hits), is_stable=False)]
    ppermute x8 -> x6, starting transfers between devices: 33.5 us -> 9.3 us  [swap(): return lax.ppermute(value, 'brick', pairs)]
    unnamed x32 -> x55, local copies, waits for them, and re-layouts: 4.06 us -> 22.1 us
    all_to_all x0 -> x1, blocking collectives: none -> 10.1 us  [per_device(): rows_all = lax.all_to_all(send, 'brick', 0, 0, tiled=True)]
  transfers between devices with their start and end apart: 8 -> 6, of which waited for: 2 -> 1; matrix products, arithmetic and copies ran while one was open for 1% -> 5% of each run, Pallas kernels for 0% -> 38%
where the time goes in v1:
time: 114 us
  Pallas kernels  58.8 us (52%)
  local copies, waits for them, and re-layouts  22.1 us (19%)
  blocking collectives  10.1 us (9%)
  starting transfers between devices  9.3 us (8%)
  waiting for transfers between devices  6.98 us (6%)
  other arithmetic  5.61 us (5%)
    pallas_call x9, Pallas kernels, call(): pl.pallas_call(kernel, out_shape=out_shape, in_specs=in_specs, out_specs=...  58.8 us
    unnamed x55, local copies, waits for them, and re-layouts  22.1 us
    all_to_all x1, blocking collectives, per_device(): rows_all = lax.all_to_all(send, 'brick', 0, 0, tiled=True)  10.1 us
    ppermute x6, starting transfers between devices, swap(): return lax.ppermute(value, 'brick', pairs)  9.3 us
    ppermute x6, waiting for transfers between devices, swap(): return lax.ppermute(value, 'brick', pairs)  6.98 us
    sort x1, other arithmetic, per_device(): packed = lax.sort(keys * 8192 + lax.iota(jnp.int32, hits), is_stable=False)  5.59 us
  transfers between devices with their start and end apart: 6, of which 1 were waited for; matrix products, arithmetic and copies ran while one was open for 5% of the time, Pallas kernels for 38%

profile of v1, /device:TPU:0, one launch (start us, length us, event | category | flops | bytes accessed | tf_op | source)
XLA Modules:
  0.0 113.8 jit_solution(7254910999646358194)
XLA Ops:
  0.6 0.0 copy-start.13
  0.6 1.6 %copy-done.13 = s32[8,256,256]{2,1,0:T(8,128)S(1)} copy-done((s32[8,256,256]{2,1,0:T(8,128)S(1)}, s32[8,256,256]{2,1,0:T(8,128)}, u32[]{:S(2)}) %copy-start.13) | copy-done | bytes 2097176
  2.2 0.0 copy-start.15
  2.2 1.6 %copy-done.15 = f32[8,256,256]{2,1,0:T(8,128)S(1)} copy-done((f32[8,256,256]{2,1,0:T(8,128)S(1)}, f32[8,256,256]{2,1,0:T(8,128)}, u32[]{:S(2)}) %copy-start.15) | copy-done | bytes 2097176
  3.8 0.0 copy-start.22
  3.8 0.0 copy-start.23
  3.8 0.2 shard_map.104
  4.0 0.5 collective-permute-start
  4.5 0.0 copy-start.14
  4.5 5.7 %collective-permute-start.1 = (f32[2,2,256,128]{3,2,1,0:T(8,128)S(1)}, f32[2,2,256,128]{3,2,1,0:T(8,128)S(1)}, u32[]{:S(2)}, u32[]{:S(2)}) collective-permute-start(f32[2,2,256,128]{3,2,1,0:T(8,128)S(1)} %get-tuple-element.26), channel_id=1, source_target_pairs={{1,2},{3,4},{5,6},{7,8},{9,10},{11,12},{13,14},{15,0},{2,1},{4,3},... | collective-permute-start | bytes 1572872 | tf_op jit(solution)/shard_map/ppermute | solution.py:564
  10.2 0.0 collective-permute-done.halo
  10.2 0.0 copy-done.22
  10.2 0.0 copy-done.23
  10.2 10.2 %shard_map.105 = (f32[2,2064,128]{2,1,0:T(8,128)S(1)}, f32[2,256,128]{2,1,0:T(8,128)S(1)}, f32[2,1792,128]{2,1,0:T(8,128)S(1)}, f32[2,2064,128]{2,1,0:T(8,128)S(...) custom-call(f32[8,256,256]{2,1,0:T(8,128)S(1)} %copy-done.15, ...), custom_call_target="tpu_custom_call" | custom-call | flops 10000000 | bytes 10000000 | tf_op jit(solution)/shard_map/pallas_call | solution.py:26
  20.5 0.0 copy-start.18
  20.5 1.3 %copy-done.18 = f32[2,1808,128]{2,1,0:T(8,128)} copy-done((f32[2,1808,128]{2,1,0:T(8,128)}, f32[2,1808,128]{2,1,0:T(8,128)S(1)}, u32[]{:S(2)}) %copy-start.18) | copy-done | bytes 1851416
  21.7 0.0 copy-start
  21.7 0.0 copy-start.5
  21.7 0.0 copy-start.9
  21.7 0.0 collective-permute-done.1.refs_3_
  21.8 0.0 copy-done.14
  21.8 1.3 %shard_map.106 = (f32[2,256,128]{2,1,0:T(8,128)S(1)}, f32[2,256,128]{2,1,0:T(8,128)S(1)}) custom-call(s32[8,256,256]{2,1,0:T(8,128)S(1)} %copy-done.14, f32[8]{0:T(128)S(1)} %copy-done.22, f32[2,2064,128]{2,1,0:T(8,128)S(1)} %get-tuple-element.25.refs_2_, f32[2,2,256,128]{3,2,1,0:T(8,128)S(1)} %collective-permute-done.1.refs_3_, ...), custom_call_target="tpu_custom_call" | custom-call | flops 2000000 | bytes 2000000 | tf_op jit(solution)/shard_map/pallas_call | solution.py:26
  23.1 0.6 copy-done
  23.7 0.7 copy-done.5
  24.4 0.6 copy-done.9
  25.0 1.5 %collective-permute-start.3 = (f32[2,256,128]{2,1,0:T(8,128)S(1)}, f32[2,256,128]{2,1,0:T(8,128)S(1)}, u32[]{:S(2)}, u32[]{:S(2)}) collective-permute-start(f32[2,256,128]{2,1,0:T(8,128)S(1)} %get-tuple-element.31.tb_old), channel_id=1, source_target_pairs={{1,2},{3,4},{5,6},{7,8},{9,10},{11,12},{13,14},{15,0},{2,1},{4,3},... | collective-permute-start | bytes 786440 | tf_op jit(solution)/shard_map/ppermute | solution.py:564
  26.5 0.0 collective-permute-start.2
  26.5 7.0 %collective-permute-done.3.halo = f32[2,256,128]{2,1,0:T(8,128)S(1)} collective-permute-done((f32[2,256,128]{2,1,0:T(8,128)S(1)}, f32[2,256,128]{2,1,0:T(8,128)S(1)}, u32[]{:S(2)}, u32[]{:S(2)}) %collective-permute-start.3) | collective-permute-done | bytes 262176 | tf_op jit(solution)/shard_map/ppermute | solution.py:564
  33.5 0.0 copy-start.1
  33.5 2.2 %copy-done.1 = f32[4,2048,128]{2,1,0:T(8,128)S(1)} copy-done((f32[4,2048,128]{2,1,0:T(8,128)S(1)}, f32[4,2048,128]{2,1,0:T(8,128)}, u32[]{:S(2)}) %copy-start.1) | copy-done | bytes 4194328
  35.7 0.0 copy-start.6
  35.7 1.6 %copy-done.6 = f32[2,2048,128]{2,1,0:T(8,128)S(1)} copy-done((f32[2,2048,128]{2,1,0:T(8,128)S(1)}, f32[2,2048,128]{2,1,0:T(8,128)}, u32[]{:S(2)}) %copy-start.6) | copy-done | bytes 2097176
  37.3 1.5 %copy-done.10 = f32[2,1792,128]{2,1,0:T(8,128)S(1)} copy-done((f32[2,1792,128]{2,1,0:T(8,128)S(1)}, f32[2,1792,128]{2,1,0:T(8,128)}, u32[]{:S(2)}) %copy-start.10) | copy-done | bytes 1835032
  38.8 1.5 %copy-done.19 = f32[2,1808,128]{2,1,0:T(8,128)S(1)} copy-done((f32[2,1808,128]{2,1,0:T(8,128)S(1)}, f32[2,1808,128]{2,1,0:T(8,128)}, u32[]{:S(2)}) %copy-start.19) | copy-done | bytes 1851416
  40.3 0.3 shard_map.108.tb_old.refs_1_
  40.6 1.6 %collective-permute-start.4 = (f32[2,256,128]{2,1,0:T(8,128)S(1)}, f32[2,256,128]{2,1,0:T(8,128)S(1)}, u32[]{:S(2)}, u32[]{:S(2)}) collective-permute-start(f32[2,256,128]{2,1,0:T(8,128)S(1)} %shard_map.108.tb_old.refs_1_), channel_id=1, source_target_pairs={{1,2},{3,4},{5,6},{7,8},{9,10},{11,12},{13,14},{15,0},{2,1},{4,3},... | collective-permute-start | bytes 786440 | tf_op jit(solution)/shard_map/ppermute | solution.py:564
  42.2 0.0 collective-permute-done.2.halo
  42.2 0.3 copy-done.2
  42.5 0.6 copy-done.11
  43.1 3.9 %shard_map.107 = (f32[2,1808,128]{2,1,0:T(8,128)S(1)}, f32[2,256,128]{2,1,0:T(8,128)}) custom-call(f32[2,1808,128]{2,1,0:T(8,128)S(1)} %copy-done.19, f32[2,256,128]{2,1,0:T(8,128)S(1)} %get-tuple-element.31.tb_old, f32[2,256,128]{2,1,0:T(8,128)} %collective-permute-done.2.halo, f32[2,256,128]{2,1,0:T(8,128)S(1)} %get-tuple-element.33.gxa, ...), custom_call_target="tpu_custom_call" | custom-call | flops 4000000 | bytes 4000000 | tf_op jit(solution)/shard_map/pallas_call | solution.py:26
  46.9 1.3 %copy-done.16 = f32[2,1808,128]{2,1,0:T(8,128)} copy-done((f32[2,1808,128]{2,1,0:T(8,128)}, f32[2,1808,128]{2,1,0:T(8,128)S(1)}, u32[]{:S(2)}) %copy-start.16) | copy-done | bytes 1851416
  48.2 0.0 collective-permute-start.5
  48.2 0.0 copy-done.26
  48.3 5.6 %sort.7.refs_2_ = s32[8192]{0:T(1024)S(1)} sort(s32[8192]{0:T(1024)S(1)} %iota_add_fusion), dimensions={0}, to_apply=%region_0.1 | sort | flops 106496 | bytes 65536 | tf_op jit(solution)/shard_map/sort | solution.py:583
  53.9 18.6 %shard_map.109 = (s32[4096,128]{1,0:T(8,128)S(1)}, s32[8192]{0:T(1024)S(1)}, s32[1]{0:T(128)}) custom-call(s32[8192]{0:T(1024)S(1)} %bitcast.13, s32[64,128]{1,0:T(8,128)S(1)} %bitcast.11, s32[8192]{0:T(1024)S(1)} %sort.7.refs_2_), custom_call_target="tpu_custom_call" | custom-call | flops 20000000 | bytes 20000000 | tf_op jit(solution)/shard_map/pallas_call | solution.py:26
  72.5 0.0 collective-permute-done.5.halo
  72.5 0.0 copy-start.3
  72.5 2.2 %copy-done.3 = f32[4,2048,128]{2,1,0:T(8,128)S(1)} copy-done((f32[4,2048,128]{2,1,0:T(8,128)S(1)}, f32[4,2048,128]{2,1,0:T(8,128)}, u32[]{:S(2)}) %copy-start.3) | copy-done | bytes 4194328
  74.7 1.6 %copy-done.7 = f32[2,2048,128]{2,1,0:T(8,128)S(1)} copy-done((f32[2,2048,128]{2,1,0:T(8,128)S(1)}, f32[2,2048,128]{2,1,0:T(8,128)}, u32[]{:S(2)}) %copy-start.7) | copy-done | bytes 2097176
  76.3 1.5 %copy-done.12 = f32[2,1792,128]{2,1,0:T(8,128)S(1)} copy-done((f32[2,1792,128]{2,1,0:T(8,128)S(1)}, f32[2,1792,128]{2,1,0:T(8,128)}, u32[]{:S(2)}) %copy-start.12) | copy-done | bytes 1835032
  77.8 1.5 %copy-done.17 = f32[2,1808,128]{2,1,0:T(8,128)S(1)} copy-done((f32[2,1808,128]{2,1,0:T(8,128)S(1)}, f32[2,1808,128]{2,1,0:T(8,128)}, u32[]{:S(2)}) %copy-start.17) | copy-done | bytes 1851416
  79.3 10.0 %shard_map.110 = (f32[4096,128]{1,0:T(8,128)S(1)}, f32[32,8,128]{2,1,0:T(8,128)S(1)}) custom-call(f32[2,1808,128]{2,1,0:T(8,128)S(1)} %copy-done.17, f32[2,256,128]{2,1,0:T(8,128)S(1)} %shard_map.108.tb_old.refs_1_, f32[2,256,128]{2,1,0:T(8,128)} %collective-permute-done.5.halo, f32[2,256,128]{2,1,0:T(8,128)S(1)} %get-tuple-element.33.gxa, ...), custom_call_target="tpu_custom_call" | custom-call | flops 10000000 | bytes 10000000 | tf_op jit(solution)/shard_map/pallas_call | solution.py:26
  89.3 0.0 collective-permute-done.4.refs_2_
  89.4 0.0 copy-done.4
  89.4 0.0 copy-done.8
  89.4 0.0 copy-done.20
  89.4 0.0 copy-done.21
  89.4 0.0 copy-start.24
  89.4 0.0 copy-start.25
  89.4 3.9 %shard_map.111 = (f32[4096,128]{1,0:T(8,128)S(1)}, f32[16,128]{1,0:T(8,128)S(1)}) custom-call(f32[2,1808,128]{2,1,0:T(8,128)S(1)} %copy-done.17, f32[2,256,128]{2,1,0:T(8,128)S(1)} %shard_map.108.tb_old.refs_1_, f32[2,256,128]{2,1,0:T(8,128)S(1)} %collective-permute-done.4.refs_2_, ...), custom_call_target="tpu_custom_call", output_to_operand_aliasing={{0}: (14, {})} | custom-call | flops 2000000 | bytes 2000000 | tf_op jit(solution)/shard_map/pallas_call | solution.py:26
  93.3 10.1 %all_to_all.11 = f32[16,1,128]{2,1,0:T(1,128)S(1)} all-to-all(f32[16,1,128]{2,1,0:T(1,128)S(1)} %bitcast.15), channel_id=1, replica_groups=mesh['pour'=2,'brick'=16] {'brick'}, dimensions={0} | all-to-all | bytes 16384 | tf_op jit(solution)/shard_map/all_to_all | solution.py:664
  103.4 0.0 copy-done.24
  103.4 0.0 copy-done.25
  103.4 10.4 %shard_map.112 = (f32[8,256,256]{2,1,0:T(8,128)}, f32[1,32]{1,0:T(1,128)}) custom-call(f32[4096,128]{1,0:T(8,128)S(1)} %get-tuple-element.42.refs_0_, s32[4096,128]{1,0:T(8,128)S(1)} %get-tuple-element.36.owner.refs_8_.refs_1_, s32[8192]{0:T(1024)S(1)} %get-tuple-element.37.refs_9_.refs_2_, s32[1]{0:T(128)} %get-tuple-element.38.refs_10_.refs_3_, ...), custom_call_target="tpu_custom_call" | custom-call | flops 2000000 | bytes 2000000 | tf_op jit(solution)/shard_map/pallas_call | solution.py:26
  (16 shorter events, 0.1 us)
Async XLA Ops:
  0.6 1.6 %copy-start.13 = (s32[8,256,256]{2,1,0:T(8,128)S(1)}, s32[8,256,256]{2,1,0:T(8,128)}, u32[]{:S(2)}) copy-start(s32[8,256,256]{2,1,0:T(8,128)} %refs_0_.1) | copy-start | bytes 6291460
  2.2 1.6 %copy-start.15 = (f32[8,256,256]{2,1,0:T(8,128)S(1)}, f32[8,256,256]{2,1,0:T(8,128)}, u32[]{:S(2)}) copy-start(f32[8,256,256]{2,1,0:T(8,128)} %t_ref.3) | copy-start | bytes 6291460
  3.8 6.4 %copy-start.22 = (f32[8]{0:T(128)S(1)}, f32[8]{0:T(128)}, u32[]{:S(2)}) copy-start(f32[8]{0:T(128)} %refs_1_.1) | copy-start | bytes 100
  3.8 6.4 %copy-start.23 = (f32[8]{0:T(128)S(1)}, f32[8]{0:T(128)}, u32[]{:S(2)}) copy-start(f32[8]{0:T(128)} %store_ref.1) | copy-start | bytes 100
  4.0 6.2 %collective-permute-start = (f32[2,2,256,128]{3,2,1,0:T(8,128)S(1)}, f32[2,2,256,128]{3,2,1,0:T(8,128)S(1)}, u32[]{:S(2)}, u32[]{:S(2)}) collective-permute-start(f32[2,2,256,128]{3,2,1,0:T(8,128)S(1)} %get-tuple-element.23), channel_id=1, source_target_pairs={{0,1},{1,0},{2,3},{3,2},{4,5},{5,4},{6,7},{7,6},{8,9},{9,8},{10,11... | collective-permute-start | bytes 1572872 | tf_op jit(solution)/shard_map/ppermute | solution.py:564
  4.5 17.2 %copy-start.14 = (s32[8,256,256]{2,1,0:T(8,128)S(1)}, s32[8,256,256]{2,1,0:T(8,128)}, u32[]{:S(2)}) copy-start(s32[8,256,256]{2,1,0:T(8,128)} %refs_0_.1) | copy-start | bytes 6291460
  4.5 17.2 %collective-permute-start.1 = (f32[2,2,256,128]{3,2,1,0:T(8,128)S(1)}, f32[2,2,256,128]{3,2,1,0:T(8,128)S(1)}, u32[]{:S(2)}, u32[]{:S(2)}) collective-permute-start(f32[2,2,256,128]{3,2,1,0:T(8,128)S(1)} %get-tuple-element.26), channel_id=1, source_target_pairs={{1,2},{3,4},{5,6},{7,8},{9,10},{11,12},{13,14},{15,0},{2,1},{4,3},... | collective-permute-start | bytes 1572872 | tf_op jit(solution)/shard_map/ppermute | solution.py:564
  20.5 1.3 %copy-start.18 = (f32[2,1808,128]{2,1,0:T(8,128)}, f32[2,1808,128]{2,1,0:T(8,128)S(1)}, u32[]{:S(2)}) copy-start(f32[2,1808,128]{2,1,0:T(8,128)S(1)} %get-tuple-element.24.tm) | copy-start | bytes 5554180
  21.7 2.0 %copy-start = (f32[4,2048,128]{2,1,0:T(8,128)}, f32[4,2048,128]{2,1,0:T(8,128)S(1)}, u32[]{:S(2)}) copy-start(f32[4,2048,128]{2,1,0:T(8,128)S(1)} %get-tuple-element.29.refs_6_.gz) | copy-start | bytes 12582916
  21.7 2.7 %copy-start.5 = (f32[2,2048,128]{2,1,0:T(8,128)}, f32[2,2048,128]{2,1,0:T(8,128)S(1)}, u32[]{:S(2)}) copy-start(f32[2,2048,128]{2,1,0:T(8,128)S(1)} %get-tuple-element.30.refs_7_.coeff) | copy-start | bytes 6291460
  21.7 3.3 %copy-start.9 = (f32[2,1792,128]{2,1,0:T(8,128)}, f32[2,1792,128]{2,1,0:T(8,128)S(1)}, u32[]{:S(2)}) copy-start(f32[2,1792,128]{2,1,0:T(8,128)S(1)} %get-tuple-element.27.refs_4_.gxm) | copy-start | bytes 5505028
  25.0 8.5 %collective-permute-start.3 = (f32[2,256,128]{2,1,0:T(8,128)S(1)}, f32[2,256,128]{2,1,0:T(8,128)S(1)}, u32[]{:S(2)}, u32[]{:S(2)}) collective-permute-start(f32[2,256,128]{2,1,0:T(8,128)S(1)} %get-tuple-element.31.tb_old), channel_id=1, source_target_pairs={{1,2},{3,4},{5,6},{7,8},{9,10},{11,12},{13,14},{15,0},{2,1},{4,3},... | collective-permute-start | bytes 786440 | tf_op jit(solution)/shard_map/ppermute | solution.py:564
  26.5 15.7 %collective-permute-start.2 = (f32[2,256,128]{2,1,0:T(8,128)}, f32[2,256,128]{2,1,0:T(8,128)}, u32[]{:S(2)}, u32[]{:S(2)}) collective-permute-start(f32[2,256,128]{2,1,0:T(8,128)} %get-tuple-element.32), channel_id=1, source_target_pairs={{0,1},{1,0},{2,3},{3,2},{4,5},{5,4},{6,7},{7,6},{8,9},{9,8},{10,11... | collective-permute-start | bytes 786440 | tf_op jit(solution)/shard_map/ppermute | solution.py:564
  33.5 2.2 %copy-start.1 = (f32[4,2048,128]{2,1,0:T(8,128)S(1)}, f32[4,2048,128]{2,1,0:T(8,128)}, u32[]{:S(2)}) copy-start(f32[4,2048,128]{2,1,0:T(8,128)} %copy-done) | copy-start | bytes 12582916
  35.7 1.6 %copy-start.6 = (f32[2,2048,128]{2,1,0:T(8,128)S(1)}, f32[2,2048,128]{2,1,0:T(8,128)}, u32[]{:S(2)}) copy-start(f32[2,2048,128]{2,1,0:T(8,128)} %copy-done.5) | copy-start | bytes 6291460
  37.3 1.5 %copy-start.10 = (f32[2,1792,128]{2,1,0:T(8,128)S(1)}, f32[2,1792,128]{2,1,0:T(8,128)}, u32[]{:S(2)}) copy-start(f32[2,1792,128]{2,1,0:T(8,128)} %copy-done.9) | copy-start | bytes 5505028
  38.8 1.5 %copy-start.19 = (f32[2,1808,128]{2,1,0:T(8,128)S(1)}, f32[2,1808,128]{2,1,0:T(8,128)}, u32[]{:S(2)}) copy-start(f32[2,1808,128]{2,1,0:T(8,128)} %copy-done.18) | copy-start | bytes 5554180
  40.3 2.2 %copy-start.2 = (f32[4,2048,128]{2,1,0:T(8,128)S(1)}, f32[4,2048,128]{2,1,0:T(8,128)}, u32[]{:S(2)}) copy-start(f32[4,2048,128]{2,1,0:T(8,128)} %copy-done) | copy-start | bytes 12582916
  40.3 2.8 %copy-start.11 = (f32[2,1792,128]{2,1,0:T(8,128)S(1)}, f32[2,1792,128]{2,1,0:T(8,128)}, u32[]{:S(2)}) copy-start(f32[2,1792,128]{2,1,0:T(8,128)} %copy-done.9) | copy-start | bytes 5505028
  40.6 48.7 %collective-permute-start.4 = (f32[2,256,128]{2,1,0:T(8,128)S(1)}, f32[2,256,128]{2,1,0:T(8,128)S(1)}, u32[]{:S(2)}, u32[]{:S(2)}) collective-permute-start(f32[2,256,128]{2,1,0:T(8,128)S(1)} %shard_map.108.tb_old.refs_1_), channel_id=1, source_target_pairs={{1,2},{3,4},{5,6},{7,8},{9,10},{11,12},{13,14},{15,0},{2,1},{4,3},... | collective-permute-start | bytes 786440 | tf_op jit(solution)/shard_map/ppermute | solution.py:564
  43.1 5.2 %copy-start.26 = (s32[1,32,256]{2,1,0:T(8,128)S(1)}, s32[1,32,256]{2,1,0:T(8,128)}, u32[]{:S(2)}) copy-start(s32[1,32,256]{2,1,0:T(8,128)} %param.13) | copy-start | bytes 98308
  46.9 1.3 %copy-start.16 = (f32[2,1808,128]{2,1,0:T(8,128)}, f32[2,1808,128]{2,1,0:T(8,128)S(1)}, u32[]{:S(2)}) copy-start(f32[2,1808,128]{2,1,0:T(8,128)S(1)} %get-tuple-element.34.tm.refs_0_) | copy-start | bytes 5554180
  48.2 24.3 %collective-permute-start.5 = (f32[2,256,128]{2,1,0:T(8,128)}, f32[2,256,128]{2,1,0:T(8,128)}, u32[]{:S(2)}, u32[]{:S(2)}) collective-permute-start(f32[2,256,128]{2,1,0:T(8,128)} %get-tuple-element.39), channel_id=1, source_target_pairs={{0,1},{1,0},{2,3},{3,2},{4,5},{5,4},{6,7},{7,6},{8,9},{9,8},{10,11... | collective-permute-start | bytes 786440 | tf_op jit(solution)/shard_map/ppermute | solution.py:564
  72.5 2.2 %copy-start.3 = (f32[4,2048,128]{2,1,0:T(8,128)S(1)}, f32[4,2048,128]{2,1,0:T(8,128)}, u32[]{:S(2)}) copy-start(f32[4,2048,128]{2,1,0:T(8,128)} %copy-done) | copy-start | bytes 12582916
  74.7 1.6 %copy-start.7 = (f32[2,2048,128]{2,1,0:T(8,128)S(1)}, f32[2,2048,128]{2,1,0:T(8,128)}, u32[]{:S(2)}) copy-start(f32[2,2048,128]{2,1,0:T(8,128)} %copy-done.5) | copy-start | bytes 6291460
  76.3 1.5 %copy-start.12 = (f32[2,1792,128]{2,1,0:T(8,128)S(1)}, f32[2,1792,128]{2,1,0:T(8,128)}, u32[]{:S(2)}) copy-start(f32[2,1792,128]{2,1,0:T(8,128)} %copy-done.9) | copy-start | bytes 5505028
  77.8 1.5 %copy-start.17 = (f32[2,1808,128]{2,1,0:T(8,128)S(1)}, f32[2,1808,128]{2,1,0:T(8,128)}, u32[]{:S(2)}) copy-start(f32[2,1808,128]{2,1,0:T(8,128)} %copy-done.16) | copy-start | bytes 5554180
  79.3 10.1 %copy-start.4 = (f32[4,2048,128]{2,1,0:T(8,128)S(1)}, f32[4,2048,128]{2,1,0:T(8,128)}, u32[]{:S(2)}) copy-start(f32[4,2048,128]{2,1,0:T(8,128)} %copy-done) | copy-start | bytes 12582916
  79.3 10.1 %copy-start.8 = (f32[2,2048,128]{2,1,0:T(8,128)S(1)}, f32[2,2048,128]{2,1,0:T(8,128)}, u32[]{:S(2)}) copy-start(f32[2,2048,128]{2,1,0:T(8,128)} %copy-done.5) | copy-start | bytes 6291460
  79.3 10.1 %copy-start.20 = (f32[1,32]{1,0:T(1,128)S(1)}, f32[1,32]{1,0:T(1,128)}, u32[]{:S(2)}) copy-start(f32[1,32]{1,0:T(1,128)} %refs_5_.1) | copy-start | bytes 388
  79.3 10.1 %copy-start.21 = (f32[32]{0:T(128)S(1)}, f32[32]{0:T(128)}, u32[]{:S(2)}) copy-start(f32[32]{0:T(128)} %param.15) | copy-start | bytes 388
  89.4 14.0 %copy-start.24 = (s32[32]{0:T(128)S(1)}, s32[32]{0:T(128)}, u32[]{:S(2)}) copy-start(s32[32]{0:T(128)} %param.16) | copy-start | bytes 388
  89.4 14.0 %copy-start.25 = (f32[32]{0:T(128)S(1)}, f32[32]{0:T(128)}, u32[]{:S(2)}) copy-start(f32[32]{0:T(128)} %param.17) | copy-start | bytes 388

commit v2 on v1

--- a/solution.py
+++ b/solution.py
@@ -348,7 +348,7 @@
 
     def emit(j, y, new, first):
         for h in HALVES:
-            heat[pl.ds(h * rows + j * ny + y, STRIP), :] = new[h]
+            heat[pl.ds(h * rows + plane_of(j, planes) * ny + y, STRIP), :] = new[h]
 
     def last(h, y):
         return tb_old[h, pl.ds(y, STRIP), :]
@@ -356,7 +356,8 @@
     main_planes(tm, last, halo, gxa, gxm, gy, gz, coeff, planes, ny, emit)
     totals[...] = jnp.zeros_like(totals)
     for h in HALVES:
-        bin_rows(heat, owner, h * rows, rows - ny, totals, totals.shape[0])
+        first = jnp.where(plane_of(planes - 1, planes) == 0, ny, 0)
+        bin_rows(heat, owner, h * rows + first, rows - ny, totals, totals.shape[0])
 
 
 def unpack(entry):
@@ -372,11 +373,12 @@
     rows = gz.shape[1]
     planes = rows // ny
     lines = totals.shape[0]
+    at = plane_of(planes - 1, planes) * ny
     padded(pad, lambda h, y: tb_old[h, pl.ds(y, STRIP), :], ny)
 
     def emit(y, new):
         for h in HALVES:
-            heat[pl.ds(h * rows + rows - ny + y, STRIP), :] = new[h]
+            heat[pl.ds(h * rows + at + y, STRIP), :] = new[h]
 
     def below(h, y):
         return tm[h, pl.ds(PAD + (planes - 2) * ny + y, STRIP), :]
@@ -384,7 +386,7 @@
     last_plane(pad, below, halo, gxb, gxm, gy, gz, coeff, ny, emit)
     totals[...] = totals_in[...]
     for h in HALVES:
-        bin_rows(heat, owner, h * rows + rows - ny, ny, totals, lines)
+        bin_rows(heat, owner, h * rows + at, ny, totals, lines)
     sums[...] = jnp.sum(totals[...], axis=1)
     lane = lanes_iota(1)
 
@@ -523,14 +525,13 @@
 
     lax.fori_loop(0, extra_n[0], more, 0)
     copies = []
-    for j in range(planes):
-        x = plane_of(j, planes)
+    for x in range(planes):
         for h in HALVES:
             copies.append(
                 pltpu.make_async_copy(
-                    final.at[pl.ds(h * rows + j * ny, ny), :],
+                    final.at[pl.ds(h * rows + x * ny, ny), :],
                     out.at[x, :, pl.ds(h * LANES, LANES)],
-                    sem.at[j, h],
+                    sem.at[x, h],
                 )
             )
     for copy in copies:
@@ -554,7 +555,6 @@
     _, lines, wall = bore_boundary_positions.shape
     rows, hits = planes * ny, lines * wall
     count = lax.axis_size("brick")
-    me = lax.axis_index("brick")
     dma = pltpu.SemaphoreType.DMA
     on_chip = [(i, i ^ 1) for i in range(count)]
     across = [(i, (i + 1) % count) for i in range(1, count, 2)]
@@ -562,6 +562,9 @@
 
     def swap(value, pairs):
         return lax.ppermute(value, "brick", pairs)
+
+    initial_voxel_degrees = pltpu.with_memory_space_constraint(initial_voxel_degrees, pltpu.HBM)
+    alloy_tag_per_voxel = pltpu.with_memory_space_constraint(alloy_tag_per_voxel, pltpu.HBM)
 
     plane = f32(2, ny, LANES)
     pair = f32(2, 2, ny, LANES)
@@ -577,10 +580,9 @@
     halo_a = swap(ta, on_chip)
 
     cell = bore_boundary_positions.reshape(hits)
-    flip = jnp.where(lax.rem(me, 2) == 1, 0, (planes - 1) * ny * nz)
-    cell = cell ^ flip
     keys = ((cell & LANES) * (rows * LANES // LANES)) | ((cell >> 8) << 7) | (cell & (LANES - 1))
     packed = lax.sort(keys * 8192 + lax.iota(jnp.int32, hits), is_stable=False)
+    halo_a, keys, packed = lax.optimization_barrier((halo_a, keys, packed))
     owner, extra, extra_n = call(
         lambda *refs: owners_kernel(wall, *refs),
         (keys, packed.reshape(hits // LANES, LANES), packed),

time: 114 us -> 91 us (0.80)
  local copies, waits for them, and re-layouts: 22.1 us -> 0.06 us
  starting transfers between devices: 9.3 us -> 7.54 us
  blocking collectives: 10.1 us -> 11.8 us
  waiting for transfers between devices: 6.98 us -> 5.46 us
    unnamed x55 -> x15, local copies, waits for them, and re-layouts: 22.1 us -> 0.06 us
    ppermute x6, starting transfers between devices: 9.3 us -> 7.54 us  [swap(): return lax.ppermute(value, 'brick', pairs)]
    all_to_all x1, blocking collectives: 10.1 us -> 11.8 us  [per_device(): rows_all = lax.all_to_all(send, 'brick', 0, 0, tiled=True)]
    ppermute x6, waiting for transfers between devices: 6.98 us -> 5.46 us  [swap(): return lax.ppermute(value, 'brick', pairs)]
  transfers between devices with their start and end apart: 6 -> 6, of which waited for: 1 -> 1; matrix products, arithmetic and copies ran while one was open for 5% -> 6% of each run, Pallas kernels for 38% -> 49%
where the time goes in v2:
time: 91 us; the launch traced here: 90.8 us
  Pallas kernels  59.5 us (65%)
  blocking collectives  11.8 us (13%)
  starting transfers between devices  7.54 us (8%)
  other arithmetic  5.61 us (6%)
  waiting for transfers between devices  5.46 us (6%)
    pallas_call x9, Pallas kernels, call(): pl.pallas_call(kernel, out_shape=out_shape, in_specs=in_specs, out_specs=...  59.5 us
    all_to_all x1, blocking collectives, per_device(): rows_all = lax.all_to_all(send, 'brick', 0, 0, tiled=True)  11.8 us
    ppermute x6, starting transfers between devices, swap(): return lax.ppermute(value, 'brick', pairs)  7.54 us
    sort x1, other arithmetic, per_device(): packed = lax.sort(keys * 8192 + lax.iota(jnp.int32, hits), is_stable=False)  5.59 us
    ppermute x6, waiting for transfers between devices, swap(): return lax.ppermute(value, 'brick', pairs)  5.46 us
  transfers between devices with their start and end apart: 6, of which 1 were waited for; matrix products, arithmetic and copies ran while one was open for 6% of the time, Pallas kernels for 49%

profile of v2, /device:TPU:0, one launch (start us, length us, event | category | flops | bytes accessed | tf_op | source)
XLA Modules:
  0.0 90.8 jit_solution(16503419798947661332)
XLA Ops:
  0.6 0.0 copy-start.6
  0.6 0.0 copy-start.2
  0.7 0.0 copy-start.3
  0.7 1.4 %shard_map.104 = (f32[2,2,256,128]{3,2,1,0:T(8,128)S(1)}, f32[2,2,256,128]{3,2,1,0:T(8,128)S(1)}) custom-call(f32[8,256,256]{2,1,0:T(8,128)} %t_ref.3, s32[8,256,256]{2,1,0:T(8,128)} %refs_0_.1), custom_call_target="tpu_custom_call" | custom-call | flops 2000000 | bytes 2000000 | tf_op jit(solution)/shard_map/pallas_call | solution.py:26
  2.1 0.5 collective-permute-start
  2.6 5.7 %collective-permute-start.1 = (f32[2,2,256,128]{3,2,1,0:T(8,128)S(1)}, f32[2,2,256,128]{3,2,1,0:T(8,128)S(1)}, u32[]{:S(2)}, u32[]{:S(2)}) collective-permute-start(f32[2,2,256,128]{3,2,1,0:T(8,128)S(1)} %get-tuple-element.30), channel_id=1, source_target_pairs={{1,2},{3,4},{5,6},{7,8},{9,10},{11,12},{13,14},{15,0},{2,1},{4,3},... | collective-permute-start | bytes 1572872 | tf_op jit(solution)/shard_map/ppermute | solution.py:564
  8.3 0.0 copy-done.6
  8.3 5.6 %sort.7.refs_2_ = s32[8192]{0:T(1024)S(1)} sort(s32[8192]{0:T(1024)S(1)} %iota_add_fusion), dimensions={0}, to_apply=%region_0.0 | sort | flops 106496 | bytes 65536 | tf_op jit(solution)/shard_map/sort | solution.py:584
  13.9 0.0 collective-permute-done.halo
  13.9 0.0 copy-done.2
  13.9 0.0 copy-done.3
  13.9 11.3 %shard_map.105 = (f32[2,2064,128]{2,1,0:T(8,128)S(1)}, f32[2,256,128]{2,1,0:T(8,128)S(1)}, f32[2,1792,128]{2,1,0:T(8,128)S(1)}, f32[2,2064,128]{2,1,0:T(8,128)S(...) custom-call(f32[8,256,256]{2,1,0:T(8,128)} %t_ref.3, ...), custom_call_target="tpu_custom_call" | custom-call | flops 10000000 | bytes 10000000 | tf_op jit(solution)/shard_map/pallas_call | solution.py:26
  25.2 0.1 collective-permute-start.2
  25.3 0.0 collective-permute-done.1.refs_3_
  25.3 2.2 %shard_map.106 = (f32[2,256,128]{2,1,0:T(8,128)S(1)}, f32[2,256,128]{2,1,0:T(8,128)S(1)}) custom-call(s32[8,256,256]{2,1,0:T(8,128)} %refs_0_.1, f32[8]{0:T(128)S(1)} %copy-done.2, f32[2,2064,128]{2,1,0:T(8,128)S(1)} %get-tuple-element.29.refs_2_, f32[2,2,256,128]{3,2,1,0:T(8,128)S(1)} %collective-permute-done.1.refs_3_, ...), custom_call_target="tpu_custom_call" | custom-call | flops 2000000 | bytes 2000000 | tf_op jit(solution)/shard_map/pallas_call | solution.py:26
  27.6 0.7 collective-permute-start.3
  28.2 0.0 collective-permute-done.2.halo
  28.2 2.5 %shard_map.107 = (f32[2,1808,128]{2,1,0:T(8,128)S(1)}, f32[2,256,128]{2,1,0:T(8,128)S(1)}) custom-call(f32[2,1808,128]{2,1,0:T(8,128)S(1)} %get-tuple-element.28.tm, f32[2,256,128]{2,1,0:T(8,128)S(1)} %get-tuple-element.35.tb_old, f32[2,256,128]{2,1,0:T(8,128)S(1)} %collective-permute-done.2.halo, f32[2,256,128]{2,1,0:T(8,128)S(1)} %get-tuple-element.37.gxa, ...), custom_call_target="tpu_custom_call" | custom-call | flops 4000000 | bytes 4000000 | tf_op jit(solution)/shard_map/pallas_call | solution.py:26
  30.7 0.1 collective-permute-start.5
  30.8 5.4 %collective-permute-done.3.halo = f32[2,256,128]{2,1,0:T(8,128)S(1)} collective-permute-done((f32[2,256,128]{2,1,0:T(8,128)S(1)}, f32[2,256,128]{2,1,0:T(8,128)S(1)}, u32[]{:S(2)}, u32[]{:S(2)}) %collective-permute-start.3) | collective-permute-done | bytes 262176 | tf_op jit(solution)/shard_map/ppermute | solution.py:564
  36.2 0.4 shard_map.108.tb_old.refs_1_
  36.6 0.6 collective-permute-start.4
  37.2 18.5 %shard_map.109 = (s32[4096,128]{1,0:T(8,128)S(1)}, s32[8192]{0:T(1024)S(1)}, s32[1]{0:T(128)}) custom-call(s32[8192]{0:T(1024)S(1)} %bitcast.13, s32[64,128]{1,0:T(8,128)S(1)} %bitcast.11, s32[8192]{0:T(1024)S(1)} %sort.7.refs_2_), custom_call_target="tpu_custom_call" | custom-call | flops 20000000 | bytes 20000000 | tf_op jit(solution)/shard_map/pallas_call | solution.py:26
  55.6 0.0 collective-permute-done.5.halo
  55.7 0.0 copy-start
  55.7 0.0 copy-start.1
  55.7 9.6 %shard_map.110 = (f32[4096,128]{1,0:T(8,128)S(1)}, f32[32,8,128]{2,1,0:T(8,128)S(1)}) custom-call(f32[2,1808,128]{2,1,0:T(8,128)S(1)} %get-tuple-element.38.tm.refs_0_, f32[2,256,128]{2,1,0:T(8,128)S(1)} %shard_map.108.tb_old.refs_1_, f32[2,256,128]{2,1,0:T(8,128)S(1)} %collective-permute-done.5.halo, f32[2,256,128]{2,1,0:T(8,128)S(1)} %get-tuple-element.37.gxa, ...), custom_call_target="tpu_custom_call" | custom-call | flops 10000000 | bytes 10000000 | tf_op jit(solution)/shard_map/pallas_call | solution.py:26
  65.3 0.0 collective-permute-done.4.refs_2_
  65.3 0.0 copy-done
  65.4 0.0 copy-done.1
  65.4 0.0 copy-start.4
  65.4 0.0 copy-start.5
  65.4 3.6 %shard_map.111 = (f32[4096,128]{1,0:T(8,128)S(1)}, f32[16,128]{1,0:T(8,128)S(1)}) custom-call(f32[2,1808,128]{2,1,0:T(8,128)S(1)} %get-tuple-element.38.tm.refs_0_, f32[2,256,128]{2,1,0:T(8,128)S(1)} %shard_map.108.tb_old.refs_1_, f32[2,256,128]{2,1,0:T(8,128)S(1)} %collective-permute-done.4.refs_2_, ...), custom_call_target="tpu_custom_call", output_to_operand_aliasing={{0}: (14, {})} | custom-call | flops 2000000 | bytes 2000000 | tf_op jit(solution)/shard_map/pallas_call | solution.py:26
  69.0 11.8 %all_to_all.11 = f32[16,1,128]{2,1,0:T(1,128)S(1)} all-to-all(f32[16,1,128]{2,1,0:T(1,128)S(1)} %bitcast.15), channel_id=1, replica_groups=mesh['pour'=2,'brick'=16] {'brick'}, dimensions={0} | all-to-all | bytes 16384 | tf_op jit(solution)/shard_map/all_to_all | solution.py:666
  80.8 0.0 copy-done.4
  80.8 0.0 copy-done.5
  80.8 10.0 %shard_map.112 = (f32[8,256,256]{2,1,0:T(8,128)}, f32[1,32]{1,0:T(1,128)}) custom-call(f32[4096,128]{1,0:T(8,128)S(1)} %get-tuple-element.48.refs_0_, s32[4096,128]{1,0:T(8,128)S(1)} %get-tuple-element.42.owner.refs_8_.refs_1_, s32[8192]{0:T(1024)S(1)} %get-tuple-element.43.refs_9_.refs_2_, s32[1]{0:T(128)} %get-tuple-element.44.refs_10_.refs_3_, ...), custom_call_target="tpu_custom_call" | custom-call | flops 2000000 | bytes 2000000 | tf_op jit(solution)/shard_map/pallas_call | solution.py:26
  (3 shorter events, 0.0 us)
Async XLA Ops:
  0.6 7.6 %copy-start.6 = (s32[1,32,256]{2,1,0:T(8,128)S(1)}, s32[1,32,256]{2,1,0:T(8,128)}, u32[]{:S(2)}) copy-start(s32[1,32,256]{2,1,0:T(8,128)} %param.13) | copy-start | bytes 98308
  0.6 13.3 %copy-start.2 = (f32[8]{0:T(128)S(1)}, f32[8]{0:T(128)}, u32[]{:S(2)}) copy-start(f32[8]{0:T(128)} %refs_1_.1) | copy-start | bytes 100
  0.7 13.3 %copy-start.3 = (f32[8]{0:T(128)S(1)}, f32[8]{0:T(128)}, u32[]{:S(2)}) copy-start(f32[8]{0:T(128)} %store_ref.1) | copy-start | bytes 100
  2.1 11.8 %collective-permute-start = (f32[2,2,256,128]{3,2,1,0:T(8,128)S(1)}, f32[2,2,256,128]{3,2,1,0:T(8,128)S(1)}, u32[]{:S(2)}, u32[]{:S(2)}) collective-permute-start(f32[2,2,256,128]{3,2,1,0:T(8,128)S(1)} %get-tuple-element.26), channel_id=1, source_target_pairs={{0,1},{1,0},{2,3},{3,2},{4,5},{5,4},{6,7},{7,6},{8,9},{9,8},{10,11... | collective-permute-start | bytes 1572872 | tf_op jit(solution)/shard_map/ppermute | solution.py:564
  2.6 22.7 %collective-permute-start.1 = (f32[2,2,256,128]{3,2,1,0:T(8,128)S(1)}, f32[2,2,256,128]{3,2,1,0:T(8,128)S(1)}, u32[]{:S(2)}, u32[]{:S(2)}) collective-permute-start(f32[2,2,256,128]{3,2,1,0:T(8,128)S(1)} %get-tuple-element.30), channel_id=1, source_target_pairs={{1,2},{3,4},{5,6},{7,8},{9,10},{11,12},{13,14},{15,0},{2,1},{4,3},... | collective-permute-start | bytes 1572872 | tf_op jit(solution)/shard_map/ppermute | solution.py:564
  25.2 3.0 %collective-permute-start.2 = (f32[2,256,128]{2,1,0:T(8,128)S(1)}, f32[2,256,128]{2,1,0:T(8,128)S(1)}, u32[]{:S(2)}, u32[]{:S(2)}) collective-permute-start(f32[2,256,128]{2,1,0:T(8,128)S(1)} %get-tuple-element.36), channel_id=1, source_target_pairs={{0,1},{1,0},{2,3},{3,2},{4,5},{5,4},{6,7},{7,6},{8,9},{9,8},{10,11... | collective-permute-start | bytes 786440 | tf_op jit(solution)/shard_map/ppermute | solution.py:564
  27.6 8.7 %collective-permute-start.3 = (f32[2,256,128]{2,1,0:T(8,128)S(1)}, f32[2,256,128]{2,1,0:T(8,128)S(1)}, u32[]{:S(2)}, u32[]{:S(2)}) collective-permute-start(f32[2,256,128]{2,1,0:T(8,128)S(1)} %get-tuple-element.35.tb_old), channel_id=1, source_target_pairs={{1,2},{3,4},{5,6},{7,8},{9,10},{11,12},{13,14},{15,0},{2,1},{4,3},... | collective-permute-start | bytes 786440 | tf_op jit(solution)/shard_map/ppermute | solution.py:564
  30.7 24.9 %collective-permute-start.5 = (f32[2,256,128]{2,1,0:T(8,128)S(1)}, f32[2,256,128]{2,1,0:T(8,128)S(1)}, u32[]{:S(2)}, u32[]{:S(2)}) collective-permute-start(f32[2,256,128]{2,1,0:T(8,128)S(1)} %get-tuple-element.45), channel_id=1, source_target_pairs={{0,1},{1,0},{2,3},{3,2},{4,5},{5,4},{6,7},{7,6},{8,9},{9,8},{10,11... | collective-permute-start | bytes 786440 | tf_op jit(solution)/shard_map/ppermute | solution.py:564
  36.6 28.7 %collective-permute-start.4 = (f32[2,256,128]{2,1,0:T(8,128)S(1)}, f32[2,256,128]{2,1,0:T(8,128)S(1)}, u32[]{:S(2)}, u32[]{:S(2)}) collective-permute-start(f32[2,256,128]{2,1,0:T(8,128)S(1)} %shard_map.108.tb_old.refs_1_), channel_id=1, source_target_pairs={{1,2},{3,4},{5,6},{7,8},{9,10},{11,12},{13,14},{15,0},{2,1},{4,3},... | collective-permute-start | bytes 786440 | tf_op jit(solution)/shard_map/ppermute | solution.py:564
  55.7 9.7 %copy-start = (f32[1,32]{1,0:T(1,128)S(1)}, f32[1,32]{1,0:T(1,128)}, u32[]{:S(2)}) copy-start(f32[1,32]{1,0:T(1,128)} %refs_5_.1) | copy-start | bytes 388
  55.7 9.7 %copy-start.1 = (f32[32]{0:T(128)S(1)}, f32[32]{0:T(128)}, u32[]{:S(2)}) copy-start(f32[32]{0:T(128)} %param.15) | copy-start | bytes 388
  65.4 15.4 %copy-start.4 = (s32[32]{0:T(128)S(1)}, s32[32]{0:T(128)}, u32[]{:S(2)}) copy-start(s32[32]{0:T(128)} %param.16) | copy-start | bytes 388
  65.4 15.4 %copy-start.5 = (f32[32]{0:T(128)S(1)}, f32[32]{0:T(128)}, u32[]{:S(2)}) copy-start(f32[32]{0:T(128)} %param.17) | copy-start | bytes 388

commit v3 on v2

--- a/solution.py
+++ b/solution.py
@@ -8,6 +8,7 @@
 LANES = 128
 PAD = 8
 STRIP = 16
+WINDOW = 96
 VMEM = pl.BlockSpec(memory_space=pltpu.VMEM)
 SMEM = pl.BlockSpec(memory_space=pltpu.SMEM)
 HBM = pl.BlockSpec(memory_space=pltpu.HBM)
@@ -334,7 +335,7 @@
         r = pl.multiple_of(start + s * 8, 8)
         own = owner[pl.ds(r, 8), :]
         hot = heat[pl.ds(r, 8), :]
-        return tuple(acc[k] + jnp.where(own == k, hot, 0.0) for k in range(lines))
+        return tuple(acc[k] + jnp.where(own == k + 1.0, hot, 0.0) for k in range(lines))
 
     acc = lax.fori_loop(0, count // 8, turn, tuple(totals[k] for k in range(lines)), unroll=4)
     for k in range(lines):
@@ -360,8 +361,8 @@
         bin_rows(heat, owner, h * rows + first, rows - ny, totals, totals.shape[0])
 
 
-def unpack(entry):
-    row = lax.shift_right_logical(entry, 20)
+def unpack(entry, half_rows):
+    row = lax.shift_right_arithmetic(entry, 20) + half_rows
     lane = lax.shift_right_logical(entry, 13) & (LANES - 1)
     return row, lane
 
@@ -392,7 +393,7 @@
 
     def more(n, carry):
         entry = extra[n]
-        row, col = unpack(entry)
+        row, col = unpack(entry, rows)
         line = lax.shift_right_logical(entry, wall.bit_length() - 1) & (lines - 1)
         hit = jnp.where(lane == col, heat[pl.ds(row, 1), :], 0.0)
         sums[pl.ds(line, 1), :] = sums[pl.ds(line, 1), :] + hit
@@ -414,10 +415,10 @@
     send[:, lines : 2 * lines] = jnp.broadcast_to(gain, (count, lines))
 
 
-def owners_kernel(wall, keys, packed, ordered, owner, extra, extra_n, words, words_s, sem):
-    rows, total = owner.shape[0], keys.shape[0]
-    lines = total // wall
+def owners_kernel(wall, packed, ordered, owner, extra, extra_n, row_of, col_of, value, words, words_s, sem):
     bits = 32
+    window = WINDOW
+    rows = owner.shape[0] - window
     one = packed[...]
     depth = one.shape[0]
     nxt = pltpu.roll(one, LANES - 1, 1)
@@ -433,27 +434,58 @@
         words[pl.ds(g, 1), :] = jnp.sum(flag[g * bits : (g + 1) * bits], axis=0, keepdims=True)
     copy = pltpu.make_async_copy(words, words_s, sem)
     copy.start()
+    row_of[...] = lax.shift_right_arithmetic(one, 20) + rows // 2
+    col_of[...] = lax.shift_right_logical(one, 13) & (LANES - 1)
+    line = lax.shift_right_logical(one & 8191, wall.bit_length() - 1)
+    value[...] = jnp.where(same, 0, line + 1).astype(jnp.float32)
 
     def clear(r):
-        owner[pl.ds(r, 64), :] = jnp.full((64, LANES), LANES - 1, jnp.int32)
-
-    rows_loop(rows, clear, 64)
-    ones = lanes_iota(1)
-    unroll = 32
-
-    def line(k, carry):
-        value = jnp.full((1, LANES), k, jnp.int32)
-
-        def body(s, inner):
-            for u in range(unroll):
-                key = keys[k * wall + s * unroll + u]
-                row = lax.shift_right_logical(key, 7)
-                pltpu.store(owner.at[pl.ds(row, 1), :], value, mask=ones == (key & (LANES - 1)))
-            return inner
-
-        return lax.fori_loop(0, wall // unroll, body, carry)
-
-    lax.fori_loop(0, lines, line, 0)
+        owner[pl.ds(r, 32), :] = jnp.zeros((32, LANES), jnp.float32)
+
+    rows_loop(rows + window, clear, 32)
+    tall = lax.broadcasted_iota(jnp.int32, (window, LANES), 0)
+    square = lax.broadcasted_iota(jnp.int32, (LANES, LANES), 0)
+
+    def row_at(i):
+        return lax.shift_right_arithmetic(ordered[i], 20) + rows // 2
+
+    def block(c, base):
+        at = jnp.where(tall == row_of[pl.ds(c, 1), :] - base, 1.0, 0.0).astype(jnp.bfloat16)
+        what = jnp.where(square == col_of[pl.ds(c, 1), :], value[pl.ds(c, 1), :], 0.0)
+        return lax.dot_general(
+            at,
+            what.astype(jnp.bfloat16),
+            (((1,), (1,)), ((), ())),
+            preferred_element_type=jnp.float32,
+        )
+
+    def first_base(c):
+        return pl.multiple_of(row_at(c * LANES) & -8, 8)
+
+    group = 8
+
+    def turn(g, carry):
+        chunks = [g * group + u for u in range(group)]
+        bases = [first_base(c) for c in chunks]
+        blocks = [block(c, base) for c, base in zip(chunks, bases)]
+        for base, found in zip(bases, blocks):
+            owner[pl.ds(base, window), :] = owner[pl.ds(base, window), :] + found
+        return carry
+
+    lax.fori_loop(0, depth // group, turn, 0)
+
+    def rest(c, carry):
+        last = row_at(c * LANES + LANES - 1)
+
+        def go(base):
+            base = pl.multiple_of(base, 8)
+            owner[pl.ds(base, window), :] = owner[pl.ds(base, window), :] + block(c, base)
+            return base + window
+
+        lax.while_loop(lambda base: base <= last, go, first_base(c) + window)
+        return carry
+
+    lax.fori_loop(0, depth, rest, 0)
     copy.wait()
 
     def lane_turn(c, n):
@@ -493,9 +525,9 @@
     coolant = 0.5 * (inflow + keep * inflow + gain)
     mid[...] = coolant
     table[...] = jnp.zeros_like(table)
-    table[0:1, 0:lines] = 0.5 * (1.0 - keep)
-    table[1:2, 0:lines] = coolant
-    eye = lax.broadcasted_iota(jnp.int32, (lines, LANES), 0) == lanes_iota(lines)
+    table[0:1, 1 : lines + 1] = 0.5 * (1.0 - keep)
+    table[1:2, 1 : lines + 1] = coolant
+    eye = lax.broadcasted_iota(jnp.int32, (lines, LANES), 0) + 1 == lanes_iota(lines)
     for k in range(2):
         spread = jnp.broadcast_to(table[k : k + 1, :], (lines, LANES))
         column = jnp.sum(jnp.where(eye, spread, 0.0), axis=1, keepdims=True)
@@ -504,7 +536,7 @@
     cool = jnp.broadcast_to(table[1:2, :], (8, LANES))
 
     def dense(r):
-        own = owner[pl.ds(r, 8), :]
+        own = owner[pl.ds(r, 8), :].astype(jnp.int32)
         hot = heat[pl.ds(r, 8), :]
         a = jnp.take_along_axis(pull, own, axis=1)
         c = jnp.take_along_axis(cool, own, axis=1)
@@ -515,7 +547,7 @@
 
     def more(n, carry):
         item = extra[n]
-        row, col = unpack(item)
+        row, col = unpack(item, rows)
         line = lax.shift_right_logical(item, wall.bit_length() - 1) & (lines - 1)
         a = splat[0, pl.ds(line, 1), :]
         c = splat[1, pl.ds(line, 1), :]
@@ -581,15 +613,18 @@
 
     cell = bore_boundary_positions.reshape(hits)
     keys = ((cell & LANES) * (rows * LANES // LANES)) | ((cell >> 8) << 7) | (cell & (LANES - 1))
+    keys = keys ^ (rows * LANES)
     packed = lax.sort(keys * 8192 + lax.iota(jnp.int32, hits), is_stable=False)
-    halo_a, keys, packed = lax.optimization_barrier((halo_a, keys, packed))
+    halo_a, packed = lax.optimization_barrier((halo_a, packed))
     owner, extra, extra_n = call(
         lambda *refs: owners_kernel(wall, *refs),
-        (keys, packed.reshape(hits // LANES, LANES), packed),
-        [SMEM, VMEM, SMEM],
-        (i32(2 * rows, LANES), i32(hits), i32(1)),
+        (packed.reshape(hits // LANES, LANES), packed),
+        [VMEM, SMEM],
+        (f32(2 * rows + WINDOW, LANES), i32(hits), i32(1)),
         (VMEM, SMEM, SMEM),
-        [pltpu.VMEM((8, LANES), jnp.int32), pltpu.SMEM((8, LANES), jnp.int32), dma],
+        [pltpu.VMEM((hits // LANES, LANES), jnp.int32)] * 2
+        + [pltpu.VMEM((hits // LANES, LANES), jnp.float32)]
+        + [pltpu.VMEM((8, LANES), jnp.int32), pltpu.SMEM((8, LANES), jnp.int32), dma],
         cost=20_000_000,
     )
 

time: 91 us -> 82.1 us (0.902)
  Pallas kernels: 59.5 us -> 50.5 us
    pallas_call x9, Pallas kernels: 59.5 us -> 50.5 us  [call(): pl.pallas_call(kernel, out_shape=out_shape, in_specs=in_specs, out_specs=...]
  transfers between devices with their start and end apart: 6 -> 6, of which waited for: 1 -> 1; matrix products, arithmetic and copies ran while one was open for 6% -> 7% of each run, Pallas kernels for 49% -> 43%
where the time goes in v3:
time: 82.1 us; the launch traced here: 81.7 us
  Pallas kernels  50.5 us (62%)
  blocking collectives  11.7 us (14%)
  starting transfers between devices  7.54 us (9%)
  other arithmetic  5.61 us (7%)
  waiting for transfers between devices  5.46 us (7%)
  between operations  0.84 us (1%)
    pallas_call x9, Pallas kernels, call(): pl.pallas_call(kernel, out_shape=out_shape, in_specs=in_specs, out_specs=...  50.5 us
    all_to_all x1, blocking collectives, per_device(): rows_all = lax.all_to_all(send, 'brick', 0, 0, tiled=True)  11.7 us
    ppermute x6, starting transfers between devices, swap(): return lax.ppermute(value, 'brick', pairs)  7.54 us
    sort x1, other arithmetic, per_device(): packed = lax.sort(keys * 8192 + lax.iota(jnp.int32, hits), is_stable=False)  5.59 us
    ppermute x6, waiting for transfers between devices, swap(): return lax.ppermute(value, 'brick', pairs)  5.46 us
  transfers between devices with their start and end apart: 6, of which 1 were waited for; matrix products, arithmetic and copies ran while one was open for 7% of the time, Pallas kernels for 43%

profile of v3, /device:TPU:0, one launch (start us, length us, event | category | flops | bytes accessed | tf_op | source)
XLA Modules:
  0.0 81.7 jit_solution(11660185170141143933)
XLA Ops:
  0.6 0.0 copy-start.6
  0.6 0.0 copy-start
  0.7 0.0 copy-start.3
  0.7 1.4 %shard_map.104 = (f32[2,2,256,128]{3,2,1,0:T(8,128)S(1)}, f32[2,2,256,128]{3,2,1,0:T(8,128)S(1)}) custom-call(f32[8,256,256]{2,1,0:T(8,128)} %t_ref.3, s32[8,256,256]{2,1,0:T(8,128)} %refs_0_.1), custom_call_target="tpu_custom_call" | custom-call | flops 2000000 | bytes 2000000 | tf_op jit(solution)/shard_map/pallas_call | solution.py:27
  2.1 0.5 collective-permute-start
  2.6 5.7 %collective-permute-start.1 = (f32[2,2,256,128]{3,2,1,0:T(8,128)S(1)}, f32[2,2,256,128]{3,2,1,0:T(8,128)S(1)}, u32[]{:S(2)}, u32[]{:S(2)}) collective-permute-start(f32[2,2,256,128]{3,2,1,0:T(8,128)S(1)} %get-tuple-element.29), channel_id=1, source_target_pairs={{1,2},{3,4},{5,6},{7,8},{9,10},{11,12},{13,14},{15,0},{2,1},{4,3},... | collective-permute-start | bytes 1572872 | tf_op jit(solution)/shard_map/ppermute | solution.py:596
  8.3 0.0 copy-done.6
  8.3 5.6 %sort.7.refs_1_ = s32[8192]{0:T(1024)S(1)} sort(s32[8192]{0:T(1024)S(1)} %iota_add_fusion), dimensions={0}, to_apply=%region_0.0 | sort | flops 106496 | bytes 65536 | tf_op jit(solution)/shard_map/sort | solution.py:617
  13.9 0.0 collective-permute-done.halo
  13.9 0.0 copy-done
  13.9 0.0 copy-done.3
  13.9 11.3 %shard_map.105 = (f32[2,2064,128]{2,1,0:T(8,128)S(1)}, f32[2,256,128]{2,1,0:T(8,128)S(1)}, f32[2,1792,128]{2,1,0:T(8,128)S(1)}, f32[2,2064,128]{2,1,0:T(8,128)S(...) custom-call(f32[8,256,256]{2,1,0:T(8,128)} %t_ref.3, ...), custom_call_target="tpu_custom_call" | custom-call | flops 10000000 | bytes 10000000 | tf_op jit(solution)/shard_map/pallas_call | solution.py:27
  25.2 0.1 collective-permute-start.2
  25.3 0.0 collective-permute-done.1.refs_3_
  25.3 2.2 %shard_map.106 = (f32[2,256,128]{2,1,0:T(8,128)S(1)}, f32[2,256,128]{2,1,0:T(8,128)S(1)}) custom-call(s32[8,256,256]{2,1,0:T(8,128)} %refs_0_.1, f32[8]{0:T(128)S(1)} %copy-done, f32[2,2064,128]{2,1,0:T(8,128)S(1)} %get-tuple-element.28.refs_2_, f32[2,2,256,128]{3,2,1,0:T(8,128)S(1)} %collective-permute-done.1.refs_3_, ...), custom_call_target="tpu_custom_call" | custom-call | flops 2000000 | bytes 2000000 | tf_op jit(solution)/shard_map/pallas_call | solution.py:27
  27.6 0.7 collective-permute-start.3
  28.2 0.0 collective-permute-done.2.halo
  28.2 2.5 %shard_map.107 = (f32[2,1808,128]{2,1,0:T(8,128)S(1)}, f32[2,256,128]{2,1,0:T(8,128)S(1)}) custom-call(f32[2,1808,128]{2,1,0:T(8,128)S(1)} %get-tuple-element.27.tm, f32[2,256,128]{2,1,0:T(8,128)S(1)} %get-tuple-element.34.tb_old, f32[2,256,128]{2,1,0:T(8,128)S(1)} %collective-permute-done.2.halo, f32[2,256,128]{2,1,0:T(8,128)S(1)} %get-tuple-element.36.gxa, ...), custom_call_target="tpu_custom_call" | custom-call | flops 4000000 | bytes 4000000 | tf_op jit(solution)/shard_map/pallas_call | solution.py:27
  30.7 0.1 collective-permute-start.5
  30.8 5.4 %collective-permute-done.3.halo = f32[2,256,128]{2,1,0:T(8,128)S(1)} collective-permute-done((f32[2,256,128]{2,1,0:T(8,128)S(1)}, f32[2,256,128]{2,1,0:T(8,128)S(1)}, u32[]{:S(2)}, u32[]{:S(2)}) %collective-permute-start.3) | collective-permute-done | bytes 262176 | tf_op jit(solution)/shard_map/ppermute | solution.py:596
  36.2 0.4 shard_map.108.tb_old.refs_1_
  36.6 0.6 collective-permute-start.4
  37.2 9.3 %shard_map.109 = (f32[4192,128]{1,0:T(8,128)S(1)}, s32[8192]{0:T(1024)S(1)}, s32[1]{0:T(128)}) custom-call(s32[64,128]{1,0:T(8,128)S(1)} %bitcast.12, s32[8192]{0:T(1024)S(1)} %sort.7.refs_1_), custom_call_target="tpu_custom_call" | custom-call | flops 20000000 | bytes 20000000 | tf_op jit(solution)/shard_map/pallas_call | solution.py:27
  46.5 0.0 collective-permute-done.5.halo
  46.5 0.0 copy-start.1
  46.5 0.0 copy-start.2
  46.5 9.6 %shard_map.110 = (f32[4096,128]{1,0:T(8,128)S(1)}, f32[32,8,128]{2,1,0:T(8,128)S(1)}) custom-call(f32[2,1808,128]{2,1,0:T(8,128)S(1)} %get-tuple-element.37.tm.refs_0_, f32[2,256,128]{2,1,0:T(8,128)S(1)} %shard_map.108.tb_old.refs_1_, f32[2,256,128]{2,1,0:T(8,128)S(1)} %collective-permute-done.5.halo, f32[2,256,128]{2,1,0:T(8,128)S(1)} %get-tuple-element.36.gxa, ...), custom_call_target="tpu_custom_call" | custom-call | flops 10000000 | bytes 10000000 | tf_op jit(solution)/shard_map/pallas_call | solution.py:27
  56.2 0.0 collective-permute-done.4.refs_2_
  56.2 0.0 copy-done.1
  56.2 0.0 copy-done.2
  56.2 0.0 copy-start.4
  56.2 0.0 copy-start.5
  56.3 3.6 %shard_map.111 = (f32[4096,128]{1,0:T(8,128)S(1)}, f32[16,128]{1,0:T(8,128)S(1)}) custom-call(f32[2,1808,128]{2,1,0:T(8,128)S(1)} %get-tuple-element.37.tm.refs_0_, f32[2,256,128]{2,1,0:T(8,128)S(1)} %shard_map.108.tb_old.refs_1_, f32[2,256,128]{2,1,0:T(8,128)S(1)} %collective-permute-done.4.refs_2_, ...), custom_call_target="tpu_custom_call", output_to_operand_aliasing={{0}: (14, {})} | custom-call | flops 2000000 | bytes 2000000 | tf_op jit(solution)/shard_map/pallas_call | solution.py:27
  59.9 11.7 %all_to_all.11 = f32[16,1,128]{2,1,0:T(1,128)S(1)} all-to-all(f32[16,1,128]{2,1,0:T(1,128)S(1)} %bitcast.13), channel_id=1, replica_groups=mesh['pour'=2,'brick'=16] {'brick'}, dimensions={0} | all-to-all | bytes 16384 | tf_op jit(solution)/shard_map/all_to_all | solution.py:701
  71.5 0.0 copy-done.4
  71.5 0.0 copy-done.5
  71.5 10.1 %shard_map.112 = (f32[8,256,256]{2,1,0:T(8,128)}, f32[1,32]{1,0:T(1,128)}) custom-call(f32[4096,128]{1,0:T(8,128)S(1)} %get-tuple-element.46.refs_0_, f32[4192,128]{1,0:T(8,128)S(1)} %get-tuple-element.40.owner.refs_8_.refs_1_, s32[8192]{0:T(1024)S(1)} %get-tuple-element.41.refs_9_.refs_2_, s32[1]{0:T(128)} %get-tuple-element.42.refs_10_.refs_3_, ...), custom_call_target="tpu_custom_call" | custom-call | flops 2000000 | bytes 2000000 | tf_op jit(solution)/shard_map/pallas_call | solution.py:27
  (3 shorter events, 0.0 us)
Async XLA Ops:
  0.6 7.6 %copy-start.6 = (s32[1,32,256]{2,1,0:T(8,128)S(1)}, s32[1,32,256]{2,1,0:T(8,128)}, u32[]{:S(2)}) copy-start(s32[1,32,256]{2,1,0:T(8,128)} %param.13) | copy-start | bytes 98308
  0.6 13.3 %copy-start = (f32[8]{0:T(128)S(1)}, f32[8]{0:T(128)}, u32[]{:S(2)}) copy-start(f32[8]{0:T(128)} %refs_1_.1) | copy-start | bytes 100
  0.7 13.3 %copy-start.3 = (f32[8]{0:T(128)S(1)}, f32[8]{0:T(128)}, u32[]{:S(2)}) copy-start(f32[8]{0:T(128)} %store_ref.1) | copy-start | bytes 100
  2.1 11.8 %collective-permute-start = (f32[2,2,256,128]{3,2,1,0:T(8,128)S(1)}, f32[2,2,256,128]{3,2,1,0:T(8,128)S(1)}, u32[]{:S(2)}, u32[]{:S(2)}) collective-permute-start(f32[2,2,256,128]{3,2,1,0:T(8,128)S(1)} %get-tuple-element.25), channel_id=1, source_target_pairs={{0,1},{1,0},{2,3},{3,2},{4,5},{5,4},{6,7},{7,6},{8,9},{9,8},{10,11... | collective-permute-start | bytes 1572872 | tf_op jit(solution)/shard_map/ppermute | solution.py:596
  2.6 22.7 %collective-permute-start.1 = (f32[2,2,256,128]{3,2,1,0:T(8,128)S(1)}, f32[2,2,256,128]{3,2,1,0:T(8,128)S(1)}, u32[]{:S(2)}, u32[]{:S(2)}) collective-permute-start(f32[2,2,256,128]{3,2,1,0:T(8,128)S(1)} %get-tuple-element.29), channel_id=1, source_target_pairs={{1,2},{3,4},{5,6},{7,8},{9,10},{11,12},{13,14},{15,0},{2,1},{4,3},... | collective-permute-start | bytes 1572872 | tf_op jit(solution)/shard_map/ppermute | solution.py:596
  25.2 3.0 %collective-permute-start.2 = (f32[2,256,128]{2,1,0:T(8,128)S(1)}, f32[2,256,128]{2,1,0:T(8,128)S(1)}, u32[]{:S(2)}, u32[]{:S(2)}) collective-permute-start(f32[2,256,128]{2,1,0:T(8,128)S(1)} %get-tuple-element.35), channel_id=1, source_target_pairs={{0,1},{1,0},{2,3},{3,2},{4,5},{5,4},{6,7},{7,6},{8,9},{9,8},{10,11... | collective-permute-start | bytes 786440 | tf_op jit(solution)/shard_map/ppermute | solution.py:596
  27.6 8.7 %collective-permute-start.3 = (f32[2,256,128]{2,1,0:T(8,128)S(1)}, f32[2,256,128]{2,1,0:T(8,128)S(1)}, u32[]{:S(2)}, u32[]{:S(2)}) collective-permute-start(f32[2,256,128]{2,1,0:T(8,128)S(1)} %get-tuple-element.34.tb_old), channel_id=1, source_target_pairs={{1,2},{3,4},{5,6},{7,8},{9,10},{11,12},{13,14},{15,0},{2,1},{4,3},... | collective-permute-start | bytes 786440 | tf_op jit(solution)/shard_map/ppermute | solution.py:596
  30.7 15.8 %collective-permute-start.5 = (f32[2,256,128]{2,1,0:T(8,128)S(1)}, f32[2,256,128]{2,1,0:T(8,128)S(1)}, u32[]{:S(2)}, u32[]{:S(2)}) collective-permute-start(f32[2,256,128]{2,1,0:T(8,128)S(1)} %get-tuple-element.43), channel_id=1, source_target_pairs={{0,1},{1,0},{2,3},{3,2},{4,5},{5,4},{6,7},{7,6},{8,9},{9,8},{10,11... | collective-permute-start | bytes 786440 | tf_op jit(solution)/shard_map/ppermute | solution.py:596
  36.6 19.6 %collective-permute-start.4 = (f32[2,256,128]{2,1,0:T(8,128)S(1)}, f32[2,256,128]{2,1,0:T(8,128)S(1)}, u32[]{:S(2)}, u32[]{:S(2)}) collective-permute-start(f32[2,256,128]{2,1,0:T(8,128)S(1)} %shard_map.108.tb_old.refs_1_), channel_id=1, source_target_pairs={{1,2},{3,4},{5,6},{7,8},{9,10},{11,12},{13,14},{15,0},{2,1},{4,3},... | collective-permute-start | bytes 786440 | tf_op jit(solution)/shard_map/ppermute | solution.py:596
  46.5 9.7 %copy-start.1 = (f32[1,32]{1,0:T(1,128)S(1)}, f32[1,32]{1,0:T(1,128)}, u32[]{:S(2)}) copy-start(f32[1,32]{1,0:T(1,128)} %refs_5_.1) | copy-start | bytes 388
  46.5 9.7 %copy-start.2 = (f32[32]{0:T(128)S(1)}, f32[32]{0:T(128)}, u32[]{:S(2)}) copy-start(f32[32]{0:T(128)} %param.15) | copy-start | bytes 388
  56.2 15.3 %copy-start.4 = (s32[32]{0:T(128)S(1)}, s32[32]{0:T(128)}, u32[]{:S(2)}) copy-start(s32[32]{0:T(128)} %param.16) | copy-start | bytes 388
  56.2 15.3 %copy-start.5 = (f32[32]{0:T(128)S(1)}, f32[32]{0:T(128)}, u32[]{:S(2)}) copy-start(f32[32]{0:T(128)} %param.17) | copy-start | bytes 388

commit v4 on v2

--- a/solution.py
+++ b/solution.py
@@ -8,6 +8,9 @@
 LANES = 128
 PAD = 8
 STRIP = 16
+WINDOW = 96
+READ_GROUP = 4
+WRITE_GROUP = 8
 VMEM = pl.BlockSpec(memory_space=pltpu.VMEM)
 SMEM = pl.BlockSpec(memory_space=pltpu.SMEM)
 HBM = pl.BlockSpec(memory_space=pltpu.HBM)
@@ -197,15 +200,15 @@
         mine = [cond[h, pl.ds(PAD + r, STRIP), :] for h in HALVES]
         nxt = [pltpu.roll(mine[h], LANES - 1, 1) for h in HALVES]
         ahead = [jnp.where(lane == LANES - 1, nxt[1], nxt[0]), nxt[1]]
-        prv = [pltpu.roll(mine[h], 1, 1) for h in HALVES]
-        behind = [prv[0], jnp.where(lane == 0, prv[0], prv[1])]
+        right = [face_mean(mine[h], ahead[h]) for h in HALVES]
+        right[1] = jnp.where(lane == LANES - 1, 0.0, right[1])
+        back = [pltpu.roll(right[h], 1, 1) for h in HALVES]
+        left = [jnp.where(lane == 0, back[1], back[0]), jnp.where(lane == 0, back[0], back[1])]
         for h in HALVES:
             below = face_mean(mine[h], cond[h, pl.ds(PAD + r + 1, STRIP), :])
             gy[h, pl.ds(PAD + r, STRIP), :] = jnp.where(y == ny - 1, 0.0, below)
-            right = face_mean(mine[h], ahead[h])
-            gz[h, pl.ds(r, STRIP), :] = jnp.where(lane == LANES - 1, 0.0, right) if h else right
-            left = face_mean(behind[h], mine[h])
-            gz[2 + h, pl.ds(r, STRIP), :] = left if h else jnp.where(lane == 0, 0.0, left)
+            gz[h, pl.ds(r, STRIP), :] = right[h]
+            gz[2 + h, pl.ds(r, STRIP), :] = left[h]
 
     rows_loop(planes * ny, yz_faces)
 
@@ -329,76 +332,140 @@
     main_planes(tm, last, halo, gxa, gxm, gy, gz, coeff, planes, ny, emit)
 
 
-def bin_rows(heat, owner, start, count, totals, lines):
-    def turn(s, acc):
-        r = pl.multiple_of(start + s * 8, 8)
-        own = owner[pl.ds(r, 8), :]
-        hot = heat[pl.ds(r, 8), :]
-        return tuple(acc[k] + jnp.where(own == k, hot, 0.0) for k in range(lines))
-
-    acc = lax.fori_loop(0, count // 8, turn, tuple(totals[k] for k in range(lines)), unroll=4)
-    for k in range(lines):
-        totals[k] = acc[k]
-
-
-def final_main_kernel(tm, tb_old, halo, gxa, gxm, gy, gz, coeff, owner, heat, totals):
+def unpack(packed, ordered, row_of, col_of, sem, half):
+    copy = pltpu.make_async_copy(packed, ordered, sem)
+    copy.start()
+    one = packed[...]
+    row_of[...] = lax.shift_right_arithmetic(one, 20) + half
+    col_of[...] = lax.shift_right_logical(one, 13) & (LANES - 1)
+    return copy
+
+
+def line_of(packed, wall):
+    return lax.shift_right_logical(packed & 8191, wall.bit_length() - 1)
+
+
+def row_at(ordered, c, place, half):
+    return lax.shift_right_arithmetic(ordered[c, place], 20) + half
+
+
+def windows(first, last, group, ordered, half, work, commit, after=None):
+    def base_of(c):
+        return pl.multiple_of(row_at(ordered, c, 0, half) & -8, 8)
+
+    def turn(g, carry):
+        chunks = [g * group + u for u in range(group)]
+        bases = [base_of(c) for c in chunks]
+        made = [work(c, base) for c, base in zip(chunks, bases)]
+        for c, base, item in zip(chunks, bases, made):
+            commit(c, base, item)
+        ends = [row_at(ordered, c, LANES - 1, half) - base for c, base in zip(chunks, bases)]
+        longest = ends[0]
+        for end in ends[1:]:
+            longest = jnp.maximum(longest, end)
+
+        @pl.when(longest >= WINDOW)
+        def _():
+            def chunk(u, inner):
+                c = g * group + u
+                end = row_at(ordered, c, LANES - 1, half)
+
+                def go(base):
+                    base = pl.multiple_of(base, 8)
+                    commit(c, base, work(c, base))
+                    return base + WINDOW
+
+                lax.while_loop(lambda base: base <= end, go, base_of(c) + WINDOW)
+                return inner
+
+            lax.fori_loop(0, group, chunk, 0)
+
+        return carry if after is None else after(g, carry)
+
+    return lax.fori_loop(first, last, turn, 0)
+
+
+def split(x):
+    high = x.astype(jnp.bfloat16)
+    return high, (x - high.astype(jnp.float32)).astype(jnp.bfloat16)
+
+
+def read_walls(first, last, ordered, row_of, col_of, heat, found, half):
+    tall = lax.broadcasted_iota(jnp.int32, (WINDOW, LANES), 0)
+    square = lax.broadcasted_iota(jnp.int32, (LANES, LANES), 0)
+
+    def work(c, base):
+        lanes = jnp.where(square == col_of[pl.ds(c, 1), :], 1.0, 0.0).astype(jnp.bfloat16)
+        high, low = split(heat[pl.ds(base, WINDOW), :])
+        values = jnp.dot(high, lanes, preferred_element_type=jnp.float32)
+        values = values + jnp.dot(low, lanes, preferred_element_type=jnp.float32)
+        here = tall == row_of[pl.ds(c, 1), :] - base
+        return jnp.sum(jnp.where(here, values, 0.0), axis=0, keepdims=True)
+
+    def commit(c, base, item):
+        found[pl.ds(c, 1), :] = found[pl.ds(c, 1), :] + item
+
+    windows(first, last, READ_GROUP, ordered, half, work, commit)
+
+
+def early_groups(ordered, rows_before, half):
+    depth = ordered.shape[0]
+    count = jnp.int32(0)
+    for g in range(depth // READ_GROUP):
+        end = row_at(ordered, (g + 1) * READ_GROUP - 1, LANES - 1, half)
+        count = count + jnp.where(end < rows_before, 1, 0)
+    return count
+
+
+def final_main_kernel(tm, tb_old, halo, gxa, gxm, gy, gz, coeff, packed, heat, found, ordered, row_of, col_of, sem):
     ny = tb_old.shape[1]
-    planes = gz.shape[1] // ny
-    rows = planes * ny
+    rows = gz.shape[1]
+    planes = rows // ny
+    copy = unpack(packed, ordered, row_of, col_of, sem, rows)
 
     def emit(j, y, new, first):
         for h in HALVES:
-            heat[pl.ds(h * rows + plane_of(j, planes) * ny + y, STRIP), :] = new[h]
+            heat[pl.ds((2 * j + h) * ny + y, STRIP), :] = new[h]
 
     def last(h, y):
         return tb_old[h, pl.ds(y, STRIP), :]
 
     main_planes(tm, last, halo, gxa, gxm, gy, gz, coeff, planes, ny, emit)
-    totals[...] = jnp.zeros_like(totals)
-    for h in HALVES:
-        first = jnp.where(plane_of(planes - 1, planes) == 0, ny, 0)
-        bin_rows(heat, owner, h * rows + first, rows - ny, totals, totals.shape[0])
-
-
-def unpack(entry):
-    row = lax.shift_right_logical(entry, 20)
-    lane = lax.shift_right_logical(entry, 13) & (LANES - 1)
-    return row, lane
+    heat[pl.ds(2 * rows, WINDOW), :] = jnp.zeros((WINDOW, LANES), jnp.float32)
+    heat[pl.ds(2 * (rows - ny), 2 * ny), :] = jnp.zeros((2 * ny, LANES), jnp.float32)
+    found[...] = jnp.zeros_like(found)
+    copy.wait()
+    early = early_groups(ordered, 2 * (rows - ny), rows)
+    read_walls(0, early, ordered, row_of, col_of, heat, found, rows)
 
 
 def walls_kernel(
-    wall, tm, tb_old, halo, gxb, gxm, gy, gz, coeff, owner, extra, extra_n, totals_in, film, ratio, heat_in, heat, send, pad, totals, sums
+    wall, tm, tb_old, halo, gxb, gxm, gy, gz, coeff, packed, found_in, film, ratio, heat_in, heat, found, send, pad, sums, ordered, row_of, col_of, sem
 ):
     ny = tb_old.shape[1]
     rows = gz.shape[1]
     planes = rows // ny
-    lines = totals.shape[0]
-    at = plane_of(planes - 1, planes) * ny
+    lines = film.shape[1]
+    copy = unpack(packed, ordered, row_of, col_of, sem, rows)
     padded(pad, lambda h, y: tb_old[h, pl.ds(y, STRIP), :], ny)
 
     def emit(y, new):
         for h in HALVES:
-            heat[pl.ds(h * rows + at + y, STRIP), :] = new[h]
+            heat[pl.ds((2 * (planes - 1) + h) * ny + y, STRIP), :] = new[h]
 
     def below(h, y):
         return tm[h, pl.ds(PAD + (planes - 2) * ny + y, STRIP), :]
 
     last_plane(pad, below, halo, gxb, gxm, gy, gz, coeff, ny, emit)
-    totals[...] = totals_in[...]
-    for h in HALVES:
-        bin_rows(heat, owner, h * rows + at, ny, totals, lines)
-    sums[...] = jnp.sum(totals[...], axis=1)
-    lane = lanes_iota(1)
-
-    def more(n, carry):
-        entry = extra[n]
-        row, col = unpack(entry)
-        line = lax.shift_right_logical(entry, wall.bit_length() - 1) & (lines - 1)
-        hit = jnp.where(lane == col, heat[pl.ds(row, 1), :], 0.0)
-        sums[pl.ds(line, 1), :] = sums[pl.ds(line, 1), :] + hit
-        return carry
-
-    lax.fori_loop(0, extra_n[0], more, 0)
+    found[...] = found_in[...]
+    copy.wait()
+    early = early_groups(ordered, 2 * (rows - ny), rows)
+    read_walls(early, ordered.shape[0] // READ_GROUP, ordered, row_of, col_of, heat, found, rows)
+    owner = line_of(packed[...], wall)
+    hot = found[...]
+    for k in range(lines):
+        part = jnp.where(owner == k, hot, 0.0)
+        sums[k : k + 1, :] = jnp.sum(part, axis=0, keepdims=True)
     mean = lax.dot_general(
         jnp.ones((8, LANES), jnp.float32),
         sums[...],
@@ -414,71 +481,14 @@
     send[:, lines : 2 * lines] = jnp.broadcast_to(gain, (count, lines))
 
 
-def owners_kernel(wall, keys, packed, ordered, owner, extra, extra_n, words, words_s, sem):
-    rows, total = owner.shape[0], keys.shape[0]
-    lines = total // wall
-    bits = 32
-    one = packed[...]
-    depth = one.shape[0]
-    nxt = pltpu.roll(one, LANES - 1, 1)
-    wrap = pltpu.roll(nxt, depth - 1, 0)
-    lane = lanes_iota(depth)
-    place = lax.broadcasted_iota(jnp.int32, (depth, LANES), 0)
-    after = jnp.where(lane == LANES - 1, wrap, nxt)
-    same = lax.shift_right_logical(one ^ after, 13) == 0
-    same = same & ((lane < LANES - 1) | (place < depth - 1))
-    flag = jnp.where(same, lax.shift_left(jnp.int32(1), place & (bits - 1)), 0)
-    words[...] = jnp.zeros_like(words)
-    for g in range(depth // bits):
-        words[pl.ds(g, 1), :] = jnp.sum(flag[g * bits : (g + 1) * bits], axis=0, keepdims=True)
-    copy = pltpu.make_async_copy(words, words_s, sem)
-    copy.start()
-
-    def clear(r):
-        owner[pl.ds(r, 64), :] = jnp.full((64, LANES), LANES - 1, jnp.int32)
-
-    rows_loop(rows, clear, 64)
-    ones = lanes_iota(1)
-    unroll = 32
-
-    def line(k, carry):
-        value = jnp.full((1, LANES), k, jnp.int32)
-
-        def body(s, inner):
-            for u in range(unroll):
-                key = keys[k * wall + s * unroll + u]
-                row = lax.shift_right_logical(key, 7)
-                pltpu.store(owner.at[pl.ds(row, 1), :], value, mask=ones == (key & (LANES - 1)))
-            return inner
-
-        return lax.fori_loop(0, wall // unroll, body, carry)
-
-    lax.fori_loop(0, lines, line, 0)
-    copy.wait()
-
-    def lane_turn(c, n):
-        for g in range(depth // bits):
-
-            def go(state):
-                word, n = state
-                low = word & (-word)
-                bit = 31 - lax.clz(low)
-                extra[n] = ordered[(g * bits + bit) * LANES + c]
-                return word ^ low, n + 1
-
-            _, n = lax.while_loop(lambda state: state[0] != 0, go, (words_s[g, c], n))
-        return n
-
-    extra_n[0] = lax.fori_loop(0, LANES, lane_turn, 0)
-
-
 def finish_kernel(
-    wall, heat, owner, extra, extra_n, rows_all, film, ratio, direction, entry, out, mid, final, table, splat, sem
+    wall, packed, found, rows_all, direction, entry, heat_in, out, mid, heat, table, change, ordered, row_of, col_of, sem, sems
 ):
     planes, ny = out.shape[0], out.shape[1]
     rows = planes * ny
     count, lines = rows_all.shape[0], mid.shape[1]
     me = lax.axis_index("brick")
+    copy = unpack(packed, ordered, row_of, col_of, sem, rows)
 
     def pass_on(k, water):
         row = rows_all[pl.ds(k, 1), :]
@@ -495,49 +505,58 @@
     table[...] = jnp.zeros_like(table)
     table[0:1, 0:lines] = 0.5 * (1.0 - keep)
     table[1:2, 0:lines] = coolant
-    eye = lax.broadcasted_iota(jnp.int32, (lines, LANES), 0) == lanes_iota(lines)
-    for k in range(2):
-        spread = jnp.broadcast_to(table[k : k + 1, :], (lines, LANES))
-        column = jnp.sum(jnp.where(eye, spread, 0.0), axis=1, keepdims=True)
-        splat[k] = jnp.broadcast_to(column, (lines, LANES))
     pull = jnp.broadcast_to(table[0:1, :], (8, LANES))
     cool = jnp.broadcast_to(table[1:2, :], (8, LANES))
-
-    def dense(r):
-        own = owner[pl.ds(r, 8), :]
-        hot = heat[pl.ds(r, 8), :]
-        a = jnp.take_along_axis(pull, own, axis=1)
-        c = jnp.take_along_axis(cool, own, axis=1)
-        final[pl.ds(r, 8), :] = hot + a * (c - hot)
-
-    rows_loop(2 * rows, dense, 8, unroll=16)
-    lane = lanes_iota(1)
-
-    def more(n, carry):
-        item = extra[n]
-        row, col = unpack(item)
-        line = lax.shift_right_logical(item, wall.bit_length() - 1) & (lines - 1)
-        a = splat[0, pl.ds(line, 1), :]
-        c = splat[1, pl.ds(line, 1), :]
-        hot = heat[pl.ds(row, 1), :]
-        final[pl.ds(row, 1), :] = final[pl.ds(row, 1), :] + jnp.where(lane == col, a * (c - hot), 0.0)
-        return carry
-
-    lax.fori_loop(0, extra_n[0], more, 0)
-    copies = []
-    for x in range(planes):
-        for h in HALVES:
-            copies.append(
-                pltpu.make_async_copy(
-                    final.at[pl.ds(h * rows + x * ny, ny), :],
-                    out.at[x, :, pl.ds(h * LANES, LANES)],
-                    sem.at[x, h],
-                )
+    depth = change.shape[0]
+    for k in range(0, depth, 8):
+        owner = line_of(packed[k : k + 8, :], wall)
+        a = jnp.take_along_axis(pull, owner, axis=1)
+        c = jnp.take_along_axis(cool, owner, axis=1)
+        change[k : k + 8, :] = a * (c - found[k : k + 8, :])
+    tall = lax.broadcasted_iota(jnp.int32, (WINDOW, LANES), 0)
+    square = lax.broadcasted_iota(jnp.int32, (LANES, LANES), 0)
+
+    def work(c, base):
+        at = jnp.where(tall == row_of[pl.ds(c, 1), :] - base, 1.0, 0.0).astype(jnp.bfloat16)
+        amount = jnp.where(square == col_of[pl.ds(c, 1), :], change[pl.ds(c, 1), :], 0.0)
+        high, low = split(amount)
+        dims = (((1,), (1,)), ((), ()))
+        return lax.dot_general(at, high, dims, preferred_element_type=jnp.float32) + lax.dot_general(
+            at, low, dims, preferred_element_type=jnp.float32
+        )
+
+    def commit(c, base, item):
+        heat[pl.ds(base, WINDOW), :] = heat[pl.ds(base, WINDOW), :] + item
+
+    def copies(j):
+        x = plane_of(j, planes)
+        return [
+            pltpu.make_async_copy(
+                heat.at[pl.ds((2 * j + h) * ny, ny), :],
+                out.at[x, :, pl.ds(h * LANES, LANES)],
+                sems.at[j, h],
             )
-    for copy in copies:
-        copy.start()
-    for copy in copies:
-        copy.wait()
+            for h in HALVES
+        ]
+
+    groups = depth // WRITE_GROUP
+
+    def after(g, sent):
+        following = row_at(ordered, jnp.minimum((g + 1) * WRITE_GROUP, depth - 1), 0, rows) & -8
+        ready = jnp.where(g == groups - 1, 2 * rows, following)
+
+        def send(j):
+            for item in copies(j):
+                item.start()
+            return j + 1
+
+        return lax.while_loop(lambda j: (j + 1) * 2 * ny <= ready, send, sent)
+
+    copy.wait()
+    windows(0, groups, WRITE_GROUP, ordered, rows, work, commit, after)
+    for j in range(planes):
+        for item in copies(j):
+            item.wait()
 
 
 def per_device(
@@ -580,18 +599,12 @@
     halo_a = swap(ta, on_chip)
 
     cell = bore_boundary_positions.reshape(hits)
-    keys = ((cell & LANES) * (rows * LANES // LANES)) | ((cell >> 8) << 7) | (cell & (LANES - 1))
-    packed = lax.sort(keys * 8192 + lax.iota(jnp.int32, hits), is_stable=False)
-    halo_a, keys, packed = lax.optimization_barrier((halo_a, keys, packed))
-    owner, extra, extra_n = call(
-        lambda *refs: owners_kernel(wall, *refs),
-        (keys, packed.reshape(hits // LANES, LANES), packed),
-        [SMEM, VMEM, SMEM],
-        (i32(2 * rows, LANES), i32(hits), i32(1)),
-        (VMEM, SMEM, SMEM),
-        [pltpu.VMEM((8, LANES), jnp.int32), pltpu.SMEM((8, LANES), jnp.int32), dma],
-        cost=20_000_000,
-    )
+    cell = cell ^ jnp.where(lax.rem(lax.axis_index("brick"), 2) == 1, 0, (planes - 1) * ny * nz)
+    row = (cell // (ny * nz) * 2 + (cell // LANES) % 2) * ny + (cell // nz) % ny
+    cell = (row * LANES + cell % LANES) ^ (rows * LANES)
+    packed = lax.sort(cell * 8192 + lax.iota(jnp.int32, hits), is_stable=False)
+    halo_a, packed = lax.optimization_barrier((halo_a, packed))
+    packed = packed.reshape(hits // LANES, LANES)
 
     full = f32(2, rows + 2 * PAD, LANES)
     most = f32(2, rows - ny + 2 * PAD, LANES)
@@ -645,47 +658,50 @@
     halo_b = swap(tb2, across)
     halo_a = swap(ta, on_chip)
 
-    heat, totals = call(
-        final_main_kernel,
-        (t2, tb2, halo_a, gxa, gxm, gy, gz, coeff, owner),
+    depth = hits // LANES
+    listing = [
+        pltpu.SMEM((depth, LANES), jnp.int32),
+        pltpu.VMEM((depth, LANES), jnp.int32),
+        pltpu.VMEM((depth, LANES), jnp.int32),
+        dma,
+    ]
+    heat, found = call(
+        lambda *refs: final_main_kernel(*refs),
+        (t2, tb2, halo_a, gxa, gxm, gy, gz, coeff, packed),
         [VMEM] * 9,
-        (f32(2 * rows, LANES), f32(lines, 8, LANES)),
+        (f32(2 * rows + WINDOW, LANES), f32(depth, LANES)),
         (VMEM, VMEM),
+        listing,
         cost=10_000_000,
     )
     ratio = surface_over_flow_ratio.reshape(1, lines)
-    heat, send = call(
+    heat, found, send = call(
         lambda *refs: walls_kernel(wall, *refs),
-        (t2, tb2, halo_b, gxb, gxm, gy, gz, coeff, owner, extra, extra_n, totals, surface_transfer_coefficient, ratio, heat),
-        [VMEM] * 9 + [SMEM, SMEM] + [VMEM] * 4,
-        (f32(2 * rows, LANES), f32(count, LANES)),
-        (VMEM, VMEM),
-        [pad, pltpu.VMEM((lines, 8, LANES), jnp.float32), pltpu.VMEM((lines, LANES), jnp.float32)],
-        input_output_aliases={14: 0},
+        (t2, tb2, halo_b, gxb, gxm, gy, gz, coeff, packed, found, surface_transfer_coefficient, ratio, heat),
+        [VMEM] * 13,
+        (f32(2 * rows + WINDOW, LANES), f32(depth, LANES), f32(count, LANES)),
+        (VMEM, VMEM, VMEM),
+        [pad, pltpu.VMEM((lines, LANES), jnp.float32)] + listing,
+        input_output_aliases={12: 0},
     )
     rows_all = lax.all_to_all(send, "brick", 0, 0, tiled=True)
-    final, mid = call(
+    final, mid, _ = call(
         lambda *refs: finish_kernel(wall, *refs),
         (
-            heat,
-            owner,
-            extra,
-            extra_n,
+            packed,
+            found,
             rows_all,
-            surface_transfer_coefficient,
-            ratio,
             flow_direction_flag.reshape(1, lines),
             entry_coolant_degrees.reshape(1, lines),
+            heat,
         ),
-        [VMEM, VMEM, SMEM, SMEM] + [VMEM] * 5,
-        (f32(planes, ny, nz), f32(1, lines)),
-        (HBM, VMEM),
-        [
-            pltpu.VMEM((2 * rows, LANES), jnp.float32),
-            pltpu.VMEM((8, LANES), jnp.float32),
-            pltpu.VMEM((2, lines, LANES), jnp.float32),
-            dma((planes, 2)),
-        ],
+        [VMEM] * 6,
+        (f32(planes, ny, nz), f32(1, lines), f32(2 * rows + WINDOW, LANES)),
+        (HBM, VMEM, VMEM),
+        [pltpu.VMEM((8, LANES), jnp.float32), pltpu.VMEM((depth, LANES), jnp.float32)]
+        + listing
+        + [dma((planes, 2))],
+        input_output_aliases={5: 2},
     )
     return final, mid
 

time: 91 us -> 65.1 us (0.72)
  Pallas kernels: 59.5 us -> 33.7 us
  blocking collectives: 11.8 us -> 9.29 us
  waiting for transfers between devices: 5.46 us -> 7.89 us
    pallas_call x9 -> x8, Pallas kernels: 59.5 us -> 33.7 us  [call(): pl.pallas_call(kernel, out_shape=out_shape, in_specs=in_specs, out_specs=...]
    all_to_all x1, blocking collectives: 11.8 us -> 9.29 us  [per_device(): rows_all = lax.all_to_all(send, 'brick', 0, 0, tiled=True)]
    ppermute x6, waiting for transfers between devices: 5.46 us -> 7.89 us  [swap(): return lax.ppermute(value, 'brick', pairs)]
  transfers between devices with their start and end apart: 6 -> 6, of which waited for: 1 -> 2; matrix products, arithmetic and copies ran while one was open for 6% -> 9% of each run, Pallas kernels for 49% -> 36%
where the time goes in v4:
time: 65.1 us; the launch traced here: 64.9 us
  Pallas kernels  33.7 us (52%)
  blocking collectives  9.29 us (14%)
  waiting for transfers between devices  7.89 us (12%)
  starting transfers between devices  7.54 us (12%)
  other arithmetic  5.69 us (9%)
  between operations  0.77 us (1%)
    pallas_call x8, Pallas kernels, call(): pl.pallas_call(kernel, out_shape=out_shape, in_specs=in_specs, out_specs=...  33.7 us
    all_to_all x1, blocking collectives, per_device(): rows_all = lax.all_to_all(send, 'brick', 0, 0, tiled=True)  9.29 us
    ppermute x6, waiting for transfers between devices, swap(): return lax.ppermute(value, 'brick', pairs)  7.89 us
    ppermute x6, starting transfers between devices, swap(): return lax.ppermute(value, 'brick', pairs)  7.54 us
    sort x1, other arithmetic, per_device(): packed = lax.sort(cell * 8192 + lax.iota(jnp.int32, hits), is_stable=False)  5.59 us
  transfers between devices with their start and end apart: 6, of which 2 were waited for; matrix products, arithmetic and copies ran while one was open for 9% of the time, Pallas kernels for 36%

profile of v4, /device:TPU:0, one launch (start us, length us, event | category | flops | bytes accessed | tf_op | source)
XLA Modules:
  0.0 64.9 jit_solution(10877389722884876591)
XLA Ops:
  0.6 0.0 copy-start.6
  0.6 0.0 copy-start
  0.7 0.0 copy-start.3
  0.7 1.4 %shard_map.104 = (f32[2,2,256,128]{3,2,1,0:T(8,128)S(1)}, f32[2,2,256,128]{3,2,1,0:T(8,128)S(1)}) custom-call(f32[8,256,256]{2,1,0:T(8,128)} %t_ref.3, s32[8,256,256]{2,1,0:T(8,128)} %refs_0_.1), custom_call_target="tpu_custom_call" | custom-call | flops 2000000 | bytes 2000000 | tf_op jit(solution)/shard_map/pallas_call | solution.py:29
  2.1 0.5 collective-permute-start
  2.6 5.7 %collective-permute-start.1 = (f32[2,2,256,128]{3,2,1,0:T(8,128)S(1)}, f32[2,2,256,128]{3,2,1,0:T(8,128)S(1)}, u32[]{:S(2)}, u32[]{:S(2)}) collective-permute-start(f32[2,2,256,128]{3,2,1,0:T(8,128)S(1)} %get-tuple-element.30), channel_id=1, source_target_pairs={{1,2},{3,4},{5,6},{7,8},{9,10},{11,12},{13,14},{15,0},{2,1},{4,3},... | collective-permute-start | bytes 1572872 | tf_op jit(solution)/shard_map/ppermute | solution.py:583
  8.3 0.0 copy-done.6
  8.3 0.1 fusion.9
  8.4 5.6 %sort.7 = s32[8192]{0:T(1024)S(1)} sort(s32[8192]{0:T(1024)S(1)} %fusion.9), dimensions={0}, to_apply=%region_0.1 | sort | flops 106496 | bytes 65536 | tf_op jit(solution)/shard_map/sort | solution.py:605
  14.0 0.0 collective-permute-done.halo
  14.0 0.0 copy-done
  14.0 0.0 copy-done.3
  14.0 12.9 %shard_map.105 = (f32[2,2064,128]{2,1,0:T(8,128)S(1)}, f32[2,256,128]{2,1,0:T(8,128)S(1)}, f32[2,1792,128]{2,1,0:T(8,128)S(1)}, f32[2,2064,128]{2,1,0:T(8,128)S(...) custom-call(f32[8,256,256]{2,1,0:T(8,128)} %t_ref.3, ...), custom_call_target="tpu_custom_call" | custom-call | flops 10000000 | bytes 10000000 | tf_op jit(solution)/shard_map/pallas_call | solution.py:29
  26.9 0.1 collective-permute-start.2
  26.9 0.0 collective-permute-done.1.refs_3_
  27.0 2.2 %shard_map.106 = (f32[2,256,128]{2,1,0:T(8,128)S(1)}, f32[2,256,128]{2,1,0:T(8,128)S(1)}) custom-call(s32[8,256,256]{2,1,0:T(8,128)} %refs_0_.1, f32[8]{0:T(128)S(1)} %copy-done, f32[2,2064,128]{2,1,0:T(8,128)S(1)} %get-tuple-element.29.refs_2_, f32[2,2,256,128]{3,2,1,0:T(8,128)S(1)} %collective-permute-done.1.refs_3_, ...), custom_call_target="tpu_custom_call" | custom-call | flops 2000000 | bytes 2000000 | tf_op jit(solution)/shard_map/pallas_call | solution.py:29
  29.2 0.7 %collective-permute-start.3 = (f32[2,256,128]{2,1,0:T(8,128)S(1)}, f32[2,256,128]{2,1,0:T(8,128)S(1)}, u32[]{:S(2)}, u32[]{:S(2)}) collective-permute-start(f32[2,256,128]{2,1,0:T(8,128)S(1)} %get-tuple-element.35.tb_old), channel_id=1, source_target_pairs={{1,2},{3,4},{5,6},{7,8},{9,10},{11,12},{13,14},{15,0},{2,1},{4,3},... | collective-permute-start | bytes 786440 | tf_op jit(solution)/shard_map/ppermute | solution.py:583
  29.9 0.0 collective-permute-done.2.halo
  29.9 2.3 %shard_map.107 = (f32[2,1808,128]{2,1,0:T(8,128)S(1)}, f32[2,256,128]{2,1,0:T(8,128)S(1)}) custom-call(f32[2,1808,128]{2,1,0:T(8,128)S(1)} %get-tuple-element.28.tm, f32[2,256,128]{2,1,0:T(8,128)S(1)} %get-tuple-element.35.tb_old, f32[2,256,128]{2,1,0:T(8,128)S(1)} %collective-permute-done.2.halo, f32[2,256,128]{2,1,0:T(8,128)S(1)} %get-tuple-element.37.gxa.refs_3_, ...), custom_call_target="tpu_custom_call" | custom-call | flops 4000000 | bytes 4000000 | tf_op jit(solution)/shard_map/pallas_call | solution.py:29
  32.2 0.1 collective-permute-start.5
  32.3 5.6 %collective-permute-done.3.halo = f32[2,256,128]{2,1,0:T(8,128)S(1)} collective-permute-done((f32[2,256,128]{2,1,0:T(8,128)S(1)}, f32[2,256,128]{2,1,0:T(8,128)S(1)}, u32[]{:S(2)}, u32[]{:S(2)}) %collective-permute-start.3) | collective-permute-done | bytes 262176 | tf_op jit(solution)/shard_map/ppermute | solution.py:583
  37.9 0.4 shard_map.108.refs_1_
  38.2 0.6 collective-permute-start.4
  38.8 0.0 collective-permute-done.5.refs_2_
  38.8 0.0 copy-start.1
  38.8 0.0 copy-start.2
  38.8 5.8 %shard_map.109 = (f32[4192,128]{1,0:T(8,128)S(1)}, f32[64,128]{1,0:T(8,128)S(1)}) custom-call(f32[2,1808,128]{2,1,0:T(8,128)S(1)} %get-tuple-element.38.refs_0_, f32[2,256,128]{2,1,0:T(8,128)S(1)} %shard_map.108.refs_1_, f32[2,256,128]{2,1,0:T(8,128)S(1)} %collective-permute-done.5.refs_2_, f32[2,256,128]{2,1,0:T(8,128)S(1)} %get-tuple-element.37.gxa.refs_3_, ...), custom_call_target="tpu_custom_call" | custom-call | flops 10000000 | bytes 10000000 | tf_op jit(solution)/shard_map/pallas_call | solution.py:29
  44.6 2.3 %collective-permute-done.4.refs_2_ = f32[2,256,128]{2,1,0:T(8,128)S(1)} collective-permute-done((f32[2,256,128]{2,1,0:T(8,128)S(1)}, f32[2,256,128]{2,1,0:T(8,128)S(1)}, u32[]{:S(2)}, u32[]{:S(2)}) %collective-permute-start.4) | collective-permute-done | bytes 262176 | tf_op jit(solution)/shard_map/ppermute | solution.py:583
  46.9 0.0 copy-done.1
  46.9 0.0 copy-done.2
  46.9 0.0 copy-start.4
  46.9 0.0 copy-start.5
  46.9 1.9 %shard_map.110 = (f32[4192,128]{1,0:T(8,128)S(1)}, f32[64,128]{1,0:T(8,128)S(1)}, f32[16,128]{1,0:T(8,128)S(1)}) custom-call(f32[2,1808,128]{2,1,0:T(8,128)S(1)} %get-tuple-element.38.refs_0_, f32[2,256,128]{2,1,0:T(8,128)S(1)} %shard_map.108.refs_1_, f32[2,256,128]{2,1,0:T(8,128)S(1)} %collective-permute-done.4.refs_2_, ...), custom_call_target="tpu_custom_call", output_to_operand_aliasing={{0}: (12, {})} | custom-call | flops 2000000 | bytes 2000000 | tf_op jit(solution)/shard_map/pallas_call | solution.py:29
  48.9 9.3 %all_to_all.11 = f32[16,1,128]{2,1,0:T(1,128)S(1)} all-to-all(f32[16,1,128]{2,1,0:T(1,128)S(1)} %bitcast.15), channel_id=1, replica_groups=mesh['pour'=2,'brick'=16] {'brick'}, dimensions={0} | all-to-all | bytes 16384 | tf_op jit(solution)/shard_map/all_to_all | solution.py:687
  58.1 0.0 copy-done.4
  58.2 0.0 copy-done.5
  58.2 6.8 %shard_map.111 = (f32[8,256,256]{2,1,0:T(8,128)}, f32[1,32]{1,0:T(1,128)}, f32[4192,128]{1,0:T(8,128)S(1)}) custom-call(s32[64,128]{1,0:T(8,128)S(1)} %bitcast.13, f32[64,128]{1,0:T(8,128)S(1)} %get-tuple-element.43.refs_1_, f32[16,128]{1,0:T(8,128)S(1)} %bitcast.14, s32[1,32]{1,0:T(1,128)S(1)} %bitcast.17, ...), custom_call_target="tpu_custom_call", output_to_operand_aliasing={{2}: (5, {})} | custom-call | flops 2000000 | bytes 2000000 | tf_op jit(solution)/shard_map/pallas_call | solution.py:29
  (2 shorter events, 0.0 us)
Async XLA Ops:
  0.6 7.6 %copy-start.6 = (s32[1,32,256]{2,1,0:T(8,128)S(1)}, s32[1,32,256]{2,1,0:T(8,128)}, u32[]{:S(2)}) copy-start(s32[1,32,256]{2,1,0:T(8,128)} %param.13) | copy-start | bytes 98308
  0.6 13.3 %copy-start = (f32[8]{0:T(128)S(1)}, f32[8]{0:T(128)}, u32[]{:S(2)}) copy-start(f32[8]{0:T(128)} %refs_1_.1) | copy-start | bytes 100
  0.7 13.3 %copy-start.3 = (f32[8]{0:T(128)S(1)}, f32[8]{0:T(128)}, u32[]{:S(2)}) copy-start(f32[8]{0:T(128)} %store_ref.1) | copy-start | bytes 100
  2.1 11.9 %collective-permute-start = (f32[2,2,256,128]{3,2,1,0:T(8,128)S(1)}, f32[2,2,256,128]{3,2,1,0:T(8,128)S(1)}, u32[]{:S(2)}, u32[]{:S(2)}) collective-permute-start(f32[2,2,256,128]{3,2,1,0:T(8,128)S(1)} %get-tuple-element.25), channel_id=1, source_target_pairs={{0,1},{1,0},{2,3},{3,2},{4,5},{5,4},{6,7},{7,6},{8,9},{9,8},{10,11... | collective-permute-start | bytes 1572872 | tf_op jit(solution)/shard_map/ppermute | solution.py:583
  2.6 24.4 %collective-permute-start.1 = (f32[2,2,256,128]{3,2,1,0:T(8,128)S(1)}, f32[2,2,256,128]{3,2,1,0:T(8,128)S(1)}, u32[]{:S(2)}, u32[]{:S(2)}) collective-permute-start(f32[2,2,256,128]{3,2,1,0:T(8,128)S(1)} %get-tuple-element.30), channel_id=1, source_target_pairs={{1,2},{3,4},{5,6},{7,8},{9,10},{11,12},{13,14},{15,0},{2,1},{4,3},... | collective-permute-start | bytes 1572872 | tf_op jit(solution)/shard_map/ppermute | solution.py:583
  26.9 3.0 %collective-permute-start.2 = (f32[2,256,128]{2,1,0:T(8,128)S(1)}, f32[2,256,128]{2,1,0:T(8,128)S(1)}, u32[]{:S(2)}, u32[]{:S(2)}) collective-permute-start(f32[2,256,128]{2,1,0:T(8,128)S(1)} %get-tuple-element.36), channel_id=1, source_target_pairs={{0,1},{1,0},{2,3},{3,2},{4,5},{5,4},{6,7},{7,6},{8,9},{9,8},{10,11... | collective-permute-start | bytes 786440 | tf_op jit(solution)/shard_map/ppermute | solution.py:583
  29.2 8.7 %collective-permute-start.3 = (f32[2,256,128]{2,1,0:T(8,128)S(1)}, f32[2,256,128]{2,1,0:T(8,128)S(1)}, u32[]{:S(2)}, u32[]{:S(2)}) collective-permute-start(f32[2,256,128]{2,1,0:T(8,128)S(1)} %get-tuple-element.35.tb_old), channel_id=1, source_target_pairs={{1,2},{3,4},{5,6},{7,8},{9,10},{11,12},{13,14},{15,0},{2,1},{4,3},... | collective-permute-start | bytes 786440 | tf_op jit(solution)/shard_map/ppermute | solution.py:583
  32.2 6.6 %collective-permute-start.5 = (f32[2,256,128]{2,1,0:T(8,128)S(1)}, f32[2,256,128]{2,1,0:T(8,128)S(1)}, u32[]{:S(2)}, u32[]{:S(2)}) collective-permute-start(f32[2,256,128]{2,1,0:T(8,128)S(1)} %get-tuple-element.40), channel_id=1, source_target_pairs={{0,1},{1,0},{2,3},{3,2},{4,5},{5,4},{6,7},{7,6},{8,9},{9,8},{10,11... | collective-permute-start | bytes 786440 | tf_op jit(solution)/shard_map/ppermute | solution.py:583
  38.2 8.7 %collective-permute-start.4 = (f32[2,256,128]{2,1,0:T(8,128)S(1)}, f32[2,256,128]{2,1,0:T(8,128)S(1)}, u32[]{:S(2)}, u32[]{:S(2)}) collective-permute-start(f32[2,256,128]{2,1,0:T(8,128)S(1)} %shard_map.108.refs_1_), channel_id=1, source_target_pairs={{1,2},{3,4},{5,6},{7,8},{9,10},{11,12},{13,14},{15,0},{2,1},{4,3},... | collective-permute-start | bytes 786440 | tf_op jit(solution)/shard_map/ppermute | solution.py:583
  38.8 8.1 %copy-start.1 = (f32[1,32]{1,0:T(1,128)S(1)}, f32[1,32]{1,0:T(1,128)}, u32[]{:S(2)}) copy-start(f32[1,32]{1,0:T(1,128)} %refs_10_.1) | copy-start | bytes 388
  38.8 8.1 %copy-start.2 = (f32[32]{0:T(128)S(1)}, f32[32]{0:T(128)}, u32[]{:S(2)}) copy-start(f32[32]{0:T(128)} %param.15) | copy-start | bytes 388
  46.9 11.2 %copy-start.4 = (s32[32]{0:T(128)S(1)}, s32[32]{0:T(128)}, u32[]{:S(2)}) copy-start(s32[32]{0:T(128)} %param.16) | copy-start | bytes 388
  46.9 11.2 %copy-start.5 = (f32[32]{0:T(128)S(1)}, f32[32]{0:T(128)}, u32[]{:S(2)}) copy-start(f32[32]{0:T(128)} %param.17) | copy-start | bytes 388

commit v5 on v4

--- a/solution.py
+++ b/solution.py
@@ -146,23 +146,11 @@
             out[1, h] = tags[side, h].astype(jnp.float32)
 
 
-def prepare_kernel(
-    t_ref, tag_ref, cond_ref, store_ref, halo, t0, gxa, gxm, gy, gz, coeff, t1, ta, tags, cond, sem
-):
+def prepare_kernel(t_ref, tag_ref, cond_ref, store_ref, halo, t0, tb, cond_b, gxa, gxm, gy, gz, coeff, cond):
     planes, ny = t_ref.shape[0], t_ref.shape[1]
-    copies = []
-    for j in range(planes):
-        x = plane_of(j, planes)
-        for h in HALVES:
-            part = pl.ds(h * LANES, LANES)
-            rows = pl.ds(PAD + j * ny, ny)
-            copies.append(pltpu.make_async_copy(tag_ref.at[x, :, part], tags.at[h, pl.ds(j * ny, ny)], sem.at[0, j, h]))
-            copies.append(pltpu.make_async_copy(t_ref.at[x, :, part], t0.at[h, rows], sem.at[1, j, h]))
-    for copy in copies:
-        copy.start()
     zero = jnp.zeros((PAD, LANES), jnp.float32)
     for h in HALVES:
-        for ref in (t0, t1, cond):
+        for ref in (t0, cond):
             ref[h, pl.ds(0, PAD), :] = zero
             ref[h, pl.ds(ref.shape[1] - PAD, PAD), :] = zero
         gy[h, pl.ds(0, PAD), :] = zero
@@ -170,16 +158,31 @@
     lane = lanes_iota(STRIP)
     conds = [jnp.full((1, LANES), cond_ref[m], jnp.float32) for m in range(cond_ref.shape[0])]
     scales = [0.16 / jnp.full((1, LANES), store_ref[m], jnp.float32) for m in range(store_ref.shape[0])]
-    for copy in copies:
-        copy.wait()
-
-    def materials(r):
-        for h in HALVES:
-            tag = tags[h, pl.ds(r, STRIP), :]
-            cond[h, pl.ds(PAD + r, STRIP), :] = pick(tag, conds)
-            coeff[h, pl.ds(r, STRIP), :] = pick(tag, scales)
-
-    rows_loop(planes * ny, materials)
+
+    def materials(j, final):
+        x = plane_of(j, planes)
+
+        def body(y):
+            for h in HALVES:
+                part = slice(h * LANES, (h + 1) * LANES)
+                tag = tag_ref[x, pl.ds(y, STRIP), part]
+                kind = pick(tag, conds)
+                cond[h, pl.ds(PAD + j * ny + y, STRIP), :] = kind
+                coeff[h, pl.ds(j * ny + y, STRIP), :] = pick(tag, scales)
+                if final:
+                    cond_b[h, pl.ds(y, STRIP), :] = kind
+                    tb[h, pl.ds(y, STRIP), :] = t_ref[x, pl.ds(y, STRIP), part]
+                else:
+                    t0[h, pl.ds(PAD + j * ny + y, STRIP), :] = t_ref[x, pl.ds(y, STRIP), part]
+
+        rows_loop(ny, body)
+
+    def main(j, carry):
+        materials(j, False)
+        return carry
+
+    lax.fori_loop(0, planes - 1, main, 0)
+    materials(planes - 1, True)
 
     def halo_face(y):
         for h in HALVES:
@@ -200,28 +203,17 @@
         mine = [cond[h, pl.ds(PAD + r, STRIP), :] for h in HALVES]
         nxt = [pltpu.roll(mine[h], LANES - 1, 1) for h in HALVES]
         ahead = [jnp.where(lane == LANES - 1, nxt[1], nxt[0]), nxt[1]]
-        right = [face_mean(mine[h], ahead[h]) for h in HALVES]
-        right[1] = jnp.where(lane == LANES - 1, 0.0, right[1])
-        back = [pltpu.roll(right[h], 1, 1) for h in HALVES]
-        left = [jnp.where(lane == 0, back[1], back[0]), jnp.where(lane == 0, back[0], back[1])]
+        prv = [pltpu.roll(mine[h], 1, 1) for h in HALVES]
+        behind = [prv[0], jnp.where(lane == 0, prv[0], prv[1])]
         for h in HALVES:
             below = face_mean(mine[h], cond[h, pl.ds(PAD + r + 1, STRIP), :])
             gy[h, pl.ds(PAD + r, STRIP), :] = jnp.where(y == ny - 1, 0.0, below)
-            gz[h, pl.ds(r, STRIP), :] = right[h]
-            gz[2 + h, pl.ds(r, STRIP), :] = left[h]
-
-    rows_loop(planes * ny, yz_faces)
-
-    def emit(j, y, new, first):
-        for h in HALVES:
-            t1[h, pl.ds(PAD + j * ny + y, STRIP), :] = new[h]
-            if first:
-                ta[h, pl.ds(y, STRIP), :] = new[h]
-
-    def last(h, y):
-        return t0[h, pl.ds(PAD + (planes - 1) * ny + y, STRIP), :]
-
-    main_planes(t0, last, halo.at[0], gxa, gxm, gy, gz, coeff, planes, ny, emit)
+            right = face_mean(mine[h], ahead[h])
+            gz[h, pl.ds(r, STRIP), :] = jnp.where(lane == LANES - 1, 0.0, right) if h else right
+            left = face_mean(behind[h], mine[h])
+            gz[2 + h, pl.ds(r, STRIP), :] = left if h else jnp.where(lane == 0, 0.0, left)
+
+    rows_loop(planes * ny, yz_faces, unroll=8)
 
 
 def last_plane(cur, below, halo, gxb, gxm, gy, gz, coeff, ny, emit):
@@ -260,41 +252,20 @@
     rows_loop(ny, body)
 
 
-def first_last_kernel(brick_count, tag_ref, cond_ref, t0, halo, gxm, gy, gz, coeff, gxb, tb, pad, tags, sem):
+def first_last_kernel(brick_count, cond_ref, tm, tb_old, cond_b, halo, gxm, gy, gz, coeff, gxb, tb, pad):
     ny = tb.shape[1]
-    planes = gz.shape[1] // ny
-    base = (planes - 1) * ny
-    x = plane_of(planes - 1, planes)
-    copies = [
-        pltpu.make_async_copy(tag_ref.at[x, :, pl.ds(h * LANES, LANES)], tags.at[h], sem.at[h])
-        for h in HALVES
-    ]
-    for copy in copies:
-        copy.start()
     me = lax.axis_index("brick")
     edge = (me == 0) | (me == brick_count - 1)
     keep = jnp.where(edge, 0.0, 1.0).astype(jnp.float32)
-    conds = [jnp.full((1, LANES), cond_ref[m], jnp.float32) for m in range(cond_ref.shape[0])]
-    padded(pad, lambda h, y: t0[h, pl.ds(PAD + base + y, STRIP), :], ny)
-    for copy in copies:
-        copy.wait()
+    conds = [keep * jnp.full((1, LANES), cond_ref[m], jnp.float32) for m in range(cond_ref.shape[0])]
 
     def faces(y):
         for h in HALVES:
-            other = keep * pick(halo[1, h, pl.ds(y, STRIP), :].astype(jnp.int32), conds)
-            mine = pick(tags[h, pl.ds(y, STRIP), :], conds)
-            gxb[h, pl.ds(y, STRIP), :] = face_mean(mine, other)
+            other = pick(halo[1, h, pl.ds(y, STRIP), :].astype(jnp.int32), conds)
+            gxb[h, pl.ds(y, STRIP), :] = face_mean(cond_b[h, pl.ds(y, STRIP), :], other)
 
     rows_loop(ny, faces)
-
-    def emit(y, new):
-        for h in HALVES:
-            tb[h, pl.ds(y, STRIP), :] = new[h]
-
-    def below(h, y):
-        return t0[h, pl.ds(PAD + base - ny + y, STRIP), :]
-
-    last_plane(pad, below, halo.at[0], gxb, gxm, gy, gz, coeff, ny, emit)
+    next_last_kernel(tm, tb_old, halo.at[0], gxb, gxm, gy, gz, coeff, tb, pad)
 
 
 def next_last_kernel(tm, tb_old, halo, gxb, gxm, gy, gz, coeff, tb, pad):
@@ -482,7 +453,7 @@
 
 
 def finish_kernel(
-    wall, packed, found, rows_all, direction, entry, heat_in, out, mid, heat, table, change, ordered, row_of, col_of, sem, sems
+    wall, packed, found, rows_all, direction, entry, heat_in, out, mid, heat, gains, table, change, ordered, row_of, col_of, sem, sems
 ):
     planes, ny = out.shape[0], out.shape[1]
     rows = planes * ny
@@ -491,18 +462,18 @@
     copy = unpack(packed, ordered, row_of, col_of, sem, rows)
 
     def pass_on(k, water):
-        row = rows_all[pl.ds(k, 1), :]
-        return row[:, 0:lines] * water + row[:, lines : 2 * lines]
-
-    start = entry[...]
+        return rows_all[pl.ds(k, 1), :] * water + gains[pl.ds(k, 1), :]
+
+    gains[...] = pltpu.roll(rows_all[...], LANES - lines, 1)
+    table[...] = jnp.zeros_like(table)
+    table[0:1, 0:lines] = entry[...]
+    start = table[0:1, :]
     ahead = lax.fori_loop(0, me, pass_on, start)
     behind = lax.fori_loop(0, count - 1 - me, lambda k, w: pass_on(count - 1 - k, w), start)
-    inflow = jnp.where(direction[...] == 0, ahead, behind)
-    own = rows_all[pl.ds(me, 1), :]
-    keep, gain = own[:, 0:lines], own[:, lines : 2 * lines]
-    coolant = 0.5 * (inflow + keep * inflow + gain)
+    inflow = jnp.where(direction[...] == 0, ahead[:, 0:lines], behind[:, 0:lines])
+    keep = rows_all[pl.ds(me, 1), :][:, 0:lines]
+    coolant = 0.5 * (inflow + keep * inflow + gains[pl.ds(me, 1), :][:, 0:lines])
     mid[...] = coolant
-    table[...] = jnp.zeros_like(table)
     table[0:1, 0:lines] = 0.5 * (1.0 - keep)
     table[1:2, 0:lines] = coolant
     pull = jnp.broadcast_to(table[0:1, :], (8, LANES))
@@ -582,6 +553,7 @@
     def swap(value, pairs):
         return lax.ppermute(value, "brick", pairs)
 
+    temperatures, tags = initial_voxel_degrees, alloy_tag_per_voxel
     initial_voxel_degrees = pltpu.with_memory_space_constraint(initial_voxel_degrees, pltpu.HBM)
     alloy_tag_per_voxel = pltpu.with_memory_space_constraint(alloy_tag_per_voxel, pltpu.HBM)
 
@@ -608,35 +580,34 @@
 
     full = f32(2, rows + 2 * PAD, LANES)
     most = f32(2, rows - ny + 2 * PAD, LANES)
-    t0, gxa, gxm, gy, gz, coeff, t1, ta = call(
+    t0, tb0, cond_b, gxa, gxm, gy, gz, coeff = call(
         prepare_kernel,
-        (
-            initial_voxel_degrees,
-            alloy_tag_per_voxel,
-            thermal_conductance_per_alloy,
-            specific_storage_per_alloy,
-            halo_a,
-        ),
-        [HBM, HBM, SMEM, SMEM, VMEM],
-        (full, plane, f32(2, rows - ny, LANES), full, f32(4, rows, LANES), f32(2, rows, LANES), most, plane),
+        (temperatures, tags, thermal_conductance_per_alloy, specific_storage_per_alloy, halo_a),
+        [VMEM, VMEM, SMEM, SMEM, VMEM],
+        (most, plane, plane, plane, f32(2, rows - ny, LANES), full, f32(4, rows, LANES), f32(2, rows, LANES)),
         (VMEM,) * 8,
-        [
-            pltpu.VMEM((2, rows, LANES), jnp.int32),
-            pltpu.VMEM((2, rows + 2 * PAD, LANES), jnp.float32),
-            dma((2, planes, 2)),
-        ],
+        [pltpu.VMEM((2, rows + 2 * PAD, LANES), jnp.float32)],
         cost=10_000_000,
     )
     pad = pltpu.VMEM((2, ny + 2 * PAD, LANES), jnp.float32)
     gxb, tb = call(
         lambda *refs: first_last_kernel(count, *refs),
-        (alloy_tag_per_voxel, thermal_conductance_per_alloy, t0, halo_b, gxm, gy, gz, coeff),
-        [HBM, SMEM] + [VMEM] * 6,
+        (thermal_conductance_per_alloy, t0, tb0, cond_b, halo_b, gxm, gy, gz, coeff),
+        [SMEM] + [VMEM] * 8,
         (plane, plane),
         (VMEM, VMEM),
-        [pad, pltpu.VMEM((2, ny, LANES), jnp.int32), dma((2,))],
-    )
+        [pad],
+    )
+    tb, t0 = lax.optimization_barrier((tb, t0))
     halo_b = swap(tb, across)
+    t1, ta = call(
+        lambda tm, old, halo, *refs: next_main_kernel(tm, old, halo.at[0], *refs),
+        (t0, tb0, halo_a, gxa, gxm, gy, gz, coeff),
+        [VMEM] * 8,
+        (most, plane),
+        (VMEM, VMEM),
+        cost=4_000_000,
+    )
     halo_a = swap(ta, on_chip)
 
     t2, ta = call(
@@ -698,7 +669,11 @@
         [VMEM] * 6,
         (f32(planes, ny, nz), f32(1, lines), f32(2 * rows + WINDOW, LANES)),
         (HBM, VMEM, VMEM),
-        [pltpu.VMEM((8, LANES), jnp.float32), pltpu.VMEM((depth, LANES), jnp.float32)]
+        [
+            pltpu.VMEM((count, LANES), jnp.float32),
+            pltpu.VMEM((8, LANES), jnp.float32),
+            pltpu.VMEM((depth, LANES), jnp.float32),
+        ]
         + listing
         + [dma((planes, 2))],
         input_output_aliases={5: 2},

time: 65.1 us -> 61.4 us (0.943)
  Pallas kernels: 33.7 us -> 28.4 us
  waiting for transfers between devices: 7.89 us -> 5.36 us
  starting transfers between devices: 7.54 us -> 9.93 us
  local copies, waits for them, and re-layouts: 0.05 us -> 1.64 us
    pallas_call x8 -> x9, Pallas kernels: 33.7 us -> 28.4 us  [call(): pl.pallas_call(kernel, out_shape=out_shape, in_specs=in_specs, out_specs=...]
    ppermute x6, waiting for transfers between devices: 7.89 us -> 5.36 us  [swap(): return lax.ppermute(value, 'brick', pairs)]
    ppermute x6, starting transfers between devices: 7.54 us -> 9.93 us  [swap(): return lax.ppermute(value, 'brick', pairs)]
    unnamed x15 -> x19, local copies, waits for them, and re-layouts: 0.05 us -> 1.64 us
  transfers between devices with their start and end apart: 6 -> 6, of which waited for: 2 -> 2; matrix products, arithmetic and copies ran while one was open for 9% -> 9% of each run, Pallas kernels for 36% -> 23%
where the time goes in v5:
time: 61.4 us; the launch traced here: 61.1 us
  Pallas kernels  28.4 us (46%)
  starting transfers between devices  9.93 us (16%)
  blocking collectives  9.27 us (15%)
  other arithmetic  5.69 us (9%)
  waiting for transfers between devices  5.36 us (9%)
  local copies, waits for them, and re-layouts  1.64 us (3%)
  between operations  0.81 us (1%)
    pallas_call x9, Pallas kernels, call(): pl.pallas_call(kernel, out_shape=out_shape, in_specs=in_specs, out_specs=...  28.4 us
    ppermute x6, starting transfers between devices, swap(): return lax.ppermute(value, 'brick', pairs)  9.93 us
    all_to_all x1, blocking collectives, per_device(): rows_all = lax.all_to_all(send, 'brick', 0, 0, tiled=True)  9.27 us
    sort x1, other arithmetic, per_device(): packed = lax.sort(cell * 8192 + lax.iota(jnp.int32, hits), is_stable=False)  5.59 us
    ppermute x6, waiting for transfers between devices, swap(): return lax.ppermute(value, 'brick', pairs)  5.36 us
    unnamed x19, local copies, waits for them, and re-layouts  1.64 us
  transfers between devices with their start and end apart: 6, of which 2 were waited for; matrix products, arithmetic and copies ran while one was open for 9% of the time, Pallas kernels for 23%

profile of v5, /device:TPU:0, one launch (start us, length us, event | category | flops | bytes accessed | tf_op | source)
XLA Modules:
  0.0 61.1 jit_solution(15706693441279678058)
XLA Ops:
  0.6 0.0 copy-start
  0.6 0.0 copy-start.8
  0.7 0.0 copy-start.2
  0.7 0.0 copy-start.5
  0.7 2.5 %shard_map.104 = (f32[2,2,256,128]{3,2,1,0:T(8,128)}, f32[2,2,256,128]{3,2,1,0:T(8,128)}) custom-call(f32[8,256,256]{2,1,0:T(8,128)} %t_ref.3, s32[8,256,256]{2,1,0:T(8,128)} %tag_ref.3), custom_call_target="tpu_custom_call" | custom-call | flops 2000000 | bytes 2000000 | tf_op jit(solution)/shard_map/pallas_call | solution.py:29
  3.2 0.5 collective-permute-start
  3.7 5.7 %collective-permute-start.1 = (f32[2,2,256,128]{3,2,1,0:T(8,128)}, f32[2,2,256,128]{3,2,1,0:T(8,128)S(1)}, u32[]{:S(2)}, u32[]{:S(2)}) collective-permute-start(f32[2,2,256,128]{3,2,1,0:T(8,128)} %get-tuple-element.35), channel_id=1, source_target_pairs={{1,2},{3,4},{5,6},{7,8},{9,10},{11,12},{13,14},{15,0},{2,1},{4,3},... | collective-permute-start | bytes 1572872 | tf_op jit(solution)/shard_map/ppermute | solution.py:554
  9.3 0.0 copy-done.8
  9.4 0.1 fusion.9
  9.5 5.6 %sort.7 = s32[8192]{0:T(1024)S(1)} sort(s32[8192]{0:T(1024)S(1)} %fusion.9), dimensions={0}, to_apply=%region_0.1 | sort | flops 106496 | bytes 65536 | tf_op jit(solution)/shard_map/sort | solution.py:577
  15.1 0.0 collective-permute-done.halo
  15.1 0.0 copy-done
  15.1 0.0 copy-done.2
  15.1 0.0 copy-done.5
  15.1 0.0 copy-start.1
  15.1 1.6 %copy-done.1 = s32[8,256,256]{2,1,0:T(8,128)S(1)} copy-done((s32[8,256,256]{2,1,0:T(8,128)S(1)}, s32[8,256,256]{2,1,0:T(8,128)}, u32[]{:S(2)}) %copy-start.1) | copy-done | bytes 2097176
  16.7 5.3 %shard_map.105 = (f32[2,1808,128]{2,1,0:T(8,128)S(1)}, f32[2,256,128]{2,1,0:T(8,128)S(1)}, f32[2,256,128]{2,1,0:T(8,128)S(1)}, f32[2,256,128]{2,1,0:T(8,128)S(1)...) custom-call(f32[8,256,256]{2,1,0:T(8,128)S(1)} %copy-done, ...), custom_call_target="tpu_custom_call" | custom-call | flops 10000000 | bytes 10000000 | tf_op jit(solution)/shard_map/pallas_call | solution.py:29
  22.0 0.0 collective-permute-done.1.refs_4_
  22.0 1.1 %shard_map.106 = (f32[2,256,128]{2,1,0:T(8,128)S(1)}, f32[2,256,128]{2,1,0:T(8,128)S(1)}) custom-call(f32[8]{0:T(128)S(1)} %copy-done.2, f32[2,1808,128]{2,1,0:T(8,128)S(1)} %get-tuple-element.41.refs_1_.tm, f32[2,256,128]{2,1,0:T(8,128)S(1)} %get-tuple-element.33.refs_2_.old, f32[2,256,128]{2,1,0:T(8,128)S(1)} %get-tuple-element.34.refs_3_, ...), custom_call_target="tpu_custom_call" | custom-call | flops 2000000 | bytes 2000000 | tf_op jit(solution)/shard_map/pallas_call | solution.py:29
  23.1 2.3 %shard_map.107 = (f32[2,1808,128]{2,1,0:T(8,128)S(1)}, f32[2,256,128]{2,1,0:T(8,128)S(1)}) custom-call(f32[2,1808,128]{2,1,0:T(8,128)S(1)} %get-tuple-element.41.refs_1_.tm, f32[2,256,128]{2,1,0:T(8,128)S(1)} %get-tuple-element.33.refs_2_.old, f32[2,2,256,128]{3,2,1,0:T(8,128)S(1)} %collective-permute-done.halo, ...), custom_call_target="tpu_custom_call" | custom-call | flops 4000000 | bytes 4000000 | tf_op jit(solution)/shard_map/pallas_call | solution.py:29
  25.5 0.1 collective-permute-start.2
  25.6 1.9 %collective-permute-start.3 = (f32[2,256,128]{2,1,0:T(8,128)S(1)}, f32[2,256,128]{2,1,0:T(8,128)S(1)}, u32[]{:S(2)}, u32[]{:S(2)}) collective-permute-start(f32[2,256,128]{2,1,0:T(8,128)S(1)} %get-tuple-element.44.tb_old), channel_id=1, source_target_pairs={{1,2},{3,4},{5,6},{7,8},{9,10},{11,12},{13,14},{15,0},{2,1},{4,3},... | collective-permute-start | bytes 786440 | tf_op jit(solution)/shard_map/ppermute | solution.py:554
  27.4 0.0 collective-permute-done.2.halo
  27.4 2.5 %shard_map.108 = (f32[2,1808,128]{2,1,0:T(8,128)S(1)}, f32[2,256,128]{2,1,0:T(8,128)S(1)}) custom-call(f32[2,1808,128]{2,1,0:T(8,128)S(1)} %get-tuple-element.43.tm, f32[2,256,128]{2,1,0:T(8,128)S(1)} %get-tuple-element.44.tb_old, f32[2,256,128]{2,1,0:T(8,128)S(1)} %collective-permute-done.2.halo, f32[2,256,128]{2,1,0:T(8,128)S(1)} %get-tuple-element.42.refs_0_.gxa.refs_3_, ...), custom_call_target="tpu_custom_call" | custom-call | flops 4000000 | bytes 4000000 | tf_op jit(solution)/shard_map/pallas_call | solution.py:29
  29.9 0.1 collective-permute-start.5
  30.0 4.2 %collective-permute-done.3.halo = f32[2,256,128]{2,1,0:T(8,128)S(1)} collective-permute-done((f32[2,256,128]{2,1,0:T(8,128)S(1)}, f32[2,256,128]{2,1,0:T(8,128)S(1)}, u32[]{:S(2)}, u32[]{:S(2)}) %collective-permute-start.3) | collective-permute-done | bytes 262176 | tf_op jit(solution)/shard_map/ppermute | solution.py:554
  34.2 0.4 shard_map.109.refs_1_
  34.6 1.7 %collective-permute-start.4 = (f32[2,256,128]{2,1,0:T(8,128)S(1)}, f32[2,256,128]{2,1,0:T(8,128)S(1)}, u32[]{:S(2)}, u32[]{:S(2)}) collective-permute-start(f32[2,256,128]{2,1,0:T(8,128)S(1)} %shard_map.109.refs_1_), channel_id=1, source_target_pairs={{1,2},{3,4},{5,6},{7,8},{9,10},{11,12},{13,14},{15,0},{2,1},{4,3},... | collective-permute-start | bytes 786440 | tf_op jit(solution)/shard_map/ppermute | solution.py:554
  36.4 0.0 collective-permute-done.5.refs_2_
  36.4 0.0 copy-start.3
  36.4 0.0 copy-start.4
  36.4 5.8 %shard_map.110 = (f32[4192,128]{1,0:T(8,128)S(1)}, f32[64,128]{1,0:T(8,128)S(1)}) custom-call(f32[2,1808,128]{2,1,0:T(8,128)S(1)} %get-tuple-element.46.refs_0_, f32[2,256,128]{2,1,0:T(8,128)S(1)} %shard_map.109.refs_1_, f32[2,256,128]{2,1,0:T(8,128)S(1)} %collective-permute-done.5.refs_2_, f32[2,256,128]{2,1,0:T(8,128)S(1)} %get-tuple-element.42.refs_0_.gxa.refs_3_, ...), custom_call_target="tpu_custom_call" | custom-call | flops 10000000 | bytes 10000000 | tf_op jit(solution)/shard_map/pallas_call | solution.py:29
  42.2 1.1 %collective-permute-done.4.refs_2_ = f32[2,256,128]{2,1,0:T(8,128)S(1)} collective-permute-done((f32[2,256,128]{2,1,0:T(8,128)S(1)}, f32[2,256,128]{2,1,0:T(8,128)S(1)}, u32[]{:S(2)}, u32[]{:S(2)}) %collective-permute-start.4) | collective-permute-done | bytes 262176 | tf_op jit(solution)/shard_map/ppermute | solution.py:554
  43.3 0.0 copy-done.3
  43.3 0.0 copy-done.4
  43.3 0.0 copy-start.6
  43.3 0.0 copy-start.7
  43.3 1.9 %shard_map.111 = (f32[4192,128]{1,0:T(8,128)S(1)}, f32[64,128]{1,0:T(8,128)S(1)}, f32[16,128]{1,0:T(8,128)S(1)}) custom-call(f32[2,1808,128]{2,1,0:T(8,128)S(1)} %get-tuple-element.46.refs_0_, f32[2,256,128]{2,1,0:T(8,128)S(1)} %shard_map.109.refs_1_, f32[2,256,128]{2,1,0:T(8,128)S(1)} %collective-permute-done.4.refs_2_, ...), custom_call_target="tpu_custom_call", output_to_operand_aliasing={{0}: (12, {})} | custom-call | flops 2000000 | bytes 2000000 | tf_op jit(solution)/shard_map/pallas_call | solution.py:29
  45.2 9.3 %all_to_all.11 = f32[16,1,128]{2,1,0:T(1,128)S(1)} all-to-all(f32[16,1,128]{2,1,0:T(1,128)S(1)} %bitcast.15), channel_id=1, replica_groups=mesh['pour'=2,'brick'=16] {'brick'}, dimensions={0} | all-to-all | bytes 16384 | tf_op jit(solution)/shard_map/all_to_all | solution.py:658
  54.5 0.0 copy-done.6
  54.5 0.0 copy-done.7
  54.5 6.6 %shard_map.112 = (f32[8,256,256]{2,1,0:T(8,128)}, f32[1,32]{1,0:T(1,128)}, f32[4192,128]{1,0:T(8,128)S(1)}) custom-call(s32[64,128]{1,0:T(8,128)S(1)} %bitcast.13, f32[64,128]{1,0:T(8,128)S(1)} %get-tuple-element.51.refs_1_, f32[16,128]{1,0:T(8,128)S(1)} %bitcast.14, s32[1,32]{1,0:T(1,128)S(1)} %bitcast.17, ...), custom_call_target="tpu_custom_call", output_to_operand_aliasing={{2}: (5, {})} | custom-call | flops 2000000 | bytes 2000000 | tf_op jit(solution)/shard_map/pallas_call | solution.py:29
  (2 shorter events, 0.0 us)
Async XLA Ops:
  0.6 14.4 %copy-start = (f32[8,256,256]{2,1,0:T(8,128)S(1)}, f32[8,256,256]{2,1,0:T(8,128)}, u32[]{:S(2)}) copy-start(f32[8,256,256]{2,1,0:T(8,128)} %t_ref.3) | copy-start | bytes 6291460
  0.6 8.7 %copy-start.8 = (s32[1,32,256]{2,1,0:T(8,128)S(1)}, s32[1,32,256]{2,1,0:T(8,128)}, u32[]{:S(2)}) copy-start(s32[1,32,256]{2,1,0:T(8,128)} %param.13) | copy-start | bytes 98308
  0.7 14.4 %copy-start.2 = (f32[8]{0:T(128)S(1)}, f32[8]{0:T(128)}, u32[]{:S(2)}) copy-start(f32[8]{0:T(128)} %refs_0_.1) | copy-start | bytes 100
  0.7 14.4 %copy-start.5 = (f32[8]{0:T(128)S(1)}, f32[8]{0:T(128)}, u32[]{:S(2)}) copy-start(f32[8]{0:T(128)} %store_ref.1) | copy-start | bytes 100
  3.2 11.9 %collective-permute-start = (f32[2,2,256,128]{3,2,1,0:T(8,128)}, f32[2,2,256,128]{3,2,1,0:T(8,128)S(1)}, u32[]{:S(2)}, u32[]{:S(2)}) collective-permute-start(f32[2,2,256,128]{3,2,1,0:T(8,128)} %get-tuple-element.29), channel_id=1, source_target_pairs={{0,1},{1,0},{2,3},{3,2},{4,5},{5,4},{6,7},{7,6},{8,9},{9,8},{10,11... | collective-permute-start | bytes 1572872 | tf_op jit(solution)/shard_map/ppermute | solution.py:554
  3.7 18.3 %collective-permute-start.1 = (f32[2,2,256,128]{3,2,1,0:T(8,128)}, f32[2,2,256,128]{3,2,1,0:T(8,128)S(1)}, u32[]{:S(2)}, u32[]{:S(2)}) collective-permute-start(f32[2,2,256,128]{3,2,1,0:T(8,128)} %get-tuple-element.35), channel_id=1, source_target_pairs={{1,2},{3,4},{5,6},{7,8},{9,10},{11,12},{13,14},{15,0},{2,1},{4,3},... | collective-permute-start | bytes 1572872 | tf_op jit(solution)/shard_map/ppermute | solution.py:554
  15.1 1.6 %copy-start.1 = (s32[8,256,256]{2,1,0:T(8,128)S(1)}, s32[8,256,256]{2,1,0:T(8,128)}, u32[]{:S(2)}) copy-start(s32[8,256,256]{2,1,0:T(8,128)} %tag_ref.3) | copy-start | bytes 6291460
  25.5 1.9 %collective-permute-start.2 = (f32[2,256,128]{2,1,0:T(8,128)S(1)}, f32[2,256,128]{2,1,0:T(8,128)S(1)}, u32[]{:S(2)}, u32[]{:S(2)}) collective-permute-start(f32[2,256,128]{2,1,0:T(8,128)S(1)} %get-tuple-element.45), channel_id=1, source_target_pairs={{0,1},{1,0},{2,3},{3,2},{4,5},{5,4},{6,7},{7,6},{8,9},{9,8},{10,11... | collective-permute-start | bytes 786440 | tf_op jit(solution)/shard_map/ppermute | solution.py:554
  25.6 8.7 %collective-permute-start.3 = (f32[2,256,128]{2,1,0:T(8,128)S(1)}, f32[2,256,128]{2,1,0:T(8,128)S(1)}, u32[]{:S(2)}, u32[]{:S(2)}) collective-permute-start(f32[2,256,128]{2,1,0:T(8,128)S(1)} %get-tuple-element.44.tb_old), channel_id=1, source_target_pairs={{1,2},{3,4},{5,6},{7,8},{9,10},{11,12},{13,14},{15,0},{2,1},{4,3},... | collective-permute-start | bytes 786440 | tf_op jit(solution)/shard_map/ppermute | solution.py:554
  29.9 6.4 %collective-permute-start.5 = (f32[2,256,128]{2,1,0:T(8,128)S(1)}, f32[2,256,128]{2,1,0:T(8,128)S(1)}, u32[]{:S(2)}, u32[]{:S(2)}) collective-permute-start(f32[2,256,128]{2,1,0:T(8,128)S(1)} %get-tuple-element.48), channel_id=1, source_target_pairs={{0,1},{1,0},{2,3},{3,2},{4,5},{5,4},{6,7},{7,6},{8,9},{9,8},{10,11... | collective-permute-start | bytes 786440 | tf_op jit(solution)/shard_map/ppermute | solution.py:554
  34.6 8.7 %collective-permute-start.4 = (f32[2,256,128]{2,1,0:T(8,128)S(1)}, f32[2,256,128]{2,1,0:T(8,128)S(1)}, u32[]{:S(2)}, u32[]{:S(2)}) collective-permute-start(f32[2,256,128]{2,1,0:T(8,128)S(1)} %shard_map.109.refs_1_), channel_id=1, source_target_pairs={{1,2},{3,4},{5,6},{7,8},{9,10},{11,12},{13,14},{15,0},{2,1},{4,3},... | collective-permute-start | bytes 786440 | tf_op jit(solution)/shard_map/ppermute | solution.py:554
  36.4 6.9 %copy-start.3 = (f32[1,32]{1,0:T(1,128)S(1)}, f32[1,32]{1,0:T(1,128)}, u32[]{:S(2)}) copy-start(f32[1,32]{1,0:T(1,128)} %refs_10_.1) | copy-start | bytes 388
  36.4 6.9 %copy-start.4 = (f32[32]{0:T(128)S(1)}, f32[32]{0:T(128)}, u32[]{:S(2)}) copy-start(f32[32]{0:T(128)} %param.15) | copy-start | bytes 388
  43.3 11.2 %copy-start.6 = (s32[32]{0:T(128)S(1)}, s32[32]{0:T(128)}, u32[]{:S(2)}) copy-start(s32[32]{0:T(128)} %param.16) | copy-start | bytes 388
  43.3 11.2 %copy-start.7 = (f32[32]{0:T(128)S(1)}, f32[32]{0:T(128)}, u32[]{:S(2)}) copy-start(f32[32]{0:T(128)} %param.17) | copy-start | bytes 388

commit v6 on v5

--- a/solution.py
+++ b/solution.py
@@ -8,9 +8,10 @@
 LANES = 128
 PAD = 8
 STRIP = 16
+DEEP = 3
 WINDOW = 96
-READ_GROUP = 4
-WRITE_GROUP = 8
+READ_GROUP = 16
+WRITE_GROUP = 16
 VMEM = pl.BlockSpec(memory_space=pltpu.VMEM)
 SMEM = pl.BlockSpec(memory_space=pltpu.SMEM)
 HBM = pl.BlockSpec(memory_space=pltpu.HBM)
@@ -91,81 +92,128 @@
     return new
 
 
+def step_plane(cur, r, up, down, gx_up, gx_down, gy, ry, gz, coeff, rz, ny, emit):
+    def body(y):
+        new = advance_rows(
+            cur,
+            r + y,
+            lambda h: up(h, y),
+            lambda h: down(h, y),
+            lambda h: gx_up(h, y),
+            lambda h: gx_down(h, y),
+            gy,
+            ry + y,
+            gz,
+            coeff,
+            rz + y,
+        )
+        emit(y, new)
+
+    rows_loop(ny, body, unroll=16)
+
+
+def rows_of(ref, start=0):
+    return lambda h, y: ref[h, pl.ds(start + y, STRIP), :]
+
+
 def main_planes(cur, last, halo, gxa, gxm, gy, gz, coeff, planes, ny, emit):
     def plane(j, first, final):
-        def body(y):
-            r = PAD + j * ny + y
-            rz = j * ny + y
-
-            def down(h):
-                return halo[h, pl.ds(y, STRIP), :] if first else cur[h, pl.ds(r - ny, STRIP), :]
-
-            def gx_down(h):
-                return gxa[h, pl.ds(y, STRIP), :] if first else gxm[h, pl.ds(rz - ny, STRIP), :]
-
-            def up(h):
-                return last(h, y) if final else cur[h, pl.ds(r + ny, STRIP), :]
-
-            def gx_up(h):
-                return gxm[h, pl.ds(rz, STRIP), :]
-
-            new = advance_rows(cur, r, up, down, gx_up, gx_down, gy, PAD + rz, gz, coeff, rz)
-            emit(j, y, new, first)
-
-        rows_loop(ny, body, unroll=8)
-
-    plane(0, True, planes == 2)
+        r, rz = PAD + j * ny, j * ny
+        step_plane(
+            cur,
+            r,
+            rows_of(last) if final else rows_of(cur, r + ny),
+            halo if first else rows_of(cur, r - ny),
+            rows_of(gxm, rz),
+            rows_of(gxa) if first else rows_of(gxm, rz - ny),
+            gy,
+            PAD + rz,
+            gz,
+            coeff,
+            rz,
+            ny,
+            lambda y, new: emit(j, y, new),
+        )
 
     def inner(j, carry):
         plane(j, False, False)
         return carry
 
+    plane(0, True, planes == 2)
     lax.fori_loop(1, planes - 2, inner, 0)
     plane(planes - 2, False, True)
 
 
 def send_kernel(t_ref, tag_ref, a_ref, b_ref, tags, sem):
     planes = t_ref.shape[0]
+    parts = [(b_ref, 0, planes - 1)] + [(a_ref, k, k) for k in range(DEEP)]
     copies = []
-    for side, out in ((1, b_ref), (0, a_ref)):
-        x = plane_of(0 if side == 0 else planes - 1, planes)
+    for n, (out, k, j) in enumerate(parts):
+        x = plane_of(j, planes)
         for h in HALVES:
             part = pl.ds(h * LANES, LANES)
-            copies.append(
-                pltpu.make_async_copy(t_ref.at[x, :, part], out.at[0, h], sem.at[len(copies)])
-            )
-            copies.append(
-                pltpu.make_async_copy(tag_ref.at[x, :, part], tags.at[side, h], sem.at[len(copies)])
-            )
+            copies.append(pltpu.make_async_copy(tag_ref.at[x, :, part], tags.at[n, h], sem.at[1, n, h]))
+            copies.append(pltpu.make_async_copy(t_ref.at[x, :, part], out.at[0, k, h], sem.at[0, n, h]))
     for copy in copies:
         copy.start()
     for copy in copies:
         copy.wait()
-    for side, out in ((1, b_ref), (0, a_ref)):
-        for h in HALVES:
-            out[1, h] = tags[side, h].astype(jnp.float32)
-
-
-def prepare_kernel(t_ref, tag_ref, cond_ref, store_ref, halo, t0, tb, cond_b, gxa, gxm, gy, gz, coeff, cond):
+    for n, (out, k, j) in enumerate(parts):
+        for h in HALVES:
+            out[1, k, h] = tags[n, h].astype(jnp.float32)
+
+
+def tables(cond_ref, store_ref):
+    conds = [jnp.full((1, LANES), cond_ref[m], jnp.float32) for m in range(cond_ref.shape[0])]
+    scales = [0.16 / jnp.full((1, LANES), store_ref[m], jnp.float32) for m in range(store_ref.shape[0])]
+    return conds, scales
+
+
+def plane_faces(cond, gy, gz, planes, ny):
+    lane = lanes_iota(STRIP)
+
+    def body(r):
+        y = lax.rem(r, ny) + lax.broadcasted_iota(jnp.int32, (STRIP, LANES), 0)
+        mine = [cond[h, pl.ds(PAD + r, STRIP), :] for h in HALVES]
+        nxt = [pltpu.roll(mine[h], LANES - 1, 1) for h in HALVES]
+        ahead = [jnp.where(lane == LANES - 1, nxt[1], nxt[0]), nxt[1]]
+        prv = [pltpu.roll(mine[h], 1, 1) for h in HALVES]
+        behind = [prv[0], jnp.where(lane == 0, prv[0], prv[1])]
+        for h in HALVES:
+            below = face_mean(mine[h], cond[h, pl.ds(PAD + r + 1, STRIP), :])
+            gy[h, pl.ds(PAD + r, STRIP), :] = jnp.where(y == ny - 1, 0.0, below)
+            right = face_mean(mine[h], ahead[h])
+            gz[h, pl.ds(r, STRIP), :] = jnp.where(lane == LANES - 1, 0.0, right) if h else right
+            left = face_mean(behind[h], mine[h])
+            gz[2 + h, pl.ds(r, STRIP), :] = left if h else jnp.where(lane == 0, 0.0, left)
+
+    rows_loop(planes * ny, body, unroll=16)
+
+
+def prepare_kernel(t_ref, tag_ref, cond_ref, store_ref, t0, tb, cond_a, cond_b, gxm, gy, gz, coeff, cond, tags, sem):
     planes, ny = t_ref.shape[0], t_ref.shape[1]
+
+    def fetch(j):
+        return pltpu.make_async_copy(tag_ref.at[plane_of(j, planes)], tags.at[j], sem.at[j])
+
+    for j in range(planes):
+        fetch(j).start()
     zero = jnp.zeros((PAD, LANES), jnp.float32)
     for h in HALVES:
         for ref in (t0, cond):
             ref[h, pl.ds(0, PAD), :] = zero
             ref[h, pl.ds(ref.shape[1] - PAD, PAD), :] = zero
         gy[h, pl.ds(0, PAD), :] = zero
-    shape = (STRIP, LANES)
-    lane = lanes_iota(STRIP)
-    conds = [jnp.full((1, LANES), cond_ref[m], jnp.float32) for m in range(cond_ref.shape[0])]
-    scales = [0.16 / jnp.full((1, LANES), store_ref[m], jnp.float32) for m in range(store_ref.shape[0])]
+    conds, scales = tables(cond_ref, store_ref)
 
     def materials(j, final):
         x = plane_of(j, planes)
+        fetch(j).wait()
 
         def body(y):
             for h in HALVES:
                 part = slice(h * LANES, (h + 1) * LANES)
-                tag = tag_ref[x, pl.ds(y, STRIP), part]
+                tag = tags[j, pl.ds(y, STRIP), part]
                 kind = pick(tag, conds)
                 cond[h, pl.ds(PAD + j * ny + y, STRIP), :] = kind
                 coeff[h, pl.ds(j * ny + y, STRIP), :] = pick(tag, scales)
@@ -184,13 +232,6 @@
     lax.fori_loop(0, planes - 1, main, 0)
     materials(planes - 1, True)
 
-    def halo_face(y):
-        for h in HALVES:
-            other = pick(halo[1, h, pl.ds(y, STRIP), :].astype(jnp.int32), conds)
-            gxa[h, pl.ds(y, STRIP), :] = face_mean(cond[h, pl.ds(PAD + y, STRIP), :], other)
-
-    rows_loop(ny, halo_face)
-
     def x_faces(r):
         for h in HALVES:
             mine = cond[h, pl.ds(PAD + r, STRIP), :]
@@ -198,61 +239,58 @@
 
     rows_loop((planes - 1) * ny, x_faces)
 
-    def yz_faces(r):
-        y = lax.rem(r, ny) + lax.broadcasted_iota(jnp.int32, shape, 0)
-        mine = [cond[h, pl.ds(PAD + r, STRIP), :] for h in HALVES]
-        nxt = [pltpu.roll(mine[h], LANES - 1, 1) for h in HALVES]
-        ahead = [jnp.where(lane == LANES - 1, nxt[1], nxt[0]), nxt[1]]
-        prv = [pltpu.roll(mine[h], 1, 1) for h in HALVES]
-        behind = [prv[0], jnp.where(lane == 0, prv[0], prv[1])]
-        for h in HALVES:
-            below = face_mean(mine[h], cond[h, pl.ds(PAD + r + 1, STRIP), :])
-            gy[h, pl.ds(PAD + r, STRIP), :] = jnp.where(y == ny - 1, 0.0, below)
-            right = face_mean(mine[h], ahead[h])
-            gz[h, pl.ds(r, STRIP), :] = jnp.where(lane == LANES - 1, 0.0, right) if h else right
-            left = face_mean(behind[h], mine[h])
-            gz[2 + h, pl.ds(r, STRIP), :] = left if h else jnp.where(lane == 0, 0.0, left)
-
-    rows_loop(planes * ny, yz_faces, unroll=8)
-
-
-def last_plane(cur, below, halo, gxb, gxm, gy, gz, coeff, ny, emit):
-    rows = gz.shape[1]
-    base = rows - ny
-
-    def body(y):
-        new = advance_rows(
-            cur,
-            PAD + y,
-            lambda h: halo[h, pl.ds(y, STRIP), :],
-            lambda h: below(h, y),
-            lambda h: gxb[h, pl.ds(y, STRIP), :],
-            lambda h: gxm[h, pl.ds(base - ny + y, STRIP), :],
-            gy,
-            PAD + base + y,
-            gz,
-            coeff,
-            base + y,
-        )
-        emit(y, new)
-
-    rows_loop(ny, body, unroll=8)
-
-
-def padded(pad, rows_of, ny):
+    def first_conds(y):
+        for h in HALVES:
+            cond_a[h, pl.ds(y, STRIP), :] = cond[h, pl.ds(PAD + y, STRIP), :]
+
+    rows_loop(ny, first_conds)
+
+    plane_faces(cond, gy, gz, planes, ny)
+
+
+def clear_pads(ref):
     zero = jnp.zeros((PAD, LANES), jnp.float32)
     for h in HALVES:
-        pad[h, pl.ds(0, PAD), :] = zero
-        pad[h, pl.ds(PAD + ny, PAD), :] = zero
+        ref[h, pl.ds(0, PAD), :] = zero
+        ref[h, pl.ds(ref.shape[1] - PAD, PAD), :] = zero
+
+
+def last_plane(pad, old, below, halo, gxb, gxm, gy, gz, coeff, emit):
+    ny = gxb.shape[1]
+    base = gz.shape[1] - ny
+    clear_pads(pad)
 
     def body(y):
         for h in HALVES:
-            pad[h, pl.ds(PAD + y, STRIP), :] = rows_of(h, y)
+            pad[h, pl.ds(PAD + y, STRIP), :] = old[h, pl.ds(y, STRIP), :]
 
     rows_loop(ny, body)
-
-
-def first_last_kernel(brick_count, cond_ref, tm, tb_old, cond_b, halo, gxm, gy, gz, coeff, gxb, tb, pad):
+    step_plane(
+        pad,
+        PAD,
+        halo,
+        below,
+        rows_of(gxb),
+        rows_of(gxm, base - ny),
+        gy,
+        PAD + base,
+        gz,
+        coeff,
+        base,
+        ny,
+        emit,
+    )
+
+
+def keep_rows(ref):
+    def emit(y, new):
+        for h in HALVES:
+            ref[h, pl.ds(y, STRIP), :] = new[h]
+
+    return emit
+
+
+def first_last_kernel(brick_count, cond_ref, t0, tb_old, cond_b, halo, gxm, gy, gz, coeff, gxb, tb, pad):
     ny = tb.shape[1]
     me = lax.axis_index("brick")
     edge = (me == 0) | (me == brick_count - 1)
@@ -261,46 +299,84 @@
 
     def faces(y):
         for h in HALVES:
-            other = pick(halo[1, h, pl.ds(y, STRIP), :].astype(jnp.int32), conds)
+            other = pick(halo[1, 0, h, pl.ds(y, STRIP), :].astype(jnp.int32), conds)
             gxb[h, pl.ds(y, STRIP), :] = face_mean(cond_b[h, pl.ds(y, STRIP), :], other)
 
     rows_loop(ny, faces)
-    next_last_kernel(tm, tb_old, halo.at[0], gxb, gxm, gy, gz, coeff, tb, pad)
-
-
-def next_last_kernel(tm, tb_old, halo, gxb, gxm, gy, gz, coeff, tb, pad):
-    ny = tb.shape[1]
+    below = rows_of(t0, t0.shape[1] - PAD - ny)
+    last_plane(pad, tb_old, below, rows_of(halo.at[0, 0]), gxb, gxm, gy, gz, coeff, keep_rows(tb))
+
+
+def next_last_kernel(below, tb_old, halo, gxb, gxm, gy, gz, coeff, tb, pad):
+    last_plane(pad, tb_old, rows_of(below), rows_of(halo), gxb, gxm, gy, gz, coeff, keep_rows(tb))
+
+
+def two_steps_kernel(
+    cond_ref, store_ref, t0, tb0, tb1, cond_a, halo, gxm, gy, gz, coeff, t1_last, t2, t2_before, gxa, t1, t0x, t1x, condx, gxx, gyx, gzx, coeffx
+):
+    ny = tb0.shape[1]
     planes = gz.shape[1] // ny
-    padded(pad, lambda h, y: tb_old[h, pl.ds(y, STRIP), :], ny)
-
-    def emit(y, new):
-        for h in HALVES:
-            tb[h, pl.ds(y, STRIP), :] = new[h]
-
-    def below(h, y):
-        return tm[h, pl.ds(PAD + (planes - 2) * ny + y, STRIP), :]
-
-    last_plane(pad, below, halo, gxb, gxm, gy, gz, coeff, ny, emit)
-
-
-def next_main_kernel(tm, tb_old, halo, gxa, gxm, gy, gz, coeff, out, ta):
-    ny = ta.shape[1]
-    planes = gz.shape[1] // ny
-    zero = jnp.zeros((PAD, LANES), jnp.float32)
-    for h in HALVES:
-        out[h, pl.ds(0, PAD), :] = zero
-        out[h, pl.ds(out.shape[1] - PAD, PAD), :] = zero
-
-    def emit(j, y, new, first):
-        for h in HALVES:
-            out[h, pl.ds(PAD + j * ny + y, STRIP), :] = new[h]
-            if first:
-                ta[h, pl.ds(y, STRIP), :] = new[h]
-
-    def last(h, y):
-        return tb_old[h, pl.ds(y, STRIP), :]
-
-    main_planes(tm, last, halo, gxa, gxm, gy, gz, coeff, planes, ny, emit)
+    conds, scales = tables(cond_ref, store_ref)
+    for ref in (t0x, t1x, condx, gyx, t1, t2):
+        clear_pads(ref)
+
+    def material(k, y):
+        return [halo[1, k, h, pl.ds(y, STRIP), :].astype(jnp.int32) for h in HALVES]
+
+    def beside(y):
+        far, mid, near = material(2, y), material(1, y), material(0, y)
+        for h in HALVES:
+            kinds = [pick(far[h], conds), pick(mid[h], conds), pick(near[h], conds), cond_a[h, pl.ds(y, STRIP), :]]
+            for n, tag in enumerate((mid[h], near[h])):
+                rows = pl.ds(n * ny + y, STRIP)
+                condx[h, pl.ds(PAD + n * ny + y, STRIP), :] = kinds[n + 1]
+                coeffx[h, rows, :] = pick(tag, scales)
+                t0x[h, pl.ds(PAD + n * ny + y, STRIP), :] = halo[0, 1 - n, h, pl.ds(y, STRIP), :]
+                gxx[h, rows, :] = face_mean(kinds[n], kinds[n + 1])
+            gxa[h, pl.ds(y, STRIP), :] = face_mean(kinds[2], kinds[3])
+
+    rows_loop(ny, beside, unroll=2)
+    plane_faces(condx, gyx, gzx, 2, ny)
+
+    def beside_step(cur, n, up, down, emit):
+        step_plane(
+            cur,
+            PAD + n * ny,
+            up,
+            down,
+            rows_of(gxx, ny) if n == 0 else rows_of(gxa),
+            rows_of(gxx, n * ny),
+            gyx,
+            PAD + n * ny,
+            gzx,
+            coeffx,
+            n * ny,
+            ny,
+            emit,
+        )
+
+    def into(ref, start):
+        def emit(y, new):
+            for h in HALVES:
+                ref[h, pl.ds(start + y, STRIP), :] = new[h]
+
+        return emit
+
+    beside_step(t0x, 0, rows_of(t0x, PAD + ny), rows_of(halo.at[0, 2]), into(t1x, PAD))
+    beside_step(t0x, 1, rows_of(t0, PAD), rows_of(t0x, PAD), into(t1x, PAD + ny))
+    main_planes(
+        t0, tb0, rows_of(t0x, PAD + ny), gxa, gxm, gy, gz, coeff, planes, ny, lambda j, y, new: into(t1, PAD + j * ny)(y, new)
+    )
+
+    def out_last(y):
+        for h in HALVES:
+            t1_last[h, pl.ds(y, STRIP), :] = t1[h, pl.ds(PAD + (planes - 2) * ny + y, STRIP), :]
+
+    rows_loop(ny, out_last)
+    beside_step(t1x, 1, rows_of(t1, PAD), rows_of(t1x, PAD), keep_rows(t2_before))
+    main_planes(
+        t1, tb1, rows_of(t1x, PAD + ny), gxa, gxm, gy, gz, coeff, planes, ny, lambda j, y, new: into(t2, PAD + j * ny)(y, new)
+    )
 
 
 def unpack(packed, ordered, row_of, col_of, sem, half):
@@ -394,14 +470,11 @@
     planes = rows // ny
     copy = unpack(packed, ordered, row_of, col_of, sem, rows)
 
-    def emit(j, y, new, first):
+    def emit(j, y, new):
         for h in HALVES:
             heat[pl.ds((2 * j + h) * ny + y, STRIP), :] = new[h]
 
-    def last(h, y):
-        return tb_old[h, pl.ds(y, STRIP), :]
-
-    main_planes(tm, last, halo, gxa, gxm, gy, gz, coeff, planes, ny, emit)
+    main_planes(tm, tb_old, rows_of(halo), gxa, gxm, gy, gz, coeff, planes, ny, emit)
     heat[pl.ds(2 * rows, WINDOW), :] = jnp.zeros((WINDOW, LANES), jnp.float32)
     heat[pl.ds(2 * (rows - ny), 2 * ny), :] = jnp.zeros((2 * ny, LANES), jnp.float32)
     found[...] = jnp.zeros_like(found)
@@ -418,16 +491,13 @@
     planes = rows // ny
     lines = film.shape[1]
     copy = unpack(packed, ordered, row_of, col_of, sem, rows)
-    padded(pad, lambda h, y: tb_old[h, pl.ds(y, STRIP), :], ny)
 
     def emit(y, new):
         for h in HALVES:
             heat[pl.ds((2 * (planes - 1) + h) * ny + y, STRIP), :] = new[h]
 
-    def below(h, y):
-        return tm[h, pl.ds(PAD + (planes - 2) * ny + y, STRIP), :]
-
-    last_plane(pad, below, halo, gxb, gxm, gy, gz, coeff, ny, emit)
+    below = rows_of(tm, PAD + (planes - 2) * ny)
+    last_plane(pad, tb_old, below, rows_of(halo), gxb, gxm, gy, gz, coeff, emit)
     found[...] = found_in[...]
     copy.wait()
     early = early_groups(ordered, 2 * (rows - ny), rows)
@@ -546,26 +616,32 @@
     rows, hits = planes * ny, lines * wall
     count = lax.axis_size("brick")
     dma = pltpu.SemaphoreType.DMA
-    on_chip = [(i, i ^ 1) for i in range(count)]
-    across = [(i, (i + 1) % count) for i in range(1, count, 2)]
-    across = across + [(b, a) for a, b in across]
+    axes = ("pour", "brick")
+    pours = lax.axis_size("pour")
+    on_chip, across = [], []
+    for p in range(pours):
+        for i in range(count):
+            on_chip.append((p * count + i, p * count + (i ^ 1)))
+            to = i + 1 if i % 2 else i - 1
+            other = p ^ 1 if (p ^ 1) < pours else p
+            inside = 0 <= to < count
+            across.append((p * count + i, p * count + to if inside else other * count + i))
 
     def swap(value, pairs):
-        return lax.ppermute(value, "brick", pairs)
-
-    temperatures, tags = initial_voxel_degrees, alloy_tag_per_voxel
+        return lax.ppermute(value, axes, pairs)
+
+    temperatures = initial_voxel_degrees
     initial_voxel_degrees = pltpu.with_memory_space_constraint(initial_voxel_degrees, pltpu.HBM)
     alloy_tag_per_voxel = pltpu.with_memory_space_constraint(alloy_tag_per_voxel, pltpu.HBM)
 
     plane = f32(2, ny, LANES)
-    pair = f32(2, 2, ny, LANES)
     ta, tb = call(
         send_kernel,
         (initial_voxel_degrees, alloy_tag_per_voxel),
         [HBM, HBM],
-        (pair, pair),
+        (f32(2, DEEP, 2, ny, LANES), f32(2, 1, 2, ny, LANES)),
         (VMEM, VMEM),
-        [pltpu.VMEM((2, 2, ny, LANES), jnp.int32), dma((8,))],
+        [pltpu.VMEM((DEEP + 1, 2, ny, LANES), jnp.int32), dma((2, DEEP + 1, 2))],
     )
     halo_b = swap(tb, across)
     halo_a = swap(ta, on_chip)
@@ -575,22 +651,25 @@
     row = (cell // (ny * nz) * 2 + (cell // LANES) % 2) * ny + (cell // nz) % ny
     cell = (row * LANES + cell % LANES) ^ (rows * LANES)
     packed = lax.sort(cell * 8192 + lax.iota(jnp.int32, hits), is_stable=False)
-    halo_a, packed = lax.optimization_barrier((halo_a, packed))
+    specific_storage_per_alloy, packed = lax.optimization_barrier((specific_storage_per_alloy, packed))
     packed = packed.reshape(hits // LANES, LANES)
 
     full = f32(2, rows + 2 * PAD, LANES)
     most = f32(2, rows - ny + 2 * PAD, LANES)
-    t0, tb0, cond_b, gxa, gxm, gy, gz, coeff = call(
+    t0, tb0, cond_a, cond_b, gxm, gy, gz, coeff = call(
         prepare_kernel,
-        (temperatures, tags, thermal_conductance_per_alloy, specific_storage_per_alloy, halo_a),
-        [VMEM, VMEM, SMEM, SMEM, VMEM],
+        (temperatures, alloy_tag_per_voxel, thermal_conductance_per_alloy, specific_storage_per_alloy),
+        [VMEM, HBM, SMEM, SMEM],
         (most, plane, plane, plane, f32(2, rows - ny, LANES), full, f32(4, rows, LANES), f32(2, rows, LANES)),
         (VMEM,) * 8,
-        [pltpu.VMEM((2, rows + 2 * PAD, LANES), jnp.float32)],
-        cost=10_000_000,
+        [
+            pltpu.VMEM((2, rows + 2 * PAD, LANES), jnp.float32),
+            pltpu.VMEM((planes, ny, nz), jnp.int32),
+            dma((planes,)),
+        ],
     )
     pad = pltpu.VMEM((2, ny + 2 * PAD, LANES), jnp.float32)
-    gxb, tb = call(
+    gxb, tb1 = call(
         lambda *refs: first_last_kernel(count, *refs),
         (thermal_conductance_per_alloy, t0, tb0, cond_b, halo_b, gxm, gy, gz, coeff),
         [SMEM] + [VMEM] * 8,
@@ -598,36 +677,35 @@
         (VMEM, VMEM),
         [pad],
     )
-    tb, t0 = lax.optimization_barrier((tb, t0))
-    halo_b = swap(tb, across)
-    t1, ta = call(
-        lambda tm, old, halo, *refs: next_main_kernel(tm, old, halo.at[0], *refs),
-        (t0, tb0, halo_a, gxa, gxm, gy, gz, coeff),
-        [VMEM] * 8,
-        (most, plane),
-        (VMEM, VMEM),
-        cost=4_000_000,
-    )
-    halo_a = swap(ta, on_chip)
-
-    t2, ta = call(
-        next_main_kernel,
-        (t1, tb, halo_a, gxa, gxm, gy, gz, coeff),
-        [VMEM] * 8,
-        (most, plane),
-        (VMEM, VMEM),
-        cost=4_000_000,
+    halo_b = swap(tb1, across)
+    two = pltpu.VMEM((2, 2 * ny + 2 * PAD, LANES), jnp.float32)
+    flat = pltpu.VMEM((2, 2 * ny, LANES), jnp.float32)
+    t1_last, t2, t2_before, gxa = call(
+        two_steps_kernel,
+        (thermal_conductance_per_alloy, specific_storage_per_alloy, t0, tb0, tb1, cond_a, halo_a, gxm, gy, gz, coeff),
+        [SMEM, SMEM] + [VMEM] * 9,
+        (plane, most, plane, plane),
+        (VMEM,) * 4,
+        [
+            pltpu.VMEM(most.shape, jnp.float32),
+            two,
+            two,
+            two,
+            flat,
+            two,
+            pltpu.VMEM((4, 2 * ny, LANES), jnp.float32),
+            flat,
+        ],
     )
     tb2 = call(
         next_last_kernel,
-        (t1, tb, halo_b, gxb, gxm, gy, gz, coeff),
+        (t1_last, tb1, halo_b, gxb, gxm, gy, gz, coeff),
         [VMEM] * 8,
         plane,
         VMEM,
         [pad],
     )
     halo_b = swap(tb2, across)
-    halo_a = swap(ta, on_chip)
 
     depth = hits // LANES
     listing = [
@@ -638,7 +716,7 @@
     ]
     heat, found = call(
         lambda *refs: final_main_kernel(*refs),
-        (t2, tb2, halo_a, gxa, gxm, gy, gz, coeff, packed),
+        (t2, tb2, t2_before, gxa, gxm, gy, gz, coeff, packed),
         [VMEM] * 9,
         (f32(2 * rows + WINDOW, LANES), f32(depth, LANES)),
         (VMEM, VMEM),

time: 61.4 us -> 57.5 us (0.936)
  blocking collectives: 9.27 us -> 16 us
  starting transfers between devices: 9.93 us -> 5.24 us
  waiting for transfers between devices: 5.36 us -> 1.16 us
  local copies, waits for them, and re-layouts: 1.64 us -> 0.05 us
    all_to_all x1, blocking collectives: 9.27 us -> 16 us  [per_device(): rows_all = lax.all_to_all(send, 'brick', 0, 0, tiled=True)]
    ppermute x6 -> x4, starting transfers between devices: 9.93 us -> 5.24 us  [swap(): return lax.ppermute(value, axes, pairs)]
    ppermute x6 -> x4, waiting for transfers between devices: 5.36 us -> 1.16 us  [swap(): return lax.ppermute(value, axes, pairs)]
    unnamed x19 -> x17, local copies, waits for them, and re-layouts: 1.64 us -> 0.05 us
    pallas_call x9 -> x8, Pallas kernels: 28.4 us -> 28.3 us  [call(): pl.pallas_call(kernel, out_shape=out_shape, in_specs=in_specs, out_specs=...]
  transfers between devices with their start and end apart: 6 -> 4, of which waited for: 2 -> 1; matrix products, arithmetic and copies ran while one was open for 9% -> 10% of each run, Pallas kernels for 23% -> 30%
where the time goes in v6:
time: 57.5 us; the launch traced here: 57.3 us
  Pallas kernels  28.3 us (49%)
  blocking collectives  16 us (28%)
  other arithmetic  5.69 us (10%)
  starting transfers between devices  5.24 us (9%)
  waiting for transfers between devices  1.16 us (2%)
  between operations  0.77 us (1%)
    pallas_call x8, Pallas kernels, call(): pl.pallas_call(kernel, out_shape=out_shape, in_specs=in_specs, out_specs=...  28.3 us
    all_to_all x1, blocking collectives, per_device(): rows_all = lax.all_to_all(send, 'brick', 0, 0, tiled=True)  16 us
    sort x1, other arithmetic, per_device(): packed = lax.sort(cell * 8192 + lax.iota(jnp.int32, hits), is_stable=False)  5.59 us
    ppermute x4, starting transfers between devices, swap(): return lax.ppermute(value, axes, pairs)  5.24 us
    ppermute x4, waiting for transfers between devices, swap(): return lax.ppermute(value, axes, pairs)  1.16 us
  transfers between devices with their start and end apart: 4, of which 1 were waited for; matrix products, arithmetic and copies ran while one was open for 10% of the time, Pallas kernels for 30%

profile of v6, /device:TPU:0, one launch (start us, length us, event | category | flops | bytes accessed | tf_op | source)
XLA Modules:
  0.0 57.3 jit_solution(1764373447123005019)
XLA Ops:
  0.6 0.0 copy-start
  0.6 0.0 copy-start.7
  0.7 0.0 copy-start.2
  0.7 0.0 copy-start.1
  0.7 3.1 %shard_map.105 = (f32[2,3,2,256,128]{4,3,2,1,0:T(8,128)}, f32[2,1,2,256,128]{4,3,2,1,0:T(8,128)S(1)}) custom-call(f32[8,256,256]{2,1,0:T(8,128)} %t_ref.3, s32[8,256,256]{2,1,0:T(8,128)} %tag_ref.3), custom_call_target="tpu_custom_call" | custom-call | flops 2000000 | bytes 2000000 | tf_op jit(solution)/shard_map/pallas_call | solution.py:30
  3.8 0.5 collective-permute-start.1
  4.3 2.6 %collective-permute-start = (f32[2,1,2,256,128]{4,3,2,1,0:T(8,128)S(1)}, f32[2,1,2,256,128]{4,3,2,1,0:T(8,128)S(1)}, u32[]{:S(2)}, u32[]{:S(2)}) collective-permute-start(f32[2,1,2,256,128]{4,3,2,1,0:T(8,128)S(1)} %get-tuple-element.32), channel_id=1, source_target_pairs={{0,16},{1,2},{2,1},{3,4},{4,3},{5,6},{6,5},{7,8},{8,7},{9,10},{10,... | collective-permute-start | bytes 1572872 | tf_op jit(solution)/shard_map/ppermute | solution.py:631
  6.8 0.0 copy-done.7
  6.9 0.1 fusion.9
  7.0 5.6 %sort.7 = s32[8192]{0:T(1024)S(1)} sort(s32[8192]{0:T(1024)S(1)} %fusion.9), dimensions={0}, to_apply=%region_0.1 | sort | flops 106496 | bytes 65536 | tf_op jit(solution)/shard_map/sort | solution.py:653
  12.6 0.0 copy-done
  12.6 0.0 copy-done.2
  12.6 0.0 copy-done.1
  12.6 5.6 %shard_map.104 = (f32[2,1808,128]{2,1,0:T(8,128)S(1)}, f32[2,256,128]{2,1,0:T(8,128)S(1)}, f32[2,256,128]{2,1,0:T(8,128)S(1)}, f32[2,256,128]{2,1,0:T(8,128)S(1)...) custom-call(f32[8,256,256]{2,1,0:T(8,128)S(1)} %copy-done, ...), custom_call_target="tpu_custom_call" | custom-call | flops 2000000 | bytes 2000000 | tf_op jit(solution)/shard_map/pallas_call | solution.py:30
  18.2 0.0 collective-permute-done.refs_4_
  18.2 1.1 %shard_map.106 = (f32[2,256,128]{2,1,0:T(8,128)S(1)}, f32[2,256,128]{2,1,0:T(8,128)S(1)}) custom-call(f32[8]{0:T(128)S(1)} %copy-done.1, f32[2,1808,128]{2,1,0:T(8,128)S(1)} %get-tuple-element.29.refs_1_.t0, f32[2,256,128]{2,1,0:T(8,128)S(1)} %get-tuple-element.30.refs_2_.tb0, f32[2,256,128]{2,1,0:T(8,128)S(1)} %get-tuple-element.31.refs_3_, ...), custom_call_target="tpu_custom_call" | custom-call | flops 2000000 | bytes 2000000 | tf_op jit(solution)/shard_map/pallas_call | solution.py:30
  19.3 0.1 collective-permute-start.2
  19.4 0.0 collective-permute-done.1.halo
  19.4 7.1 %shard_map.107 = (f32[2,256,128]{2,1,0:T(8,128)S(1)}, f32[2,1808,128]{2,1,0:T(8,128)S(1)}, f32[2,256,128]{2,1,0:T(8,128)S(1)}, f32[2,256,128]{2,1,0:T(8,128)S(1)}) custom-call(f32[8]{0:T(128)S(1)} %copy-done.1, f32[8]{0:T(128)S(1)} %copy-done.2, f32[2,1808,128]{2,1,0:T(8,128)S(1)} %get-tuple-element.29.refs_1_.t0, ...), custom_call_target="tpu_custom_call" | custom-call | flops 2000000 | bytes 2000000 | tf_op jit(solution)/shard_map/pallas_call | solution.py:30
  26.5 0.0 collective-permute-done.2.halo
  26.5 0.3 shard_map.108.refs_1_
  26.8 2.1 %collective-permute-start.3 = (f32[2,256,128]{2,1,0:T(8,128)S(1)}, f32[2,256,128]{2,1,0:T(8,128)S(1)}, u32[]{:S(2)}, u32[]{:S(2)}) collective-permute-start(f32[2,256,128]{2,1,0:T(8,128)S(1)} %shard_map.108.refs_1_), channel_id=1, source_target_pairs={{0,16},{1,2},{2,1},{3,4},{4,3},{5,6},{6,5},{7,8},{8,7},{9,10},{10,... | collective-permute-start | bytes 786440 | tf_op jit(solution)/shard_map/ppermute | solution.py:631
  28.9 0.0 copy-start.3
  28.9 0.0 copy-start.4
  28.9 3.2 %shard_map.109 = (f32[4192,128]{1,0:T(8,128)S(1)}, f32[64,128]{1,0:T(8,128)S(1)}) custom-call(f32[2,1808,128]{2,1,0:T(8,128)S(1)} %get-tuple-element.40.refs_0_, f32[2,256,128]{2,1,0:T(8,128)S(1)} %shard_map.108.refs_1_, f32[2,256,128]{2,1,0:T(8,128)S(1)} %get-tuple-element.43.refs_2_, f32[2,256,128]{2,1,0:T(8,128)S(1)} %get-tuple-element.44.refs_3_, ...), custom_call_target="tpu_custom_call" | custom-call | flops 10000000 | bytes 10000000 | tf_op jit(solution)/shard_map/pallas_call | solution.py:30
  32.1 1.1 %collective-permute-done.3.refs_2_ = f32[2,256,128]{2,1,0:T(8,128)S(1)} collective-permute-done((f32[2,256,128]{2,1,0:T(8,128)S(1)}, f32[2,256,128]{2,1,0:T(8,128)S(1)}, u32[]{:S(2)}, u32[]{:S(2)}) %collective-permute-start.3) | collective-permute-done | bytes 262176 | tf_op jit(solution)/shard_map/ppermute | solution.py:631
  33.2 0.0 copy-done.3
  33.2 0.0 copy-done.4
  33.2 0.0 copy-start.5
  33.2 0.0 copy-start.6
  33.3 1.9 %shard_map.110 = (f32[4192,128]{1,0:T(8,128)S(1)}, f32[64,128]{1,0:T(8,128)S(1)}, f32[16,128]{1,0:T(8,128)S(1)}) custom-call(f32[2,1808,128]{2,1,0:T(8,128)S(1)} %get-tuple-element.40.refs_0_, f32[2,256,128]{2,1,0:T(8,128)S(1)} %shard_map.108.refs_1_, f32[2,256,128]{2,1,0:T(8,128)S(1)} %collective-permute-done.3.refs_2_, ...), custom_call_target="tpu_custom_call", output_to_operand_aliasing={{0}: (12, {})} | custom-call | flops 2000000 | bytes 2000000 | tf_op jit(solution)/shard_map/pallas_call | solution.py:30
  35.2 16.0 %all_to_all.11 = f32[16,1,128]{2,1,0:T(1,128)S(1)} all-to-all(f32[16,1,128]{2,1,0:T(1,128)S(1)} %bitcast.15), channel_id=1, replica_groups=mesh['pour'=2,'brick'=16] {'brick'}, dimensions={0} | all-to-all | bytes 16384 | tf_op jit(solution)/shard_map/all_to_all | solution.py:736
  51.2 0.0 copy-done.5
  51.2 0.0 copy-done.6
  51.2 6.1 %shard_map.111 = (f32[8,256,256]{2,1,0:T(8,128)}, f32[1,32]{1,0:T(1,128)}, f32[4192,128]{1,0:T(8,128)S(1)}) custom-call(s32[64,128]{1,0:T(8,128)S(1)} %bitcast.13, f32[64,128]{1,0:T(8,128)S(1)} %get-tuple-element.47.refs_1_, f32[16,128]{1,0:T(8,128)S(1)} %bitcast.14, s32[1,32]{1,0:T(1,128)S(1)} %bitcast.17, ...), custom_call_target="tpu_custom_call", output_to_operand_aliasing={{2}: (5, {})} | custom-call | flops 2000000 | bytes 2000000 | tf_op jit(solution)/shard_map/pallas_call | solution.py:30
  (2 shorter events, 0.0 us)
Async XLA Ops:
  0.6 11.9 %copy-start = (f32[8,256,256]{2,1,0:T(8,128)S(1)}, f32[8,256,256]{2,1,0:T(8,128)}, u32[]{:S(2)}) copy-start(f32[8,256,256]{2,1,0:T(8,128)} %t_ref.3) | copy-start | bytes 6291460
  0.6 6.2 %copy-start.7 = (s32[1,32,256]{2,1,0:T(8,128)S(1)}, s32[1,32,256]{2,1,0:T(8,128)}, u32[]{:S(2)}) copy-start(s32[1,32,256]{2,1,0:T(8,128)} %param.13) | copy-start | bytes 98308
  0.7 11.9 %copy-start.2 = (f32[8]{0:T(128)S(1)}, f32[8]{0:T(128)}, u32[]{:S(2)}) copy-start(f32[8]{0:T(128)} %store_ref.1) | copy-start | bytes 100
  0.7 11.9 %copy-start.1 = (f32[8]{0:T(128)S(1)}, f32[8]{0:T(128)}, u32[]{:S(2)}) copy-start(f32[8]{0:T(128)} %cond_ref.3) | copy-start | bytes 100
  3.8 15.6 %collective-permute-start.1 = (f32[2,3,2,256,128]{4,3,2,1,0:T(8,128)}, f32[2,3,2,256,128]{4,3,2,1,0:T(8,128)}, u32[]{:S(2)}, u32[]{:S(2)}) collective-permute-start(f32[2,3,2,256,128]{4,3,2,1,0:T(8,128)} %get-tuple-element.39), channel_id=1, source_target_pairs={{0,1},{1,0},{2,3},{3,2},{4,5},{5,4},{6,7},{7,6},{8,9},{9,8},{10,11... | collective-permute-start | bytes 4718600 | tf_op jit(solution)/shard_map/ppermute | solution.py:631
  4.3 13.9 %collective-permute-start = (f32[2,1,2,256,128]{4,3,2,1,0:T(8,128)S(1)}, f32[2,1,2,256,128]{4,3,2,1,0:T(8,128)S(1)}, u32[]{:S(2)}, u32[]{:S(2)}) collective-permute-start(f32[2,1,2,256,128]{4,3,2,1,0:T(8,128)S(1)} %get-tuple-element.32), channel_id=1, source_target_pairs={{0,16},{1,2},{2,1},{3,4},{4,3},{5,6},{6,5},{7,8},{8,7},{9,10},{10,... | collective-permute-start | bytes 1572872 | tf_op jit(solution)/shard_map/ppermute | solution.py:631
  19.3 7.2 %collective-permute-start.2 = (f32[2,256,128]{2,1,0:T(8,128)S(1)}, f32[2,256,128]{2,1,0:T(8,128)S(1)}, u32[]{:S(2)}, u32[]{:S(2)}) collective-permute-start(f32[2,256,128]{2,1,0:T(8,128)S(1)} %get-tuple-element.37.tb1.tb_old), channel_id=1, source_target_pairs={{0,16},{1,2},{2,1},{3,4},{4,3},{5,6},{6,5},{7,8},{8,7},{9,10},{10,... | collective-permute-start | bytes 786440 | tf_op jit(solution)/shard_map/ppermute | solution.py:631
  26.8 6.4 %collective-permute-start.3 = (f32[2,256,128]{2,1,0:T(8,128)S(1)}, f32[2,256,128]{2,1,0:T(8,128)S(1)}, u32[]{:S(2)}, u32[]{:S(2)}) collective-permute-start(f32[2,256,128]{2,1,0:T(8,128)S(1)} %shard_map.108.refs_1_), channel_id=1, source_target_pairs={{0,16},{1,2},{2,1},{3,4},{4,3},{5,6},{6,5},{7,8},{8,7},{9,10},{10,... | collective-permute-start | bytes 786440 | tf_op jit(solution)/shard_map/ppermute | solution.py:631
  28.9 4.4 %copy-start.3 = (f32[1,32]{1,0:T(1,128)S(1)}, f32[1,32]{1,0:T(1,128)}, u32[]{:S(2)}) copy-start(f32[1,32]{1,0:T(1,128)} %refs_10_.1) | copy-start | bytes 388
  28.9 4.4 %copy-start.4 = (f32[32]{0:T(128)S(1)}, f32[32]{0:T(128)}, u32[]{:S(2)}) copy-start(f32[32]{0:T(128)} %param.15) | copy-start | bytes 388
  33.2 17.9 %copy-start.5 = (s32[32]{0:T(128)S(1)}, s32[32]{0:T(128)}, u32[]{:S(2)}) copy-start(s32[32]{0:T(128)} %param.16) | copy-start | bytes 388
  33.2 17.9 %copy-start.6 = (f32[32]{0:T(128)S(1)}, f32[32]{0:T(128)}, u32[]{:S(2)}) copy-start(f32[32]{0:T(128)} %param.17) | copy-start | bytes 388

commit v7 on v6

--- a/solution.py
+++ b/solution.py
@@ -156,9 +156,9 @@
             copies.append(pltpu.make_async_copy(t_ref.at[x, :, part], out.at[0, k, h], sem.at[0, n, h]))
     for copy in copies:
         copy.start()
-    for copy in copies:
-        copy.wait()
     for n, (out, k, j) in enumerate(parts):
+        for copy in copies[4 * n : 4 * n + 4]:
+            copy.wait()
         for h in HALVES:
             out[1, k, h] = tags[n, h].astype(jnp.float32)
 
@@ -190,14 +190,23 @@
     rows_loop(planes * ny, body, unroll=16)
 
 
-def prepare_kernel(t_ref, tag_ref, cond_ref, store_ref, t0, tb, cond_a, cond_b, gxm, gy, gz, coeff, cond, tags, sem):
+def prepare_kernel(t_ref, tag_ref, cond_ref, store_ref, t0, tb, cond_a, cond_b, gxm, gy, gz, coeff, cond, tags, sem, sems):
     planes, ny = t_ref.shape[0], t_ref.shape[1]
 
     def fetch(j):
         return pltpu.make_async_copy(tag_ref.at[plane_of(j, planes)], tags.at[j], sem.at[j])
 
+    def bring(j):
+        x = plane_of(j, planes)
+        for h in HALVES:
+            to = tb.at[h] if j == planes - 1 else t0.at[h, pl.ds(PAD + j * ny, ny)]
+            yield pltpu.make_async_copy(t_ref.at[x, :, pl.ds(h * LANES, LANES)], to, sems.at[j, h])
+
     for j in range(planes):
         fetch(j).start()
+    for j in range(planes):
+        for copy in bring(j):
+            copy.start()
     zero = jnp.zeros((PAD, LANES), jnp.float32)
     for h in HALVES:
         for ref in (t0, cond):
@@ -207,7 +216,6 @@
     conds, scales = tables(cond_ref, store_ref)
 
     def materials(j, final):
-        x = plane_of(j, planes)
         fetch(j).wait()
 
         def body(y):
@@ -219,9 +227,6 @@
                 coeff[h, pl.ds(j * ny + y, STRIP), :] = pick(tag, scales)
                 if final:
                     cond_b[h, pl.ds(y, STRIP), :] = kind
-                    tb[h, pl.ds(y, STRIP), :] = t_ref[x, pl.ds(y, STRIP), part]
-                else:
-                    t0[h, pl.ds(PAD + j * ny + y, STRIP), :] = t_ref[x, pl.ds(y, STRIP), part]
 
         rows_loop(ny, body)
 
@@ -246,6 +251,9 @@
     rows_loop(ny, first_conds)
 
     plane_faces(cond, gy, gz, planes, ny)
+    for j in range(planes):
+        for copy in bring(j):
+            copy.wait()
 
 
 def clear_pads(ref):
@@ -379,12 +387,10 @@
     )
 
 
-def unpack(packed, ordered, row_of, col_of, sem, half):
+def unpack(packed, ordered, row_of, sem, half):
     copy = pltpu.make_async_copy(packed, ordered, sem)
     copy.start()
-    one = packed[...]
-    row_of[...] = lax.shift_right_arithmetic(one, 20) + half
-    col_of[...] = lax.shift_right_logical(one, 13) & (LANES - 1)
+    row_of[...] = lax.shift_right_arithmetic(packed[...], 20) + half
     return copy
 
 
@@ -437,12 +443,26 @@
     return high, (x - high.astype(jnp.float32)).astype(jnp.bfloat16)
 
 
-def read_walls(first, last, ordered, row_of, col_of, heat, found, half):
+def lane_masks(col_of, masks):
+    square = lax.broadcasted_iota(jnp.int32, (LANES, LANES), 0)
+
+    def turn(c, carry):
+        mask = jnp.where(square == col_of[pl.ds(c, 1), :], 1.0, 0.0)
+        masks[pl.ds(pl.multiple_of(c * LANES, LANES), LANES), :] = mask.astype(jnp.bfloat16)
+        return carry
+
+    lax.fori_loop(0, col_of.shape[0], turn, 0, unroll=8)
+
+
+def mask_of(masks, c):
+    return masks[pl.ds(pl.multiple_of(c * LANES, LANES), LANES), :]
+
+
+def read_walls(first, last, ordered, row_of, masks, heat, found, half):
     tall = lax.broadcasted_iota(jnp.int32, (WINDOW, LANES), 0)
-    square = lax.broadcasted_iota(jnp.int32, (LANES, LANES), 0)
 
     def work(c, base):
-        lanes = jnp.where(square == col_of[pl.ds(c, 1), :], 1.0, 0.0).astype(jnp.bfloat16)
+        lanes = mask_of(masks, c)
         high, low = split(heat[pl.ds(base, WINDOW), :])
         values = jnp.dot(high, lanes, preferred_element_type=jnp.float32)
         values = values + jnp.dot(low, lanes, preferred_element_type=jnp.float32)
@@ -464,11 +484,11 @@
     return count
 
 
-def final_main_kernel(tm, tb_old, halo, gxa, gxm, gy, gz, coeff, packed, heat, found, ordered, row_of, col_of, sem):
+def final_main_kernel(tm, tb_old, halo, gxa, gxm, gy, gz, coeff, packed, heat, found, masks, ordered, row_of, sem, col_of):
     ny = tb_old.shape[1]
     rows = gz.shape[1]
     planes = rows // ny
-    copy = unpack(packed, ordered, row_of, col_of, sem, rows)
+    copy = unpack(packed, ordered, row_of, sem, rows)
 
     def emit(j, y, new):
         for h in HALVES:
@@ -478,19 +498,21 @@
     heat[pl.ds(2 * rows, WINDOW), :] = jnp.zeros((WINDOW, LANES), jnp.float32)
     heat[pl.ds(2 * (rows - ny), 2 * ny), :] = jnp.zeros((2 * ny, LANES), jnp.float32)
     found[...] = jnp.zeros_like(found)
+    col_of[...] = lax.shift_right_logical(packed[...], 13) & (LANES - 1)
+    lane_masks(col_of, masks)
     copy.wait()
     early = early_groups(ordered, 2 * (rows - ny), rows)
-    read_walls(0, early, ordered, row_of, col_of, heat, found, rows)
+    read_walls(0, early, ordered, row_of, masks, heat, found, rows)
 
 
 def walls_kernel(
-    wall, tm, tb_old, halo, gxb, gxm, gy, gz, coeff, packed, found_in, film, ratio, heat_in, heat, found, send, pad, sums, ordered, row_of, col_of, sem
+    wall, tm, tb_old, halo, gxb, gxm, gy, gz, coeff, packed, masks, found_in, film, ratio, heat_in, heat, found, send, pad, sums, ordered, row_of, sem
 ):
     ny = tb_old.shape[1]
     rows = gz.shape[1]
     planes = rows // ny
     lines = film.shape[1]
-    copy = unpack(packed, ordered, row_of, col_of, sem, rows)
+    copy = unpack(packed, ordered, row_of, sem, rows)
 
     def emit(y, new):
         for h in HALVES:
@@ -501,7 +523,7 @@
     found[...] = found_in[...]
     copy.wait()
     early = early_groups(ordered, 2 * (rows - ny), rows)
-    read_walls(early, ordered.shape[0] // READ_GROUP, ordered, row_of, col_of, heat, found, rows)
+    read_walls(early, ordered.shape[0] // READ_GROUP, ordered, row_of, masks, heat, found, rows)
     owner = line_of(packed[...], wall)
     hot = found[...]
     for k in range(lines):
@@ -523,13 +545,13 @@
 
 
 def finish_kernel(
-    wall, packed, found, rows_all, direction, entry, heat_in, out, mid, heat, gains, table, change, ordered, row_of, col_of, sem, sems
+    wall, packed, masks, found, rows_all, direction, entry, heat_in, out, mid, heat, gains, table, high, low, ordered, row_of, sem, sems
 ):
     planes, ny = out.shape[0], out.shape[1]
     rows = planes * ny
     count, lines = rows_all.shape[0], mid.shape[1]
     me = lax.axis_index("brick")
-    copy = unpack(packed, ordered, row_of, col_of, sem, rows)
+    copy = unpack(packed, ordered, row_of, sem, rows)
 
     def pass_on(k, water):
         return rows_all[pl.ds(k, 1), :] * water + gains[pl.ds(k, 1), :]
@@ -548,23 +570,27 @@
     table[1:2, 0:lines] = coolant
     pull = jnp.broadcast_to(table[0:1, :], (8, LANES))
     cool = jnp.broadcast_to(table[1:2, :], (8, LANES))
-    depth = change.shape[0]
+    depth = high.shape[0]
     for k in range(0, depth, 8):
         owner = line_of(packed[k : k + 8, :], wall)
         a = jnp.take_along_axis(pull, owner, axis=1)
         c = jnp.take_along_axis(cool, owner, axis=1)
-        change[k : k + 8, :] = a * (c - found[k : k + 8, :])
+        change = a * (c - found[k : k + 8, :])
+        first = change.astype(jnp.bfloat16).astype(jnp.float32)
+        high[k : k + 8, :] = first
+        low[k : k + 8, :] = change - first
     tall = lax.broadcasted_iota(jnp.int32, (WINDOW, LANES), 0)
-    square = lax.broadcasted_iota(jnp.int32, (LANES, LANES), 0)
 
     def work(c, base):
-        at = jnp.where(tall == row_of[pl.ds(c, 1), :] - base, 1.0, 0.0).astype(jnp.bfloat16)
-        amount = jnp.where(square == col_of[pl.ds(c, 1), :], change[pl.ds(c, 1), :], 0.0)
-        high, low = split(amount)
-        dims = (((1,), (1,)), ((), ()))
-        return lax.dot_general(at, high, dims, preferred_element_type=jnp.float32) + lax.dot_general(
-            at, low, dims, preferred_element_type=jnp.float32
+        here = tall == row_of[pl.ds(c, 1), :] - base
+        pieces = [jnp.where(here, ref[pl.ds(c, 1), :], 0.0).astype(jnp.bfloat16) for ref in (high, low)]
+        both = lax.dot_general(
+            jnp.concatenate(pieces, axis=0),
+            mask_of(masks, c),
+            (((1,), (1,)), ((), ())),
+            preferred_element_type=jnp.float32,
         )
+        return both[:WINDOW] + both[WINDOW:]
 
     def commit(c, base, item):
         heat[pl.ds(base, WINDOW), :] = heat[pl.ds(base, WINDOW), :] + item
@@ -630,7 +656,6 @@
     def swap(value, pairs):
         return lax.ppermute(value, axes, pairs)
 
-    temperatures = initial_voxel_degrees
     initial_voxel_degrees = pltpu.with_memory_space_constraint(initial_voxel_degrees, pltpu.HBM)
     alloy_tag_per_voxel = pltpu.with_memory_space_constraint(alloy_tag_per_voxel, pltpu.HBM)
 
@@ -658,14 +683,15 @@
     most = f32(2, rows - ny + 2 * PAD, LANES)
     t0, tb0, cond_a, cond_b, gxm, gy, gz, coeff = call(
         prepare_kernel,
-        (temperatures, alloy_tag_per_voxel, thermal_conductance_per_alloy, specific_storage_per_alloy),
-        [VMEM, HBM, SMEM, SMEM],
+        (initial_voxel_degrees, alloy_tag_per_voxel, thermal_conductance_per_alloy, specific_storage_per_alloy),
+        [HBM, HBM, SMEM, SMEM],
         (most, plane, plane, plane, f32(2, rows - ny, LANES), full, f32(4, rows, LANES), f32(2, rows, LANES)),
         (VMEM,) * 8,
         [
             pltpu.VMEM((2, rows + 2 * PAD, LANES), jnp.float32),
             pltpu.VMEM((planes, ny, nz), jnp.int32),
             dma((planes,)),
+            dma((planes, 2)),
         ],
     )
     pad = pltpu.VMEM((2, ny + 2 * PAD, LANES), jnp.float32)
@@ -711,50 +737,55 @@
     listing = [
         pltpu.SMEM((depth, LANES), jnp.int32),
         pltpu.VMEM((depth, LANES), jnp.int32),
-        pltpu.VMEM((depth, LANES), jnp.int32),
         dma,
     ]
-    heat, found = call(
+    heat, found, masks = call(
         lambda *refs: final_main_kernel(*refs),
         (t2, tb2, t2_before, gxa, gxm, gy, gz, coeff, packed),
         [VMEM] * 9,
-        (f32(2 * rows + WINDOW, LANES), f32(depth, LANES)),
-        (VMEM, VMEM),
-        listing,
+        (
+            f32(2 * rows + WINDOW, LANES),
+            f32(depth, LANES),
+            jax.ShapeDtypeStruct((hits, LANES), jnp.bfloat16),
+        ),
+        (VMEM,) * 3,
+        listing + [pltpu.VMEM((depth, LANES), jnp.int32)],
         cost=10_000_000,
     )
     ratio = surface_over_flow_ratio.reshape(1, lines)
     heat, found, send = call(
         lambda *refs: walls_kernel(wall, *refs),
-        (t2, tb2, halo_b, gxb, gxm, gy, gz, coeff, packed, found, surface_transfer_coefficient, ratio, heat),
-        [VMEM] * 13,
+        (t2, tb2, halo_b, gxb, gxm, gy, gz, coeff, packed, masks, found, surface_transfer_coefficient, ratio, heat),
+        [VMEM] * 14,
         (f32(2 * rows + WINDOW, LANES), f32(depth, LANES), f32(count, LANES)),
         (VMEM, VMEM, VMEM),
         [pad, pltpu.VMEM((lines, LANES), jnp.float32)] + listing,
-        input_output_aliases={12: 0},
+        input_output_aliases={13: 0},
     )
     rows_all = lax.all_to_all(send, "brick", 0, 0, tiled=True)
     final, mid, _ = call(
         lambda *refs: finish_kernel(wall, *refs),
         (
             packed,
+            masks,
             found,
             rows_all,
             flow_direction_flag.reshape(1, lines),
             entry_coolant_degrees.reshape(1, lines),
             heat,
         ),
-        [VMEM] * 6,
+        [VMEM] * 7,
         (f32(planes, ny, nz), f32(1, lines), f32(2 * rows + WINDOW, LANES)),
         (HBM, VMEM, VMEM),
         [
             pltpu.VMEM((count, LANES), jnp.float32),
             pltpu.VMEM((8, LANES), jnp.float32),
             pltpu.VMEM((depth, LANES), jnp.float32),
+            pltpu.VMEM((depth, LANES), jnp.float32),
         ]
         + listing
         + [dma((planes, 2))],
-        input_output_aliases={5: 2},
+        input_output_aliases={6: 2},
     )
     return final, mid
 

time: 57.5 us -> 55.4 us (0.963)
  Pallas kernels: 28.3 us -> 27 us
    pallas_call x8, Pallas kernels: 28.3 us -> 27 us  [call(): pl.pallas_call(kernel, out_shape=out_shape, in_specs=in_specs, out_specs=...]
  transfers between devices with their start and end apart: 4 -> 4, of which waited for: 1 -> 2; matrix products, arithmetic and copies ran while one was open for 10% -> 10% of each run, Pallas kernels for 30% -> 31%
where the time goes in v7:
time: 55.4 us; the launch traced here: 55.3 us
  Pallas kernels  27 us (49%)
  blocking collectives  15.9 us (29%)
  other arithmetic  5.69 us (10%)
  starting transfers between devices  5.13 us (9%)
  between operations  0.75 us (1%)
  waiting for transfers between devices  0.74 us (1%)
    pallas_call x8, Pallas kernels, call(): pl.pallas_call(kernel, out_shape=out_shape, in_specs=in_specs, out_specs=...  27 us
    all_to_all x1, blocking collectives, per_device(): rows_all = lax.all_to_all(send, 'brick', 0, 0, tiled=True)  15.9 us
    sort x1, other arithmetic, per_device(): packed = lax.sort(cell * 8192 + lax.iota(jnp.int32, hits), is_stable=False)  5.59 us
    ppermute x4, starting transfers between devices, swap(): return lax.ppermute(value, axes, pairs)  5.13 us
  transfers between devices with their start and end apart: 4, of which 2 were waited for; matrix products, arithmetic and copies ran while one was open for 10% of the time, Pallas kernels for 31%

profile of v7, /device:TPU:0, one launch (start us, length us, event | category | flops | bytes accessed | tf_op | source)
XLA Modules:
  0.0 55.3 jit_solution(12700642894188546468)
XLA Ops:
  0.6 0.0 copy-start.6
  0.6 0.0 copy-start.1
  0.7 0.0 copy-start
  0.7 2.9 %shard_map.105 = (f32[2,3,2,256,128]{4,3,2,1,0:T(8,128)}, f32[2,1,2,256,128]{4,3,2,1,0:T(8,128)S(1)}) custom-call(f32[8,256,256]{2,1,0:T(8,128)} %t_ref.3, s32[8,256,256]{2,1,0:T(8,128)} %tag_ref.3), custom_call_target="tpu_custom_call" | custom-call | flops 2000000 | bytes 2000000 | tf_op jit(solution)/shard_map/pallas_call | solution.py:30
  3.6 0.5 collective-permute-start.1
  4.1 2.6 %collective-permute-start = (f32[2,1,2,256,128]{4,3,2,1,0:T(8,128)S(1)}, f32[2,1,2,256,128]{4,3,2,1,0:T(8,128)S(1)}, u32[]{:S(2)}, u32[]{:S(2)}) collective-permute-start(f32[2,1,2,256,128]{4,3,2,1,0:T(8,128)S(1)} %get-tuple-element.33), channel_id=1, source_target_pairs={{0,16},{1,2},{2,1},{3,4},{4,3},{5,6},{6,5},{7,8},{8,7},{9,10},{10,... | collective-permute-start | bytes 1572872 | tf_op jit(solution)/shard_map/ppermute | solution.py:657
  6.7 0.0 copy-done.6
  6.7 0.1 fusion.9
  6.8 5.6 %sort.7 = s32[8192]{0:T(1024)S(1)} sort(s32[8192]{0:T(1024)S(1)} %fusion.9), dimensions={0}, to_apply=%region_0.1 | sort | flops 106496 | bytes 65536 | tf_op jit(solution)/shard_map/sort | solution.py:678
  12.4 0.0 copy-done.1
  12.4 0.0 copy-done
  12.4 6.2 %shard_map.104 = (f32[2,1808,128]{2,1,0:T(8,128)S(1)}, f32[2,256,128]{2,1,0:T(8,128)S(1)}, f32[2,256,128]{2,1,0:T(8,128)S(1)}, f32[2,256,128]{2,1,0:T(8,128)S(1)...) custom-call(f32[8,256,256]{2,1,0:T(8,128)} %t_ref.3, ...), custom_call_target="tpu_custom_call" | custom-call | flops 2000000 | bytes 2000000 | tf_op jit(solution)/shard_map/pallas_call | solution.py:30
  18.6 0.0 collective-permute-done.refs_4_
  18.6 1.1 %shard_map.106 = (f32[2,256,128]{2,1,0:T(8,128)S(1)}, f32[2,256,128]{2,1,0:T(8,128)S(1)}) custom-call(f32[8]{0:T(128)S(1)} %copy-done, f32[2,1808,128]{2,1,0:T(8,128)S(1)} %get-tuple-element.30.refs_1_.t0, f32[2,256,128]{2,1,0:T(8,128)S(1)} %get-tuple-element.31.refs_2_.tb0, f32[2,256,128]{2,1,0:T(8,128)S(1)} %get-tuple-element.32.refs_3_, ...), custom_call_target="tpu_custom_call" | custom-call | flops 2000000 | bytes 2000000 | tf_op jit(solution)/shard_map/pallas_call | solution.py:30
  19.7 0.1 collective-permute-start.2
  19.8 0.0 collective-permute-done.1.halo
  19.8 6.2 %shard_map.107 = (f32[2,256,128]{2,1,0:T(8,128)S(1)}, f32[2,1808,128]{2,1,0:T(8,128)S(1)}, f32[2,256,128]{2,1,0:T(8,128)S(1)}, f32[2,256,128]{2,1,0:T(8,128)S(1)}) custom-call(f32[8]{0:T(128)S(1)} %copy-done, f32[8]{0:T(128)S(1)} %copy-done.1, f32[2,1808,128]{2,1,0:T(8,128)S(1)} %get-tuple-element.30.refs_1_.t0, ...), custom_call_target="tpu_custom_call" | custom-call | flops 2000000 | bytes 2000000 | tf_op jit(solution)/shard_map/pallas_call | solution.py:30
  26.0 0.1 collective-permute-done.2.halo
  26.1 0.3 shard_map.108.refs_1_
  26.4 1.9 %collective-permute-start.3 = (f32[2,256,128]{2,1,0:T(8,128)S(1)}, f32[2,256,128]{2,1,0:T(8,128)S(1)}, u32[]{:S(2)}, u32[]{:S(2)}) collective-permute-start(f32[2,256,128]{2,1,0:T(8,128)S(1)} %shard_map.108.refs_1_), channel_id=1, source_target_pairs={{0,16},{1,2},{2,1},{3,4},{4,3},{5,6},{6,5},{7,8},{8,7},{9,10},{10,... | collective-permute-start | bytes 786440 | tf_op jit(solution)/shard_map/ppermute | solution.py:657
  28.4 0.0 copy-start.2
  28.4 0.0 copy-start.3
  28.4 3.9 %shard_map.109 = (f32[4192,128]{1,0:T(8,128)S(1)}, f32[64,128]{1,0:T(8,128)S(1)}, bf16[8192,128]{1,0:T(8,128)(2,1)S(1)}) custom-call(f32[2,1808,128]{2,1,0:T(8,128)S(1)} %get-tuple-element.41.refs_0_, f32[2,256,128]{2,1,0:T(8,128)S(1)} %shard_map.108.refs_1_, f32[2,256,128]{2,1,0:T(8,128)S(1)} %get-tuple-element.44.refs_2_, ...), custom_call_target="tpu_custom_call" | custom-call | flops 10000000 | bytes 10000000 | tf_op jit(solution)/shard_map/pallas_call | solution.py:30
  32.2 0.6 %collective-permute-done.3.refs_2_ = f32[2,256,128]{2,1,0:T(8,128)S(1)} collective-permute-done((f32[2,256,128]{2,1,0:T(8,128)S(1)}, f32[2,256,128]{2,1,0:T(8,128)S(1)}, u32[]{:S(2)}, u32[]{:S(2)}) %collective-permute-start.3) | collective-permute-done | bytes 262176 | tf_op jit(solution)/shard_map/ppermute | solution.py:657
  32.9 0.0 copy-done.2
  32.9 0.0 copy-done.3
  32.9 0.0 copy-start.4
  32.9 0.0 copy-start.5
  32.9 1.9 %shard_map.110 = (f32[4192,128]{1,0:T(8,128)S(1)}, f32[64,128]{1,0:T(8,128)S(1)}, f32[16,128]{1,0:T(8,128)S(1)}) custom-call(f32[2,1808,128]{2,1,0:T(8,128)S(1)} %get-tuple-element.41.refs_0_, f32[2,256,128]{2,1,0:T(8,128)S(1)} %shard_map.108.refs_1_, f32[2,256,128]{2,1,0:T(8,128)S(1)} %collective-permute-done.3.refs_2_, ...), custom_call_target="tpu_custom_call", output_to_operand_aliasing={{0}: (13, {})} | custom-call | flops 2000000 | bytes 2000000 | tf_op jit(solution)/shard_map/pallas_call | solution.py:30
  34.8 15.9 %all_to_all.11 = f32[16,1,128]{2,1,0:T(1,128)S(1)} all-to-all(f32[16,1,128]{2,1,0:T(1,128)S(1)} %bitcast.15), channel_id=1, replica_groups=mesh['pour'=2,'brick'=16] {'brick'}, dimensions={0} | all-to-all | bytes 16384 | tf_op jit(solution)/shard_map/all_to_all | solution.py:765
  50.7 0.0 copy-done.4
  50.7 0.0 copy-done.5
  50.7 4.6 %shard_map.111 = (f32[8,256,256]{2,1,0:T(8,128)}, f32[1,32]{1,0:T(1,128)}, f32[4192,128]{1,0:T(8,128)S(1)}) custom-call(s32[64,128]{1,0:T(8,128)S(1)} %bitcast.13, bf16[8192,128]{1,0:T(8,128)(2,1)S(1)} %get-tuple-element.46.refs_9_.refs_1_, f32[64,128]{1,0:T(8,128)S(1)} %get-tuple-element.49.refs_2_, ...), custom_call_target="tpu_custom_call", output_to_operand_aliasing={{2}: (6, {})} | custom-call | flops 2000000 | bytes 2000000 | tf_op jit(solution)/shard_map/pallas_call | solution.py:30
  (2 shorter events, 0.0 us)
Async XLA Ops:
  0.6 6.0 %copy-start.6 = (s32[1,32,256]{2,1,0:T(8,128)S(1)}, s32[1,32,256]{2,1,0:T(8,128)}, u32[]{:S(2)}) copy-start(s32[1,32,256]{2,1,0:T(8,128)} %param.13) | copy-start | bytes 98308
  0.6 11.8 %copy-start.1 = (f32[8]{0:T(128)S(1)}, f32[8]{0:T(128)}, u32[]{:S(2)}) copy-start(f32[8]{0:T(128)} %store_ref.1) | copy-start | bytes 100
  0.7 11.7 %copy-start = (f32[8]{0:T(128)S(1)}, f32[8]{0:T(128)}, u32[]{:S(2)}) copy-start(f32[8]{0:T(128)} %cond_ref.3) | copy-start | bytes 100
  3.6 16.2 %collective-permute-start.1 = (f32[2,3,2,256,128]{4,3,2,1,0:T(8,128)}, f32[2,3,2,256,128]{4,3,2,1,0:T(8,128)S(1)}, u32[]{:S(2)}, u32[]{:S(2)}) collective-permute-start(f32[2,3,2,256,128]{4,3,2,1,0:T(8,128)} %get-tuple-element.40), channel_id=1, source_target_pairs={{0,1},{1,0},{2,3},{3,2},{4,5},{5,4},{6,7},{7,6},{8,9},{9,8},{10,11... | collective-permute-start | bytes 4718600 | tf_op jit(solution)/shard_map/ppermute | solution.py:657
  4.1 14.5 %collective-permute-start = (f32[2,1,2,256,128]{4,3,2,1,0:T(8,128)S(1)}, f32[2,1,2,256,128]{4,3,2,1,0:T(8,128)S(1)}, u32[]{:S(2)}, u32[]{:S(2)}) collective-permute-start(f32[2,1,2,256,128]{4,3,2,1,0:T(8,128)S(1)} %get-tuple-element.33), channel_id=1, source_target_pairs={{0,16},{1,2},{2,1},{3,4},{4,3},{5,6},{6,5},{7,8},{8,7},{9,10},{10,... | collective-permute-start | bytes 1572872 | tf_op jit(solution)/shard_map/ppermute | solution.py:657
  19.7 6.4 %collective-permute-start.2 = (f32[2,256,128]{2,1,0:T(8,128)S(1)}, f32[2,256,128]{2,1,0:T(8,128)S(1)}, u32[]{:S(2)}, u32[]{:S(2)}) collective-permute-start(f32[2,256,128]{2,1,0:T(8,128)S(1)} %get-tuple-element.38.tb1.tb_old), channel_id=1, source_target_pairs={{0,16},{1,2},{2,1},{3,4},{4,3},{5,6},{6,5},{7,8},{8,7},{9,10},{10,... | collective-permute-start | bytes 786440 | tf_op jit(solution)/shard_map/ppermute | solution.py:657
  26.4 6.4 %collective-permute-start.3 = (f32[2,256,128]{2,1,0:T(8,128)S(1)}, f32[2,256,128]{2,1,0:T(8,128)S(1)}, u32[]{:S(2)}, u32[]{:S(2)}) collective-permute-start(f32[2,256,128]{2,1,0:T(8,128)S(1)} %shard_map.108.refs_1_), channel_id=1, source_target_pairs={{0,16},{1,2},{2,1},{3,4},{4,3},{5,6},{6,5},{7,8},{8,7},{9,10},{10,... | collective-permute-start | bytes 786440 | tf_op jit(solution)/shard_map/ppermute | solution.py:657
  28.4 4.5 %copy-start.2 = (f32[1,32]{1,0:T(1,128)S(1)}, f32[1,32]{1,0:T(1,128)}, u32[]{:S(2)}) copy-start(f32[1,32]{1,0:T(1,128)} %refs_11_.1) | copy-start | bytes 388
  28.4 4.5 %copy-start.3 = (f32[32]{0:T(128)S(1)}, f32[32]{0:T(128)}, u32[]{:S(2)}) copy-start(f32[32]{0:T(128)} %param.15) | copy-start | bytes 388
  32.9 17.8 %copy-start.4 = (s32[32]{0:T(128)S(1)}, s32[32]{0:T(128)}, u32[]{:S(2)}) copy-start(s32[32]{0:T(128)} %param.16) | copy-start | bytes 388
  32.9 17.8 %copy-start.5 = (f32[32]{0:T(128)S(1)}, f32[32]{0:T(128)}, u32[]{:S(2)}) copy-start(f32[32]{0:T(128)} %param.17) | copy-start | bytes 388

commit v8 on v7

--- a/solution.py
+++ b/solution.py
@@ -144,23 +144,27 @@
     plane(planes - 2, False, True)
 
 
-def send_kernel(t_ref, tag_ref, a_ref, b_ref, tags, sem):
-    planes = t_ref.shape[0]
+def send_kernel(t_ref, tag_ref, a_ref, b_ref, heat, tags, sem):
+    planes, ny = t_ref.shape[0], t_ref.shape[1]
     parts = [(b_ref, 0, planes - 1)] + [(a_ref, k, k) for k in range(DEEP)]
     copies = []
-    for n, (out, k, j) in enumerate(parts):
+    for n, (_, _, j) in enumerate(parts):
         x = plane_of(j, planes)
-        for h in HALVES:
-            part = pl.ds(h * LANES, LANES)
-            copies.append(pltpu.make_async_copy(tag_ref.at[x, :, part], tags.at[n, h], sem.at[1, n, h]))
-            copies.append(pltpu.make_async_copy(t_ref.at[x, :, part], out.at[0, k, h], sem.at[0, n, h]))
+        copies.append(pltpu.make_async_copy(tag_ref.at[x], tags.at[n], sem.at[1, n]))
+        copies.append(pltpu.make_async_copy(t_ref.at[x], heat.at[n], sem.at[0, n]))
     for copy in copies:
         copy.start()
     for n, (out, k, j) in enumerate(parts):
-        for copy in copies[4 * n : 4 * n + 4]:
+        for copy in copies[2 * n : 2 * n + 2]:
             copy.wait()
-        for h in HALVES:
-            out[1, k, h] = tags[n, h].astype(jnp.float32)
+
+        def body(y, n=n, out=out, k=k):
+            for h in HALVES:
+                part = slice(h * LANES, (h + 1) * LANES)
+                out[0, k, h, pl.ds(y, STRIP), :] = heat[n, pl.ds(y, STRIP), part]
+                out[1, k, h, pl.ds(y, STRIP), :] = tags[n, pl.ds(y, STRIP), part].astype(jnp.float32)
+
+        rows_loop(ny, body)
 
 
 def tables(cond_ref, store_ref):
@@ -666,7 +670,11 @@
         [HBM, HBM],
         (f32(2, DEEP, 2, ny, LANES), f32(2, 1, 2, ny, LANES)),
         (VMEM, VMEM),
-        [pltpu.VMEM((DEEP + 1, 2, ny, LANES), jnp.int32), dma((2, DEEP + 1, 2))],
+        [
+            pltpu.VMEM((DEEP + 1, ny, nz), jnp.float32),
+            pltpu.VMEM((DEEP + 1, ny, nz), jnp.int32),
+            dma((2, DEEP + 1)),
+        ],
     )
     halo_b = swap(tb, across)
     halo_a = swap(ta, on_chip)

time: 55.4 us -> 55.3 us (level)
  no operation moved by 1% of the time
where the time goes in v8:
time: 55.3 us; the launch traced here: 55.2 us
  Pallas kernels  26.9 us (49%)
  blocking collectives  15.9 us (29%)
  other arithmetic  5.69 us (10%)
  starting transfers between devices  5.13 us (9%)
  waiting for transfers between devices  0.75 us (1%)
  between operations  0.75 us (1%)
    pallas_call x8, Pallas kernels, call(): pl.pallas_call(kernel, out_shape=out_shape, in_specs=in_specs, out_specs=...  26.9 us
    all_to_all x1, blocking collectives, per_device(): rows_all = lax.all_to_all(send, 'brick', 0, 0, tiled=True)  15.9 us
    sort x1, other arithmetic, per_device(): packed = lax.sort(cell * 8192 + lax.iota(jnp.int32, hits), is_stable=False)  5.59 us
    ppermute x4, starting transfers between devices, swap(): return lax.ppermute(value, axes, pairs)  5.13 us
  transfers between devices with their start and end apart: 4, of which 2 were waited for; matrix products, arithmetic and copies ran while one was open for 10% of the time, Pallas kernels for 31%

profile of v8, /device:TPU:0, one launch (start us, length us, event | category | flops | bytes accessed | tf_op | source)
XLA Modules:
  0.0 55.2 jit_solution(4939464056630301101)
XLA Ops:
  0.6 0.0 copy-start.6
  0.6 0.0 copy-start.1
  0.7 0.0 copy-start
  0.7 2.8 %shard_map.105 = (f32[2,3,2,256,128]{4,3,2,1,0:T(8,128)}, f32[2,1,2,256,128]{4,3,2,1,0:T(8,128)S(1)}) custom-call(f32[8,256,256]{2,1,0:T(8,128)} %t_ref.3, s32[8,256,256]{2,1,0:T(8,128)} %tag_ref.3), custom_call_target="tpu_custom_call" | custom-call | flops 2000000 | bytes 2000000 | tf_op jit(solution)/shard_map/pallas_call | solution.py:30
  3.4 0.5 collective-permute-start.1
  4.0 2.6 %collective-permute-start = (f32[2,1,2,256,128]{4,3,2,1,0:T(8,128)S(1)}, f32[2,1,2,256,128]{4,3,2,1,0:T(8,128)S(1)}, u32[]{:S(2)}, u32[]{:S(2)}) collective-permute-start(f32[2,1,2,256,128]{4,3,2,1,0:T(8,128)S(1)} %get-tuple-element.33), channel_id=1, source_target_pairs={{0,16},{1,2},{2,1},{3,4},{4,3},{5,6},{6,5},{7,8},{8,7},{9,10},{10,... | collective-permute-start | bytes 1572872 | tf_op jit(solution)/shard_map/ppermute | solution.py:661
  6.5 0.0 copy-done.6
  6.6 0.1 fusion.9
  6.7 5.6 %sort.7 = s32[8192]{0:T(1024)S(1)} sort(s32[8192]{0:T(1024)S(1)} %fusion.9), dimensions={0}, to_apply=%region_0.1 | sort | flops 106496 | bytes 65536 | tf_op jit(solution)/shard_map/sort | solution.py:686
  12.2 0.0 copy-done.1
  12.3 0.0 copy-done
  12.3 6.2 %shard_map.104 = (f32[2,1808,128]{2,1,0:T(8,128)S(1)}, f32[2,256,128]{2,1,0:T(8,128)S(1)}, f32[2,256,128]{2,1,0:T(8,128)S(1)}, f32[2,256,128]{2,1,0:T(8,128)S(1)...) custom-call(f32[8,256,256]{2,1,0:T(8,128)} %t_ref.3, ...), custom_call_target="tpu_custom_call" | custom-call | flops 2000000 | bytes 2000000 | tf_op jit(solution)/shard_map/pallas_call | solution.py:30
  18.4 0.0 collective-permute-done.refs_4_
  18.4 1.1 %shard_map.106 = (f32[2,256,128]{2,1,0:T(8,128)S(1)}, f32[2,256,128]{2,1,0:T(8,128)S(1)}) custom-call(f32[8]{0:T(128)S(1)} %copy-done, f32[2,1808,128]{2,1,0:T(8,128)S(1)} %get-tuple-element.30.refs_1_.t0, f32[2,256,128]{2,1,0:T(8,128)S(1)} %get-tuple-element.31.refs_2_.tb0, f32[2,256,128]{2,1,0:T(8,128)S(1)} %get-tuple-element.32.refs_3_, ...), custom_call_target="tpu_custom_call" | custom-call | flops 2000000 | bytes 2000000 | tf_op jit(solution)/shard_map/pallas_call | solution.py:30
  19.5 0.1 collective-permute-start.2
  19.6 0.0 collective-permute-done.1.halo
  19.6 6.2 %shard_map.107 = (f32[2,256,128]{2,1,0:T(8,128)S(1)}, f32[2,1808,128]{2,1,0:T(8,128)S(1)}, f32[2,256,128]{2,1,0:T(8,128)S(1)}, f32[2,256,128]{2,1,0:T(8,128)S(1)}) custom-call(f32[8]{0:T(128)S(1)} %copy-done, f32[8]{0:T(128)S(1)} %copy-done.1, f32[2,1808,128]{2,1,0:T(8,128)S(1)} %get-tuple-element.30.refs_1_.t0, ...), custom_call_target="tpu_custom_call" | custom-call | flops 2000000 | bytes 2000000 | tf_op jit(solution)/shard_map/pallas_call | solution.py:30
  25.8 0.1 collective-permute-done.2.halo
  26.0 0.3 shard_map.108.refs_1_
  26.3 1.9 %collective-permute-start.3 = (f32[2,256,128]{2,1,0:T(8,128)S(1)}, f32[2,256,128]{2,1,0:T(8,128)S(1)}, u32[]{:S(2)}, u32[]{:S(2)}) collective-permute-start(f32[2,256,128]{2,1,0:T(8,128)S(1)} %shard_map.108.refs_1_), channel_id=1, source_target_pairs={{0,16},{1,2},{2,1},{3,4},{4,3},{5,6},{6,5},{7,8},{8,7},{9,10},{10,... | collective-permute-start | bytes 786440 | tf_op jit(solution)/shard_map/ppermute | solution.py:661
  28.2 0.0 copy-start.2
  28.2 0.0 copy-start.3
  28.2 3.9 %shard_map.109 = (f32[4192,128]{1,0:T(8,128)S(1)}, f32[64,128]{1,0:T(8,128)S(1)}, bf16[8192,128]{1,0:T(8,128)(2,1)S(1)}) custom-call(f32[2,1808,128]{2,1,0:T(8,128)S(1)} %get-tuple-element.41.refs_0_, f32[2,256,128]{2,1,0:T(8,128)S(1)} %shard_map.108.refs_1_, f32[2,256,128]{2,1,0:T(8,128)S(1)} %get-tuple-element.44.refs_2_, ...), custom_call_target="tpu_custom_call" | custom-call | flops 10000000 | bytes 10000000 | tf_op jit(solution)/shard_map/pallas_call | solution.py:30
  32.1 0.6 %collective-permute-done.3.refs_2_ = f32[2,256,128]{2,1,0:T(8,128)S(1)} collective-permute-done((f32[2,256,128]{2,1,0:T(8,128)S(1)}, f32[2,256,128]{2,1,0:T(8,128)S(1)}, u32[]{:S(2)}, u32[]{:S(2)}) %collective-permute-start.3) | collective-permute-done | bytes 262176 | tf_op jit(solution)/shard_map/ppermute | solution.py:661
  32.7 0.0 copy-done.2
  32.7 0.0 copy-done.3
  32.7 0.0 copy-start.4
  32.7 0.0 copy-start.5
  32.7 1.9 %shard_map.110 = (f32[4192,128]{1,0:T(8,128)S(1)}, f32[64,128]{1,0:T(8,128)S(1)}, f32[16,128]{1,0:T(8,128)S(1)}) custom-call(f32[2,1808,128]{2,1,0:T(8,128)S(1)} %get-tuple-element.41.refs_0_, f32[2,256,128]{2,1,0:T(8,128)S(1)} %shard_map.108.refs_1_, f32[2,256,128]{2,1,0:T(8,128)S(1)} %collective-permute-done.3.refs_2_, ...), custom_call_target="tpu_custom_call", output_to_operand_aliasing={{0}: (13, {})} | custom-call | flops 2000000 | bytes 2000000 | tf_op jit(solution)/shard_map/pallas_call | solution.py:30
  34.6 15.9 %all_to_all.11 = f32[16,1,128]{2,1,0:T(1,128)S(1)} all-to-all(f32[16,1,128]{2,1,0:T(1,128)S(1)} %bitcast.15), channel_id=1, replica_groups=mesh['pour'=2,'brick'=16] {'brick'}, dimensions={0} | all-to-all | bytes 16384 | tf_op jit(solution)/shard_map/all_to_all | solution.py:773
  50.5 0.0 copy-done.4
  50.5 0.0 copy-done.5
  50.5 4.6 %shard_map.111 = (f32[8,256,256]{2,1,0:T(8,128)}, f32[1,32]{1,0:T(1,128)}, f32[4192,128]{1,0:T(8,128)S(1)}) custom-call(s32[64,128]{1,0:T(8,128)S(1)} %bitcast.13, bf16[8192,128]{1,0:T(8,128)(2,1)S(1)} %get-tuple-element.46.refs_9_.refs_1_, f32[64,128]{1,0:T(8,128)S(1)} %get-tuple-element.49.refs_2_, ...), custom_call_target="tpu_custom_call", output_to_operand_aliasing={{2}: (6, {})} | custom-call | flops 2000000 | bytes 2000000 | tf_op jit(solution)/shard_map/pallas_call | solution.py:30
  (2 shorter events, 0.0 us)
Async XLA Ops:
  0.6 5.9 %copy-start.6 = (s32[1,32,256]{2,1,0:T(8,128)S(1)}, s32[1,32,256]{2,1,0:T(8,128)}, u32[]{:S(2)}) copy-start(s32[1,32,256]{2,1,0:T(8,128)} %param.13) | copy-start | bytes 98308
  0.6 11.6 %copy-start.1 = (f32[8]{0:T(128)S(1)}, f32[8]{0:T(128)}, u32[]{:S(2)}) copy-start(f32[8]{0:T(128)} %store_ref.1) | copy-start | bytes 100
  0.7 11.6 %copy-start = (f32[8]{0:T(128)S(1)}, f32[8]{0:T(128)}, u32[]{:S(2)}) copy-start(f32[8]{0:T(128)} %cond_ref.3) | copy-start | bytes 100
  3.4 16.2 %collective-permute-start.1 = (f32[2,3,2,256,128]{4,3,2,1,0:T(8,128)}, f32[2,3,2,256,128]{4,3,2,1,0:T(8,128)S(1)}, u32[]{:S(2)}, u32[]{:S(2)}) collective-permute-start(f32[2,3,2,256,128]{4,3,2,1,0:T(8,128)} %get-tuple-element.40), channel_id=1, source_target_pairs={{0,1},{1,0},{2,3},{3,2},{4,5},{5,4},{6,7},{7,6},{8,9},{9,8},{10,11... | collective-permute-start | bytes 4718600 | tf_op jit(solution)/shard_map/ppermute | solution.py:661
  4.0 14.5 %collective-permute-start = (f32[2,1,2,256,128]{4,3,2,1,0:T(8,128)S(1)}, f32[2,1,2,256,128]{4,3,2,1,0:T(8,128)S(1)}, u32[]{:S(2)}, u32[]{:S(2)}) collective-permute-start(f32[2,1,2,256,128]{4,3,2,1,0:T(8,128)S(1)} %get-tuple-element.33), channel_id=1, source_target_pairs={{0,16},{1,2},{2,1},{3,4},{4,3},{5,6},{6,5},{7,8},{8,7},{9,10},{10,... | collective-permute-start | bytes 1572872 | tf_op jit(solution)/shard_map/ppermute | solution.py:661
  19.5 6.4 %collective-permute-start.2 = (f32[2,256,128]{2,1,0:T(8,128)S(1)}, f32[2,256,128]{2,1,0:T(8,128)S(1)}, u32[]{:S(2)}, u32[]{:S(2)}) collective-permute-start(f32[2,256,128]{2,1,0:T(8,128)S(1)} %get-tuple-element.38.tb1.tb_old), channel_id=1, source_target_pairs={{0,16},{1,2},{2,1},{3,4},{4,3},{5,6},{6,5},{7,8},{8,7},{9,10},{10,... | collective-permute-start | bytes 786440 | tf_op jit(solution)/shard_map/ppermute | solution.py:661
  26.3 6.4 %collective-permute-start.3 = (f32[2,256,128]{2,1,0:T(8,128)S(1)}, f32[2,256,128]{2,1,0:T(8,128)S(1)}, u32[]{:S(2)}, u32[]{:S(2)}) collective-permute-start(f32[2,256,128]{2,1,0:T(8,128)S(1)} %shard_map.108.refs_1_), channel_id=1, source_target_pairs={{0,16},{1,2},{2,1},{3,4},{4,3},{5,6},{6,5},{7,8},{8,7},{9,10},{10,... | collective-permute-start | bytes 786440 | tf_op jit(solution)/shard_map/ppermute | solution.py:661
  28.2 4.5 %copy-start.2 = (f32[1,32]{1,0:T(1,128)S(1)}, f32[1,32]{1,0:T(1,128)}, u32[]{:S(2)}) copy-start(f32[1,32]{1,0:T(1,128)} %refs_11_.1) | copy-start | bytes 388
  28.2 4.5 %copy-start.3 = (f32[32]{0:T(128)S(1)}, f32[32]{0:T(128)}, u32[]{:S(2)}) copy-start(f32[32]{0:T(128)} %param.15) | copy-start | bytes 388
  32.7 17.8 %copy-start.4 = (s32[32]{0:T(128)S(1)}, s32[32]{0:T(128)}, u32[]{:S(2)}) copy-start(s32[32]{0:T(128)} %param.16) | copy-start | bytes 388
  32.7 17.8 %copy-start.5 = (f32[32]{0:T(128)S(1)}, f32[32]{0:T(128)}, u32[]{:S(2)}) copy-start(f32[32]{0:T(128)} %param.17) | copy-start | bytes 388
